TPU v7x, 32 devices: a whole 2x2x4 slice. The times are simulated.
32 devices in a mesh: dom: 4 (over y, core), shard: 4 (over z), dp: 2 (over x).
Axes of the slice: x: 2, y: 2, z: 4, core: 2. Of those that a mesh axis runs over, the one named last changes fastest.
Arguments:
- queries_in: bfloat16 [4, 1024, 1024], P('dom', ('shard', 'dp')), may hold values from -8 to 8
- encoder_weight: bfloat16 [1024, 1024], P(('dom', 'shard', 'dp')), may hold values from -0.1875 to 0.1875
- codebook: float32 [4, 128, 8, 256], P('dom', 'shard'), may hold values from -0.06 to 0.06
- codes: int32 [4, 4096, 128], P('dom', 'shard'), may hold values from 0 to 255
- positive_ids: int32 [4, 1024], P('dom'), may hold values from 0 to 4095
- loss_weight: bfloat16 [4, 1024], P('dom'), may hold values from 0.5 to 2
Outputs:
- encoder_grad: float32 [1024, 1024], P(('dom', 'shard', 'dp'))
- codebook_grad: float32 [4, 128, 8, 256], P('dom', ('shard', 'dp'))
All inputs are finite; a program needn't handle non-finite values.
Results may differ from a plain program's by a relative error of at most 0.0005.
The roundings to bfloat16 on the way count: a program that leaves them out, or rounds other values in their place, can miss the bound.
Values may be sent and summed in bfloat16 or wider, within the bound.
No kernel may reach another device: no remote copies, remote signals or barrier semaphores. Data moves between devices by JAX's collectives and lax.ppermute only.
A program may use at most 64 MiB of HBM per device.

v0:
```python
import functools
import jax
import jax.numpy as jnp
from jax import lax
from jax.experimental import pallas as pl
from jax.experimental.pallas import tpu as pltpu
from jax.sharding import PartitionSpec as P


BF16, F32, I32 = jnp.bfloat16, jnp.float32, jnp.int32
NT = (((1,), (1,)), ((), ()))
LANES = 128
SPLIT = 4
ANY = pl.BlockSpec(memory_space=pl.ANY)
VMEM = pl.BlockSpec(memory_space=pltpu.VMEM)
SMEM = pl.BlockSpec(memory_space=pltpu.SMEM)
MIB = 2**20


def ring(n, k):
    return [(i, (i + k) % n) for i in range(n)]


def flip(n, k):
    return [(i, i ^ k) for i in range(n)]


def cost(flops, bytes_accessed):
    return pl.CostEstimate(flops=flops, bytes_accessed=bytes_accessed, transcendentals=0)


def rebuild_kernel(n_t, n_b, place_ref, *refs):
    code_refs, books, (out_ref, codes_ref, table) = refs[:n_t], refs[n_t : n_t + n_b], refs[n_t + n_b :]
    held, sub, words = books[0].shape
    columns = code_refs[0].shape[1]
    for i, code_ref in enumerate(code_refs):
        codes_ref[i] = code_ref[...].astype(I32)
    for piece, book_ref in enumerate(books):
        table[pl.ds(place_ref[piece] * held, held)] = book_ref[...].astype(F32)

    def body(i, _):
        tile, first = i // n_b, lax.rem(i, n_b) * held
        for j in range(held // 8):
            rows = pl.multiple_of(first + 8 * j, 8)
            codes = codes_ref[tile, pl.ds(rows, 8), :]
            for pair in range(4):
                tables = []
                for h in range(2):
                    words_of = table[rows + 2 * pair + h]
                    tables.append([words_of[:, c : c + LANES] for c in range(0, words, LANES)])
                for t in range(0, columns, LANES):
                    parts = []
                    for h in range(2):
                        row = codes[2 * pair + h : 2 * pair + h + 1, t : t + LANES]
                        index = jnp.broadcast_to(row, (sub, LANES))
                        lane = index & (LANES - 1)
                        value = None
                        for c, part in enumerate(tables[h]):
                            found = jnp.take_along_axis(part, lane, axis=1, mode="promise_in_bounds")
                            value = found if value is None else jnp.where(index < c * LANES, value, found)
                        parts.append(value)
                    out_rows = pl.ds(pl.multiple_of((rows + 2 * pair) * sub, 2 * sub), 2 * sub)
                    out_ref[tile, out_rows, t : t + LANES] = jnp.concatenate(parts, 0).astype(BF16)
        return 0

    lax.fori_loop(0, n_t * n_b, body, 0)


def rebuild(place, codes, books):
    n_t, n_b = len(codes), len(books)
    subspaces, columns = codes[0].shape
    _, sub, words = books[0].shape
    return pl.pallas_call(
        functools.partial(rebuild_kernel, n_t, n_b),
        out_shape=(
            jax.ShapeDtypeStruct((n_t, subspaces * sub, columns), BF16),
            jax.ShapeDtypeStruct((n_t, subspaces, columns), I32),
        ),
        in_specs=[SMEM] + [VMEM] * (n_t + n_b),
        out_specs=(VMEM, VMEM),
        scratch_shapes=[pltpu.VMEM((subspaces, sub, words), F32)],
        compiler_params=pltpu.CompilerParams(vmem_limit_bytes=(6 + n_t) * MIB),
        cost_estimate=cost(n_t * 10**9, n_t * 2 * 10**6),
    )(place, *codes, *books)


def main_kernel(n_q, n_w, n_g, woff_ref, tbase_ref, frow_ref, pos_ref, wt_ref, *refs):
    q_refs, refs = refs[:n_q], refs[n_q:]
    w_refs, refs = refs[:n_w], refs[n_w:]
    g_refs, refs = refs[:n_g], refs[n_g:]
    gs_ref, nt_ref, own_ref, other_ref = refs[:4]
    w, q, exps, normed, total, gn = refs[4:]
    for i, w_ref in enumerate(w_refs):
        blocks, rows = w_ref.shape[0], w_ref.shape[1]
        for k in range(blocks):
            w[pl.ds(pl.multiple_of(woff_ref[i * blocks + k], rows), rows), :] = w_ref[k]
    own = q_refs[0].shape[0]
    for i, q_ref in enumerate(q_refs):
        q[i * own : (i + 1) * own, :] = q_ref[...]
    depth = q.shape[1]
    rows = frow_ref.shape[0]
    pick = (frow_ref[...] == lax.broadcasted_iota(I32, (rows, depth), 1)).astype(F32).astype(BF16)
    picked = lax.dot_general(pick, q[...], NT, preferred_element_type=F32).astype(BF16)
    encoded = jnp.dot(q[...], w[...], preferred_element_type=F32)
    inv_rms = lax.rsqrt(jnp.mean(encoded * encoded, axis=1, keepdims=True) + 1e-06)
    normed[...] = encoded * inv_rms
    low = normed[...].astype(BF16)
    q[...] = low
    nt_ref[...] = low.T
    total[...] = jnp.zeros_like(total)
    first = 0
    for tiles in g_refs:

        def score(j, _, tiles=tiles, first=first):
            e = jnp.exp(jnp.dot(q[...], tiles[j], preferred_element_type=F32))
            exps[first + j] = e
            total[...] += jnp.sum(e, axis=1, keepdims=True)
            return 0

        lax.fori_loop(0, tiles.shape[0], score, 0)
        first += tiles.shape[0]
    gn[...] = jnp.zeros_like(gn)
    scale = 1.0 / total[...]
    first = 0
    for tiles in g_refs:
        width = tiles.shape[2]

        def back(j, _, tiles=tiles, first=first, width=width):
            ids = tbase_ref[first + j] + lax.broadcasted_iota(I32, (1, width), 1)
            target = (pos_ref[...] == ids).astype(F32)
            gs = (wt_ref[...] * (exps[first + j] * scale - target)).astype(BF16)
            gs_ref[first + j] = gs
            gn[...] += lax.dot_general(gs, tiles[j], NT, preferred_element_type=F32)
            return 0

        lax.fori_loop(0, tiles.shape[0], back, 0)
        first += tiles.shape[0]
    inner = jnp.mean(gn[...] * normed[...], axis=1, keepdims=True)
    grad = (inv_rms * (gn[...] - normed[...] * inner)).astype(BF16)
    half = rows // 2
    own_ref[...] = jnp.dot(picked[:half], grad, preferred_element_type=F32)
    other_ref[...] = jnp.dot(picked[half:], grad, preferred_element_type=F32)


def main(woff, tbase, frow, pos, wt, q_pieces, w_pieces, groups):
    n_q, n_w, n_g = len(q_pieces), len(w_pieces), len(groups)
    own, depth = q_pieces[0].shape
    queries = own * n_q
    n_t = sum(g.shape[0] for g in groups)
    features, width = groups[0].shape[1:]
    half = frow.shape[0] // 2
    return pl.pallas_call(
        functools.partial(main_kernel, n_q, n_w, n_g),
        out_shape=(
            jax.ShapeDtypeStruct((n_t, queries, width), BF16),
            jax.ShapeDtypeStruct((features, queries), BF16),
            jax.ShapeDtypeStruct((half, features), F32),
            jax.ShapeDtypeStruct((half, features), F32),
        ),
        in_specs=[SMEM, SMEM, VMEM, VMEM, VMEM] + [VMEM] * (n_q + n_w + n_g),
        out_specs=(VMEM,) * 4,
        scratch_shapes=[
            pltpu.VMEM((depth, features), BF16),
            pltpu.VMEM((queries, depth), BF16),
            pltpu.VMEM((n_t, queries, width), F32),
            pltpu.VMEM((queries, features), F32),
            pltpu.VMEM((queries, 1), F32),
            pltpu.VMEM((queries, features), F32),
        ],
        compiler_params=pltpu.CompilerParams(vmem_limit_bytes=(28 if n_t * queries * width * 4 <= 8 * MIB else 60) * MIB),
        cost_estimate=cost(20 * 10**9, 20 * 10**6),
    )(woff, tbase, frow, pos, wt, *q_pieces, *w_pieces, *groups)


def dots_kernel(blocks_ref, nt_ref, gs_ref, *out_refs):
    rows = out_refs[0].shape[0]
    n_t, width = gs_ref.shape[0], gs_ref.shape[2]
    picked = [nt_ref[pl.ds(pl.multiple_of(blocks_ref[i] * rows, rows), rows), :] for i in range(len(out_refs))]
    picked = jnp.concatenate(picked, 0)
    for j in range(n_t):
        grads = jnp.dot(picked, gs_ref[j], preferred_element_type=F32)
        for i, out_ref in enumerate(out_refs):
            out_ref[:, j * width : (j + 1) * width] = grads[i * rows : (i + 1) * rows]


def passage_grads(blocks, rows, nt, gs):
    n_t, _, width = gs.shape
    n = blocks.shape[0]
    return pl.pallas_call(
        dots_kernel,
        out_shape=(jax.ShapeDtypeStruct((rows, n_t * width), F32),) * n,
        in_specs=[SMEM, VMEM, VMEM],
        out_specs=(VMEM,) * n,
        compiler_params=pltpu.CompilerParams(vmem_limit_bytes=12 * MIB),
        cost_estimate=cost(3 * 10**9, 8 * 10**6),
    )(blocks, nt, gs)


def words_kernel(words, block_ref, grads_ref, *refs):
    code_refs, (out_ref, codes) = refs[:-2], refs[-2:]
    held, sub = out_ref.shape[0], out_ref.shape[1]
    column = 0
    for code_ref in code_refs:
        width = code_ref.shape[2]
        for j in range(code_ref.shape[0]):
            rows = pl.ds(pl.multiple_of(block_ref[0] * held, held), held)
            codes[:, column : column + width] = code_ref[j, rows, :]
            column += width
    low = words // SPLIT
    shift = low.bit_length() - 1
    step = 1024

    def body(group, _):
        code8 = codes[pl.ds(pl.multiple_of(8 * group, 8), 8), :]
        for i in range(8):
            m = 8 * group + i
            grad = grads_ref[pl.ds(pl.multiple_of(sub * m, sub), sub), :]
            upper = grad.astype(BF16).astype(F32)
            parts = jnp.concatenate([upper, grad - upper], 0)
            row = code8[i : i + 1, :]
            acc = None
            for t in range(0, codes.shape[1], step):
                c = row[:, t : t + step]
                p = parts[:, t : t + step]
                high = jnp.broadcast_to(lax.shift_right_logical(c, shift), p.shape)
                p = jnp.concatenate([jnp.where(high == h, p, 0.0) for h in range(SPLIT)], 0)
                hot = (c & (low - 1)) == lax.broadcasted_iota(I32, (low, step), 0)
                r = lax.dot_general(
                    hot.astype(F32).astype(BF16), p.astype(BF16), NT, preferred_element_type=F32
                )
                acc = r if acc is None else acc + r
            acc = acc.T
            pieces = []
            for h in range(SPLIT):
                a = acc[2 * sub * h : 2 * sub * h + sub]
                pieces.append(a + acc[2 * sub * h + sub : 2 * sub * (h + 1)])
            out_ref[m] = jnp.concatenate(pieces, 1)
        return 0

    lax.fori_loop(0, held // 8, body, 0)


def word_grads(block, held, words, grads, codes):
    columns = grads.shape[1]
    sub = grads.shape[0] // held
    return pl.pallas_call(
        functools.partial(words_kernel, words),
        out_shape=jax.ShapeDtypeStruct((held, sub, words), F32),
        in_specs=[SMEM, VMEM] + [VMEM] * len(codes),
        out_specs=VMEM,
        scratch_shapes=[pltpu.VMEM((held, columns), I32)],
        compiler_params=pltpu.CompilerParams(vmem_limit_bytes=8 * MIB),
        cost_estimate=cost(3 * 10**9, 4 * 10**6),
    )(block, grads, *codes)


def compute(n_dom, n_sh, n_dp, queries_in, encoder_weight, codebook, codes, positive_ids, loss_weight):
    dom, z, x = (lax.axis_index(a) for a in ("dom", "shard", "dp"))
    n_dev = n_dom * n_sh * n_dp
    n_zp = n_sh // 2
    evens = range(0, n_dom, 2)
    shards = [lax.rem(z - k + n_sh, n_sh) for k in range(n_sh)]
    lanes = [lax.rem(x - t + n_dp, n_dp) for t in range(n_dp)]
    move = lax.ppermute

    w_rows, depth = encoder_weight.shape
    w_z = jnp.stack([encoder_weight] + [move(encoder_weight, "shard", ring(n_sh, k)) for k in range(1, n_sh)])

    q = queries_in[0]
    own = q.shape[0]
    q_pieces, q_from = [], []
    for t in range(n_dp):
        for a in range(2):
            pairs = []
            for s in range(n_sh):
                for d in range(n_dp):
                    pairs.append((s * n_dp + d, (s ^ a) * n_dp + (d + t) % n_dp))
            q_pieces.append(q if t == a == 0 else move(q, ("shard", "dp"), pairs))
            q_from.append((z ^ a) * n_dp + lanes[t])

    book = codebook[0].astype(BF16)
    words = book.shape[2]
    books = [book] + [move(book, "shard", ring(n_sh, k)) for k in range(1, n_sh)]
    codes_t = codes[0].T.astype(BF16)
    subspaces, pass_rows = codes_t.shape
    width = pass_rows // n_dp
    share = [lax.dynamic_slice_in_dim(codes_t, lanes[t] * width, width, 1) for t in range(n_dp)]
    tiles = {(0, 0): share[0]}
    for k in range(1, n_sh):
        tiles[0, k] = move(share[0], "shard", ring(n_sh, k))
    for t in range(1, n_dp):
        tiles[t, 0] = share[t]
        for k in range(1, n_sh):
            tiles[t, k] = move(tiles[0, k], "dp", ring(n_dp, t))

    w_x = [w_z] + [move(w_z, "dp", ring(n_dp, t)) for t in range(1, n_dp)]
    w_pieces, w_places = [], []
    for e in evens:
        for t in range(n_dp):
            w_pieces.append(w_x[t] if e == 0 else move(w_x[t], "dom", flip(n_dom, e)))
    w_pieces += [move(piece, "dom", flip(n_dom, 1)) for piece in w_pieces]
    for core in range(2):
        for e in evens:
            for t in range(n_dp):
                for k in range(n_sh):
                    w_places.append(((dom ^ (e | core)) * n_sh + shards[k]) * n_dp + lanes[t])
    w_places = jnp.stack(w_places).astype(I32)
    if w_rows % 16:
        whole = jnp.concatenate(w_pieces).reshape(n_dev, w_rows, depth)
        order = jnp.zeros((n_dev,), I32).at[w_places].set(jnp.arange(n_dev, dtype=I32))
        w_pieces = [whole[order].reshape(1, n_dev * w_rows, depth)]
        w_offsets = jnp.zeros((1,), I32)
    else:
        w_offsets = w_places * w_rows

    place = jnp.stack(shards).astype(I32)
    order = [[(t, 0) for t in range(n_dp)]] + [[(t, k) for k in range(1, n_sh)] for t in range(n_dp)]
    bases = [shards[k] * pass_rows + lanes[t] * width for group in order for t, k in group]
    built = [rebuild(place, [tiles[key] for key in group], books) for group in order]
    passages = [b[0] for b in built]
    tile_codes = [b[1] for b in built]

    def rows_of(array):
        return jnp.concatenate([lax.dynamic_slice_in_dim(array, f * own, own, 0) for f in q_from])[:, None]

    out_rows = depth // n_dev
    zp, zi = z // 2, z % 2
    blocks = []
    for core in range(2):
        for e in evens:
            for j in range(n_zp):
                to_z = lax.rem(zp + j, n_zp) * 2 + zi
                blocks.append((((dom ^ (e | core)) * n_sh + to_z) * n_dp + x) * out_rows)
    frow = (jnp.stack(blocks).astype(I32)[:, None] + jnp.arange(out_rows, dtype=I32)[None, :]).reshape(-1, 1)

    gs, low_t, own_part, other_part = main(
        w_offsets,
        jnp.stack(bases).astype(I32),
        frow,
        rows_of(positive_ids[0]),
        rows_of(loss_weight[0].astype(F32)),
        q_pieces,
        w_pieces,
        passages,
    )

    held = subspaces // (n_sh * n_dp)
    owners = [lax.rem(zp + j, n_zp) * 2 + zi for j in range(n_zp)]
    blocks = jnp.stack([o * n_dp + x for o in owners]).astype(I32)
    grads = passage_grads(blocks, low_t.shape[0] // (n_sh * n_dp), low_t, gs)

    summed = own_part + move(other_part, "dom", flip(n_dom, 1))
    summed, grads = lax.optimization_barrier((summed, grads))
    summed = summed.reshape(len(evens), n_zp, out_rows, depth)
    weight_grad = summed[0, 0]
    for i, e in enumerate(evens):
        for j in range(n_zp):
            if i == j == 0:
                continue
            pairs = []
            for d in range(n_dom):
                for s in range(n_sh):
                    pairs.append((d * n_sh + s, (d ^ e) * n_sh + (s + 2 * j) % n_sh))
            moved = move(summed[i, j], ("dom", "shard"), pairs)
            weight_grad = weight_grad + moved

    book_grad = None
    for j in reversed(range(n_zp)):
        part = word_grads(blocks[j : j + 1], held, words, grads[j], tile_codes)
        if j:
            part = move(part, "shard", ring(n_sh, 2 * j))
        book_grad = part if book_grad is None else book_grad + part
    return (weight_grad, book_grad[None])


def solution(mesh):
    sizes = [mesh.shape[a] for a in ("dom", "shard", "dp")]
    return jax.shard_map(
        functools.partial(compute, *sizes),
        mesh=mesh,
        in_specs=(
            P("dom", ("shard", "dp"), None),
            P(("dom", "shard", "dp"), None),
            P("dom", "shard", None, None),
            P("dom", "shard", None),
            P("dom", None),
            P("dom", None),
        ),
        out_specs=(P(("dom", "shard", "dp"), None), P("dom", ("shard", "dp"), None, None)),
        check_vma=False,
    )
```

profile of v0, /device:TPU:0, one launch (start us, length us, event | category | flops | bytes accessed | tf_op | source)
XLA Modules:
  0.0 117.5 jit_solution(8423229682997430568)
XLA Ops:
  0.6 3.1 %collective-permute-start.3 = (bf16[32,1024]{1,0:T(8,128)(2,1)}, bf16[32,1024]{1,0:T(8,128)(2,1)S(1)}, u32[]{:S(2)}, u32[]{:S(2)}) collective-permute-start(bf16[32,1024]{1,0:T(8,128)(2,1)} %param.7), channel_id=1, source_target_pairs={{0,2},{2,4},{4,6},{6,0},{1,3},{3,5},{5,7},{7,1},{8,10},{10,12},{12... | collective-permute-start | bytes 196616 | tf_op jit(solution)/shard_map/ppermute | solution.py:267
  3.7 2.1 %collective-permute-start.5 = (bf16[32,1024]{1,0:T(8,128)(2,1)}, bf16[32,1024]{1,0:T(8,128)(2,1)S(1)}, u32[]{:S(2)}, u32[]{:S(2)}) collective-permute-start(bf16[32,1024]{1,0:T(8,128)(2,1)} %param.7), channel_id=1, source_target_pairs={{0,6},{2,0},{4,2},{6,4},{1,7},{3,1},{5,3},{7,5},{8,14},{10,8},{12,... | collective-permute-start | bytes 196616 | tf_op jit(solution)/shard_map/ppermute | solution.py:267
  5.8 0.9 collective-permute-start.4
  6.8 1.0 convert_bitcast_fusion.refs_2_.refs_3_
  7.8 1.4 %collective-permute-start.15 = (bf16[32,8,256]{2,1,0:T(8,128)(2,1)S(1)}, bf16[32,8,256]{2,1,0:T(8,128)(2,1)S(1)}, u32[]{:S(2)}, u32[]{:S(2)}) collective-permute-start(bf16[32,8,256]{2,1,0:T(8,128)(2,1)S(1)} %convert_bitcast_fusion.refs_2_.refs_3_), channel_id=1, source_target_pairs={{0,6},{2,0},{4,2},{6,4},{1,7},{3,1},{5,3},{7,5},{8,14},{10,8},{12,... | collective-permute-start | bytes 393224 | tf_op jit(solution)/shard_map/ppermute | solution.py:283
  9.2 1.7 %collective-permute-start.14 = (bf16[32,8,256]{2,1,0:T(8,128)(2,1)S(1)}, bf16[32,8,256]{2,1,0:T(8,128)(2,1)S(1)}, u32[]{:S(2)}, u32[]{:S(2)}) collective-permute-start(bf16[32,8,256]{2,1,0:T(8,128)(2,1)S(1)} %convert_bitcast_fusion.refs_2_.refs_3_), channel_id=1, source_target_pairs={{0,4},{2,6},{4,0},{6,2},{1,5},{3,7},{5,1},{7,3},{8,12},{10,14},{12... | collective-permute-start | bytes 393224 | tf_op jit(solution)/shard_map/ppermute | solution.py:283
  11.1 0.7 convert_element_type.14
  11.8 1.1 convert_element_type.15
  13.1 0.7 fusion.3
  13.8 1.0 collective-permute-start.13
  14.8 2.9 %collective-permute-start.18 = (bf16[128,512]{1,0:T(8,128)(2,1)S(1)}, bf16[128,512]{1,0:T(8,128)(2,1)S(1)}, u32[]{:S(2)}, u32[]{:S(2)}) collective-permute-start(bf16[128,512]{1,0:T(8,128)(2,1)S(1)} %bitcast.102), channel_id=1, source_target_pairs={{0,6},{2,0},{4,2},{6,4},{1,7},{3,1},{5,3},{7,5},{8,14},{10,8},{12,... | collective-permute-start | bytes 393224 | tf_op jit(solution)/shard_map/ppermute | solution.py:290
  17.7 0.9 pad_maximum_fusion.refs_4_
  18.6 1.6 %collective-permute-start.6 = (bf16[4,32,1024]{2,1,0:T(8,128)(2,1)S(1)}, bf16[4,32,1024]{2,1,0:T(8,128)(2,1)S(1)}, u32[]{:S(2)}, u32[]{:S(2)}) collective-permute-start(bf16[4,32,1024]{2,1,0:T(8,128)(2,1)S(1)} %pad_maximum_fusion.refs_4_), channel_id=1, source_target_pairs={{0,1},{1,0},{2,3},{3,2},{4,5},{5,4},{6,7},{7,6},{8,9},{9,8},{10,11... | collective-permute-start | bytes 786440 | tf_op jit(solution)/shard_map/ppermute | solution.py:296
  20.2 5.2 %collective-permute-done.14.refs_4_.refs_5_ = bf16[32,8,256]{2,1,0:T(8,128)(2,1)S(1)} collective-permute-done((bf16[32,8,256]{2,1,0:T(8,128)(2,1)S(1)}, bf16[32,8,256]{2,1,0:T(8,128)(2,1)S(1)}, u32[]{:S(2)}, u32[]{:S(2)}) %collective-permute-start.14) | collective-permute-done | bytes 131104 | tf_op jit(solution)/shard_map/ppermute | solution.py:283
  25.4 0.5 collective-permute-start.16
  25.9 2.4 %collective-permute-start.21 = (bf16[128,512]{1,0:T(8,128)(2,1)S(1)}, bf16[128,512]{1,0:T(8,128)(2,1)S(1)}, u32[]{:S(2)}, u32[]{:S(2)}) collective-permute-start(bf16[128,512]{1,0:T(8,128)(2,1)S(1)} %collective-permute-done.18.refs_2_), channel_id=1, source_target_pairs={{0,1},{1,0},{2,3},{3,2},{4,5},{5,4},{6,7},{7,6},{8,9},{9,8},{10,11... | collective-permute-start | bytes 393224 | tf_op jit(solution)/shard_map/ppermute | solution.py:294
  29.0 6.3 %collective-permute-start.2 = (bf16[128,1024]{1,0:T(8,128)(2,1)S(1)}, bf16[128,1024]{1,0:T(8,128)(2,1)S(1)}, u32[]{:S(2)}, u32[]{:S(2)}) collective-permute-start(bf16[128,1024]{1,0:T(8,128)(2,1)S(1)} %bitcast.107), channel_id=1, source_target_pairs={{0,3},{1,2},{2,1},{3,0},{4,7},{5,6},{6,5},{7,4},{8,11},{9,10},{10,... | collective-permute-start | bytes 786440 | tf_op jit(solution)/shard_map/ppermute | solution.py:278
  35.2 1.1 collective-permute-start.1
  36.4 1.5 %collective-permute-start.7 = (bf16[4,32,1024]{2,1,0:T(8,128)(2,1)S(1)}, bf16[4,32,1024]{2,1,0:T(8,128)(2,1)S(1)}, u32[]{:S(2)}, u32[]{:S(2)}) collective-permute-start(bf16[4,32,1024]{2,1,0:T(8,128)(2,1)S(1)} %pad_maximum_fusion.refs_4_), channel_id=1, source_target_pairs={{0,16},{8,24},{16,0},{24,8},{1,17},{9,25},{17,1},{25,9},{2,18},{10... | collective-permute-start | bytes 786440 | tf_op jit(solution)/shard_map/ppermute | solution.py:300
  37.9 0.5 collective-permute-start.20
  38.4 0.9 collective-permute-start.8
  39.3 6.1 %shard_map.78 = (bf16[3,1024,512]{2,1,0:T(8,128)(2,1)S(1)}, s32[3,128,512]{2,1,0:T(8,128)S(1)}) custom-call(s32[4]{0:T(128)S(1)} %pad_add_fusion.1.place_ref, bf16[128,512]{1,0:T(8,128)(2,1)S(1)} %collective-permute-done.16.refs_0_, bf16[128,512]{1,0:T(8,128)(2,1)S(1)} %collective-permute-done.17.refs_1_, ...), custom_call_target="tpu_custom_call" | custom-call | flops 3000000000 | bytes 6000000 | tf_op jit(solution)/shard_map/pallas_call | solution.py:73
  45.4 4.4 %collective-permute-done.20.refs_1_ = bf16[128,512]{1,0:T(8,128)(2,1)S(1)} collective-permute-done((bf16[128,512]{1,0:T(8,128)(2,1)S(1)}, bf16[128,512]{1,0:T(8,128)(2,1)S(1)}, u32[]{:S(2)}, u32[]{:S(2)}) %collective-permute-start.20) | collective-permute-done | bytes 131104 | tf_op jit(solution)/shard_map/ppermute | solution.py:294
  49.7 0.5 collective-permute-start.19
  50.2 4.1 %shard_map.77 = (bf16[2,1024,512]{2,1,0:T(8,128)(2,1)S(1)}, s32[2,128,512]{2,1,0:T(8,128)S(1)}) custom-call(s32[4]{0:T(128)S(1)} %pad_add_fusion.1.place_ref, bf16[128,512]{1,0:T(8,128)(2,1)S(1)} %bitcast.105, bf16[128,512]{1,0:T(8,128)(2,1)S(1)} %bitcast.106, bf16[32,8,256]{2,1,0:T(8,128)(2,1)S(1)} %convert_bitcast_fusion.refs_2_.refs_3_, ...), custom_call_target="tpu_custom_call" | custom-call | flops 2000000000 | bytes 4000000 | tf_op jit(solution)/shard_map/pallas_call | solution.py:73
  54.4 0.8 collective-permute-done.19.refs_0_
  55.1 0.7 collective-permute-start
  55.9 0.5 collective-permute-start.10
  56.5 0.4 collective-permute-start.12
  56.9 5.9 %shard_map.79 = (bf16[3,1024,512]{2,1,0:T(8,128)(2,1)S(1)}, s32[3,128,512]{2,1,0:T(8,128)S(1)}) custom-call(s32[4]{0:T(128)S(1)} %pad_add_fusion.1.place_ref, bf16[128,512]{1,0:T(8,128)(2,1)S(1)} %collective-permute-done.19.refs_0_, bf16[128,512]{1,0:T(8,128)(2,1)S(1)} %collective-permute-done.20.refs_1_, ...), custom_call_target="tpu_custom_call" | custom-call | flops 3000000000 | bytes 6000000 | tf_op jit(solution)/shard_map/pallas_call | solution.py:73
  62.8 0.9 copy-done.7
  63.7 16.8 %shard_map.80 = (bf16[8,512,512]{2,1,0:T(8,128)(2,1)S(1)}, bf16[1024,512]{1,0:T(8,128)(2,1)S(1)}, f32[128,1024]{1,0:T(8,128)S(1)}, f32[128,1024]{1,0:T(8,128)S(1)}) custom-call(s32[32]{0:T(128)S(1)} %broadcast_multiply_fusion.woff_ref, s32[8]{0:T(128)S(1)} %stack.233.tbase_ref, s32[256,1]{1,0:T(8,128)S(1)} %add.469.frow_ref, s32[512,1]{1,0:T(8,128)S(1)} %copy.13.pos_ref, ...), custom_call_target="tpu_custom_call" | custom-call | flops 20000000000 | bytes 20000000 | tf_op jit(solution)/shard_map/pallas_call | solution.py:152
  80.5 2.0 %copy-done.1 = bf16[8,512,512]{2,1,0:T(8,128)(2,1)} copy-done((bf16[8,512,512]{2,1,0:T(8,128)(2,1)}, bf16[8,512,512]{2,1,0:T(8,128)(2,1)S(1)}, u32[]{:S(2)}) %copy-start.1) | copy-done | bytes 4194328
  82.4 1.0 copy-done.3
  83.6 2.2 %copy-done.2 = bf16[8,512,512]{2,1,0:T(8,128)(2,1)S(1)} copy-done((bf16[8,512,512]{2,1,0:T(8,128)(2,1)S(1)}, bf16[8,512,512]{2,1,0:T(8,128)(2,1)}, u32[]{:S(2)}) %copy-start.2) | copy-done | bytes 4194328
  85.8 1.2 %copy-done.4 = bf16[1024,512]{1,0:T(8,128)(2,1)S(1)} copy-done((bf16[1024,512]{1,0:T(8,128)(2,1)S(1)}, bf16[1024,512]{1,0:T(8,128)(2,1)}, u32[]{:S(2)}) %copy-start.4) | copy-done | bytes 1048600
  87.0 1.8 %shard_map.81 = (f32[128,4096]{1,0:T(8,128)S(1)}, f32[128,4096]{1,0:T(8,128)S(1)}) custom-call(s32[2]{0:T(128)S(1)} %pad_add_fusion.2.blocks_ref, bf16[1024,512]{1,0:T(8,128)(2,1)S(1)} %copy-done.4, bf16[8,512,512]{2,1,0:T(8,128)(2,1)S(1)} %copy-done.2), custom_call_target="tpu_custom_call" | custom-call | flops 3000000000 | bytes 8000000 | tf_op jit(solution)/shard_map/pallas_call | solution.py:189
  88.9 2.8 %shard_map.82 = f32[16,8,256]{2,1,0:T(8,128)S(1)} custom-call(s32[1]{0:T(128)} %bitcast.74.block_ref, f32[128,4096]{1,0:T(8,128)S(1)} %get-tuple-element.27.grads_ref, s32[2,128,512]{2,1,0:T(8,128)S(1)} %get-tuple-element.28.refs_0_, s32[3,128,512]{2,1,0:T(8,128)S(1)} %copy-done.6, s32[3,128,512]{2,1,0:T(8,128)S(1)} %copy-done.8), custom_call_target="tpu_custom_call" | custom-call | flops 3000000000 | bytes 4000000 | tf_op jit(solution)/shard_map/pallas_call | solution.py:246
  91.7 2.8 %shard_map.83 = f32[16,8,256]{2,1,0:T(8,128)S(1)} custom-call(s32[1]{0:T(128)} %bitcast.73.block_ref, f32[128,4096]{1,0:T(8,128)S(1)} %get-tuple-element.31.grads_ref, s32[2,128,512]{2,1,0:T(8,128)S(1)} %get-tuple-element.28.refs_0_, s32[3,128,512]{2,1,0:T(8,128)S(1)} %copy-done.6, s32[3,128,512]{2,1,0:T(8,128)S(1)} %copy-done.8), custom_call_target="tpu_custom_call" | custom-call | flops 3000000000 | bytes 4000000 | tf_op jit(solution)/shard_map/pallas_call | solution.py:246
  94.5 1.2 collective-permute-start.26
  95.7 1.9 %collective-permute-start.23 = (f32[32,1024]{1,0:T(8,128)S(1)}, f32[32,1024]{1,0:T(8,128)S(1)}, u32[]{:S(2)}, u32[]{:S(2)}) collective-permute-start(f32[32,1024]{1,0:T(8,128)S(1)} %get-tuple-element.32), channel_id=1, source_target_pairs={{0,4},{2,6},{4,0},{6,2},{8,12},{10,14},{12,8},{14,10},{16,20},{18,... | collective-permute-start | bytes 393224 | tf_op jit(solution)/shard_map/ppermute | solution.py:364
  97.5 2.1 %collective-permute-start.25 = (f32[32,1024]{1,0:T(8,128)S(1)}, f32[32,1024]{1,0:T(8,128)S(1)}, u32[]{:S(2)}, u32[]{:S(2)}) collective-permute-start(f32[32,1024]{1,0:T(8,128)S(1)} %get-tuple-element.33), channel_id=1, source_target_pairs={{0,20},{2,22},{4,16},{6,18},{8,28},{10,30},{12,24},{14,26},{16,4},... | collective-permute-start | bytes 393224 | tf_op jit(solution)/shard_map/ppermute | solution.py:364
  99.6 0.5 collective-permute-start.24
  100.1 10.1 %collective-permute-done.26 = f32[16,8,256]{2,1,0:T(8,128)S(1)} collective-permute-done((f32[16,8,256]{2,1,0:T(8,128)S(1)}, f32[16,8,256]{2,1,0:T(8,128)S(1)}, u32[]{:S(2)}, u32[]{:S(2)}) %collective-permute-start.26) | collective-permute-done | bytes 131104 | tf_op jit(solution)/shard_map/ppermute | solution.py:371
  110.2 0.7 add_bitcast_fusion
  110.9 2.1 %collective-permute-done.23 = f32[32,1024]{1,0:T(8,128)S(1)} collective-permute-done((f32[32,1024]{1,0:T(8,128)S(1)}, f32[32,1024]{1,0:T(8,128)S(1)}, u32[]{:S(2)}, u32[]{:S(2)}) %collective-permute-start.23) | collective-permute-done | bytes 131104 | tf_op jit(solution)/shard_map/ppermute | solution.py:364
  113.0 3.7 %collective-permute-done.25 = f32[32,1024]{1,0:T(8,128)S(1)} collective-permute-done((f32[32,1024]{1,0:T(8,128)S(1)}, f32[32,1024]{1,0:T(8,128)S(1)}, u32[]{:S(2)}, u32[]{:S(2)}) %collective-permute-start.25) | collective-permute-done | bytes 131104 | tf_op jit(solution)/shard_map/ppermute | solution.py:364
  116.8 0.7 fusion.2
  (56 shorter events, 1.6 us)
Async XLA Ops:
  0.6 28.3 %copy-start = (bf16[1,128,1024]{2,1,0:T(8,128)(2,1)S(1)}, bf16[1,128,1024]{2,1,0:T(8,128)(2,1)}, u32[]{:S(2)}) copy-start(bf16[1,128,1024]{2,1,0:T(8,128)(2,1)} %param.6) | copy-start | bytes 786436
  0.6 13.2 %collective-permute-start.3 = (bf16[32,1024]{1,0:T(8,128)(2,1)}, bf16[32,1024]{1,0:T(8,128)(2,1)S(1)}, u32[]{:S(2)}, u32[]{:S(2)}) collective-permute-start(bf16[32,1024]{1,0:T(8,128)(2,1)} %param.7), channel_id=1, source_target_pairs={{0,2},{2,4},{4,6},{6,0},{1,3},{3,5},{5,7},{7,1},{8,10},{10,12},{12... | collective-permute-start | bytes 196616 | tf_op jit(solution)/shard_map/ppermute | solution.py:267
  3.7 11.1 %collective-permute-start.5 = (bf16[32,1024]{1,0:T(8,128)(2,1)}, bf16[32,1024]{1,0:T(8,128)(2,1)S(1)}, u32[]{:S(2)}, u32[]{:S(2)}) collective-permute-start(bf16[32,1024]{1,0:T(8,128)(2,1)} %param.7), channel_id=1, source_target_pairs={{0,6},{2,0},{4,2},{6,4},{1,7},{3,1},{5,3},{7,5},{8,14},{10,8},{12,... | collective-permute-start | bytes 196616 | tf_op jit(solution)/shard_map/ppermute | solution.py:267
  5.8 11.9 %collective-permute-start.4 = (bf16[32,1024]{1,0:T(8,128)(2,1)}, bf16[32,1024]{1,0:T(8,128)(2,1)S(1)}, u32[]{:S(2)}, u32[]{:S(2)}) collective-permute-start(bf16[32,1024]{1,0:T(8,128)(2,1)} %param.7), channel_id=1, source_target_pairs={{0,4},{2,6},{4,0},{6,2},{1,5},{3,7},{5,1},{7,3},{8,12},{10,14},{12... | collective-permute-start | bytes 196616 | tf_op jit(solution)/shard_map/ppermute | solution.py:267
  7.8 12.4 %collective-permute-start.15 = (bf16[32,8,256]{2,1,0:T(8,128)(2,1)S(1)}, bf16[32,8,256]{2,1,0:T(8,128)(2,1)S(1)}, u32[]{:S(2)}, u32[]{:S(2)}) collective-permute-start(bf16[32,8,256]{2,1,0:T(8,128)(2,1)S(1)} %convert_bitcast_fusion.refs_2_.refs_3_), channel_id=1, source_target_pairs={{0,6},{2,0},{4,2},{6,4},{1,7},{3,1},{5,3},{7,5},{8,14},{10,8},{12,... | collective-permute-start | bytes 393224 | tf_op jit(solution)/shard_map/ppermute | solution.py:283
  9.2 16.2 %collective-permute-start.14 = (bf16[32,8,256]{2,1,0:T(8,128)(2,1)S(1)}, bf16[32,8,256]{2,1,0:T(8,128)(2,1)S(1)}, u32[]{:S(2)}, u32[]{:S(2)}) collective-permute-start(bf16[32,8,256]{2,1,0:T(8,128)(2,1)S(1)} %convert_bitcast_fusion.refs_2_.refs_3_), channel_id=1, source_target_pairs={{0,4},{2,6},{4,0},{6,2},{1,5},{3,7},{5,1},{7,3},{8,12},{10,14},{12... | collective-permute-start | bytes 393224 | tf_op jit(solution)/shard_map/ppermute | solution.py:283
  13.8 15.1 %collective-permute-start.13 = (bf16[32,8,256]{2,1,0:T(8,128)(2,1)S(1)}, bf16[32,8,256]{2,1,0:T(8,128)(2,1)S(1)}, u32[]{:S(2)}, u32[]{:S(2)}) collective-permute-start(bf16[32,8,256]{2,1,0:T(8,128)(2,1)S(1)} %convert_bitcast_fusion.refs_2_.refs_3_), channel_id=1, source_target_pairs={{0,2},{2,4},{4,6},{6,0},{1,3},{3,5},{5,7},{7,1},{8,10},{10,12},{12... | collective-permute-start | bytes 393224 | tf_op jit(solution)/shard_map/ppermute | solution.py:283
  14.8 11.0 %collective-permute-start.18 = (bf16[128,512]{1,0:T(8,128)(2,1)S(1)}, bf16[128,512]{1,0:T(8,128)(2,1)S(1)}, u32[]{:S(2)}, u32[]{:S(2)}) collective-permute-start(bf16[128,512]{1,0:T(8,128)(2,1)S(1)} %bitcast.102), channel_id=1, source_target_pairs={{0,6},{2,0},{4,2},{6,4},{1,7},{3,1},{5,3},{7,5},{8,14},{10,8},{12,... | collective-permute-start | bytes 393224 | tf_op jit(solution)/shard_map/ppermute | solution.py:290
  18.6 19.8 %collective-permute-start.6 = (bf16[4,32,1024]{2,1,0:T(8,128)(2,1)S(1)}, bf16[4,32,1024]{2,1,0:T(8,128)(2,1)S(1)}, u32[]{:S(2)}, u32[]{:S(2)}) collective-permute-start(bf16[4,32,1024]{2,1,0:T(8,128)(2,1)S(1)} %pad_maximum_fusion.refs_4_), channel_id=1, source_target_pairs={{0,1},{1,0},{2,3},{3,2},{4,5},{5,4},{6,7},{7,6},{8,9},{9,8},{10,11... | collective-permute-start | bytes 786440 | tf_op jit(solution)/shard_map/ppermute | solution.py:296
  20.1 15.1 %collective-permute-start.17 = (bf16[128,512]{1,0:T(8,128)(2,1)S(1)}, bf16[128,512]{1,0:T(8,128)(2,1)S(1)}, u32[]{:S(2)}, u32[]{:S(2)}) collective-permute-start(bf16[128,512]{1,0:T(8,128)(2,1)S(1)} %bitcast.103), channel_id=1, source_target_pairs={{0,4},{2,6},{4,0},{6,2},{1,5},{3,7},{5,1},{7,3},{8,12},{10,14},{12... | collective-permute-start | bytes 393224 | tf_op jit(solution)/shard_map/ppermute | solution.py:290
  25.4 11.0 %collective-permute-start.16 = (bf16[128,512]{1,0:T(8,128)(2,1)S(1)}, bf16[128,512]{1,0:T(8,128)(2,1)S(1)}, u32[]{:S(2)}, u32[]{:S(2)}) collective-permute-start(bf16[128,512]{1,0:T(8,128)(2,1)S(1)} %bitcast.104), channel_id=1, source_target_pairs={{0,2},{2,4},{4,6},{6,0},{1,3},{3,5},{5,7},{7,1},{8,10},{10,12},{12... | collective-permute-start | bytes 393224 | tf_op jit(solution)/shard_map/ppermute | solution.py:290
  25.9 12.0 %collective-permute-start.21 = (bf16[128,512]{1,0:T(8,128)(2,1)S(1)}, bf16[128,512]{1,0:T(8,128)(2,1)S(1)}, u32[]{:S(2)}, u32[]{:S(2)}) collective-permute-start(bf16[128,512]{1,0:T(8,128)(2,1)S(1)} %collective-permute-done.18.refs_2_), channel_id=1, source_target_pairs={{0,1},{1,0},{2,3},{3,2},{4,5},{5,4},{6,7},{7,6},{8,9},{9,8},{10,11... | collective-permute-start | bytes 393224 | tf_op jit(solution)/shard_map/ppermute | solution.py:294
  29.0 26.9 %collective-permute-start.2 = (bf16[128,1024]{1,0:T(8,128)(2,1)S(1)}, bf16[128,1024]{1,0:T(8,128)(2,1)S(1)}, u32[]{:S(2)}, u32[]{:S(2)}) collective-permute-start(bf16[128,1024]{1,0:T(8,128)(2,1)S(1)} %bitcast.107), channel_id=1, source_target_pairs={{0,3},{1,2},{2,1},{3,0},{4,7},{5,6},{6,5},{7,4},{8,11},{9,10},{10,... | collective-permute-start | bytes 786440 | tf_op jit(solution)/shard_map/ppermute | solution.py:278
  35.2 20.6 %collective-permute-start.1 = (bf16[128,1024]{1,0:T(8,128)(2,1)S(1)}, bf16[128,1024]{1,0:T(8,128)(2,1)S(1)}, u32[]{:S(2)}, u32[]{:S(2)}) collective-permute-start(bf16[128,1024]{1,0:T(8,128)(2,1)S(1)} %bitcast.108), channel_id=1, source_target_pairs={{0,1},{1,0},{2,3},{3,2},{4,5},{5,4},{6,7},{7,6},{8,9},{9,8},{10,11... | collective-permute-start | bytes 786440 | tf_op jit(solution)/shard_map/ppermute | solution.py:278
  36.4 20.0 %collective-permute-start.7 = (bf16[4,32,1024]{2,1,0:T(8,128)(2,1)S(1)}, bf16[4,32,1024]{2,1,0:T(8,128)(2,1)S(1)}, u32[]{:S(2)}, u32[]{:S(2)}) collective-permute-start(bf16[4,32,1024]{2,1,0:T(8,128)(2,1)S(1)} %pad_maximum_fusion.refs_4_), channel_id=1, source_target_pairs={{0,16},{8,24},{16,0},{24,8},{1,17},{9,25},{17,1},{25,9},{2,18},{10... | collective-permute-start | bytes 786440 | tf_op jit(solution)/shard_map/ppermute | solution.py:300
  37.9 11.9 %collective-permute-start.20 = (bf16[128,512]{1,0:T(8,128)(2,1)S(1)}, bf16[128,512]{1,0:T(8,128)(2,1)S(1)}, u32[]{:S(2)}, u32[]{:S(2)}) collective-permute-start(bf16[128,512]{1,0:T(8,128)(2,1)S(1)} %collective-permute-done.17.refs_1_), channel_id=1, source_target_pairs={{0,1},{1,0},{2,3},{3,2},{4,5},{5,4},{6,7},{7,6},{8,9},{9,8},{10,11... | collective-permute-start | bytes 393224 | tf_op jit(solution)/shard_map/ppermute | solution.py:294
  38.4 18.0 %collective-permute-start.8 = (bf16[4,32,1024]{2,1,0:T(8,128)(2,1)S(1)}, bf16[4,32,1024]{2,1,0:T(8,128)(2,1)S(1)}, u32[]{:S(2)}, u32[]{:S(2)}) collective-permute-start(bf16[4,32,1024]{2,1,0:T(8,128)(2,1)S(1)} %collective-permute-done.6.refs_5_), channel_id=1, source_target_pairs={{0,16},{8,24},{16,0},{24,8},{1,17},{9,25},{17,1},{25,9},{2,18},{10... | collective-permute-start | bytes 786440 | tf_op jit(solution)/shard_map/ppermute | solution.py:300
  45.4 9.0 %copy-start.5 = (s32[3,128,512]{2,1,0:T(8,128)}, s32[3,128,512]{2,1,0:T(8,128)S(1)}, u32[]{:S(2)}) copy-start(s32[3,128,512]{2,1,0:T(8,128)S(1)} %get-tuple-element.29.refs_1_) | copy-start | bytes 2359300
  49.7 5.4 %collective-permute-start.19 = (bf16[128,512]{1,0:T(8,128)(2,1)S(1)}, bf16[128,512]{1,0:T(8,128)(2,1)S(1)}, u32[]{:S(2)}, u32[]{:S(2)}) collective-permute-start(bf16[128,512]{1,0:T(8,128)(2,1)S(1)} %collective-permute-done.16.refs_0_), channel_id=1, source_target_pairs={{0,1},{1,0},{2,3},{3,2},{4,5},{5,4},{6,7},{7,6},{8,9},{9,8},{10,11... | collective-permute-start | bytes 393224 | tf_op jit(solution)/shard_map/ppermute | solution.py:294
  55.1 8.5 %collective-permute-start = (bf16[128,1024]{1,0:T(8,128)(2,1)S(1)}, bf16[128,1024]{1,0:T(8,128)(2,1)S(1)}, u32[]{:S(2)}, u32[]{:S(2)}) collective-permute-start(bf16[128,1024]{1,0:T(8,128)(2,1)S(1)} %bitcast.109), channel_id=1, source_target_pairs={{0,2},{1,3},{2,0},{3,1},{4,6},{5,7},{6,4},{7,5},{8,10},{9,11},{10,... | collective-permute-start | bytes 786440 | tf_op jit(solution)/shard_map/ppermute | solution.py:278
  55.9 7.8 %collective-permute-start.9 = (bf16[4,32,1024]{2,1,0:T(8,128)(2,1)S(1)}, bf16[4,32,1024]{2,1,0:T(8,128)(2,1)S(1)}, u32[]{:S(2)}, u32[]{:S(2)}) collective-permute-start(bf16[4,32,1024]{2,1,0:T(8,128)(2,1)S(1)} %pad_maximum_fusion.refs_4_), channel_id=1, source_target_pairs={{0,8},{8,0},{16,24},{24,16},{1,9},{9,1},{17,25},{25,17},{2,10},{10... | collective-permute-start | bytes 786440 | tf_op jit(solution)/shard_map/ppermute | solution.py:301
  55.9 7.8 %collective-permute-start.10 = (bf16[4,32,1024]{2,1,0:T(8,128)(2,1)S(1)}, bf16[4,32,1024]{2,1,0:T(8,128)(2,1)S(1)}, u32[]{:S(2)}, u32[]{:S(2)}) collective-permute-start(bf16[4,32,1024]{2,1,0:T(8,128)(2,1)S(1)} %collective-permute-done.6.refs_5_), channel_id=1, source_target_pairs={{0,8},{8,0},{16,24},{24,16},{1,9},{9,1},{17,25},{25,17},{2,10},{10... | collective-permute-start | bytes 786440 | tf_op jit(solution)/shard_map/ppermute | solution.py:301
  56.4 7.3 %collective-permute-start.11 = (bf16[4,32,1024]{2,1,0:T(8,128)(2,1)S(1)}, bf16[4,32,1024]{2,1,0:T(8,128)(2,1)S(1)}, u32[]{:S(2)}, u32[]{:S(2)}) collective-permute-start(bf16[4,32,1024]{2,1,0:T(8,128)(2,1)S(1)} %collective-permute-done.7.refs_6_), channel_id=1, source_target_pairs={{0,8},{8,0},{16,24},{24,16},{1,9},{9,1},{17,25},{25,17},{2,10},{10... | collective-permute-start | bytes 786440 | tf_op jit(solution)/shard_map/ppermute | solution.py:301
  56.5 7.2 %collective-permute-start.12 = (bf16[4,32,1024]{2,1,0:T(8,128)(2,1)S(1)}, bf16[4,32,1024]{2,1,0:T(8,128)(2,1)S(1)}, u32[]{:S(2)}, u32[]{:S(2)}) collective-permute-start(bf16[4,32,1024]{2,1,0:T(8,128)(2,1)S(1)} %collective-permute-done.8.refs_7_), channel_id=1, source_target_pairs={{0,8},{8,0},{16,24},{24,16},{1,9},{9,1},{17,25},{25,17},{2,10},{10... | collective-permute-start | bytes 786440 | tf_op jit(solution)/shard_map/ppermute | solution.py:301
  62.8 0.9 copy-start.7
  80.5 2.0 %copy-start.1 = (bf16[8,512,512]{2,1,0:T(8,128)(2,1)}, bf16[8,512,512]{2,1,0:T(8,128)(2,1)S(1)}, u32[]{:S(2)}) copy-start(bf16[8,512,512]{2,1,0:T(8,128)(2,1)S(1)} %get-tuple-element.23.gs_ref) | copy-start | bytes 12582916
  82.4 1.0 copy-start.3
  83.4 5.4 %collective-permute-start.22 = (f32[128,1024]{1,0:T(8,128)S(1)}, f32[128,1024]{1,0:T(8,128)S(1)}, u32[]{:S(2)}, u32[]{:S(2)}) collective-permute-start(f32[128,1024]{1,0:T(8,128)S(1)} %get-tuple-element.21), channel_id=1, source_target_pairs={{0,8},{8,0},{16,24},{24,16},{1,9},{9,1},{17,25},{25,17},{2,10},{10... | collective-permute-start | bytes 1572872 | tf_op jit(solution)/shard_map/ppermute | solution.py:352
  83.6 2.2 %copy-start.2 = (bf16[8,512,512]{2,1,0:T(8,128)(2,1)S(1)}, bf16[8,512,512]{2,1,0:T(8,128)(2,1)}, u32[]{:S(2)}) copy-start(bf16[8,512,512]{2,1,0:T(8,128)(2,1)} %copy-done.1) | copy-start | bytes 12582916
  85.8 1.2 %copy-start.4 = (bf16[1024,512]{1,0:T(8,128)(2,1)S(1)}, bf16[1024,512]{1,0:T(8,128)(2,1)}, u32[]{:S(2)}) copy-start(bf16[1024,512]{1,0:T(8,128)(2,1)} %copy-done.3) | copy-start | bytes 3145732
  87.0 1.9 %copy-start.6 = (s32[3,128,512]{2,1,0:T(8,128)S(1)}, s32[3,128,512]{2,1,0:T(8,128)}, u32[]{:S(2)}) copy-start(s32[3,128,512]{2,1,0:T(8,128)} %copy-done.5) | copy-start | bytes 2359300
  87.0 1.9 %copy-start.8 = (s32[3,128,512]{2,1,0:T(8,128)S(1)}, s32[3,128,512]{2,1,0:T(8,128)}, u32[]{:S(2)}) copy-start(s32[3,128,512]{2,1,0:T(8,128)} %copy-done.7) | copy-start | bytes 2359300
  94.5 15.7 %collective-permute-start.26 = (f32[16,8,256]{2,1,0:T(8,128)S(1)}, f32[16,8,256]{2,1,0:T(8,128)S(1)}, u32[]{:S(2)}, u32[]{:S(2)}) collective-permute-start(f32[16,8,256]{2,1,0:T(8,128)S(1)} %shard_map.82), channel_id=1, source_target_pairs={{0,4},{2,6},{4,0},{6,2},{1,5},{3,7},{5,1},{7,3},{8,12},{10,14},{12... | collective-permute-start | bytes 393224 | tf_op jit(solution)/shard_map/ppermute | solution.py:371
  95.7 17.4 %collective-permute-start.23 = (f32[32,1024]{1,0:T(8,128)S(1)}, f32[32,1024]{1,0:T(8,128)S(1)}, u32[]{:S(2)}, u32[]{:S(2)}) collective-permute-start(f32[32,1024]{1,0:T(8,128)S(1)} %get-tuple-element.32), channel_id=1, source_target_pairs={{0,4},{2,6},{4,0},{6,2},{8,12},{10,14},{12,8},{14,10},{16,20},{18,... | collective-permute-start | bytes 393224 | tf_op jit(solution)/shard_map/ppermute | solution.py:364
  97.5 19.2 %collective-permute-start.25 = (f32[32,1024]{1,0:T(8,128)S(1)}, f32[32,1024]{1,0:T(8,128)S(1)}, u32[]{:S(2)}, u32[]{:S(2)}) collective-permute-start(f32[32,1024]{1,0:T(8,128)S(1)} %get-tuple-element.33), channel_id=1, source_target_pairs={{0,20},{2,22},{4,16},{6,18},{8,28},{10,30},{12,24},{14,26},{16,4},... | collective-permute-start | bytes 393224 | tf_op jit(solution)/shard_map/ppermute | solution.py:364
  99.6 17.2 %collective-permute-start.24 = (f32[32,1024]{1,0:T(8,128)S(1)}, f32[32,1024]{1,0:T(8,128)S(1)}, u32[]{:S(2)}, u32[]{:S(2)}) collective-permute-start(f32[32,1024]{1,0:T(8,128)S(1)} %get-tuple-element.34), channel_id=1, source_target_pairs={{0,16},{2,18},{4,20},{6,22},{8,24},{10,26},{12,28},{14,30},{16,0},... | collective-permute-start | bytes 393224 | tf_op jit(solution)/shard_map/ppermute | solution.py:364
where the time goes:
time: 118 us; the launch traced here: 117 us
  Pallas kernels  40.2 us (34%)
  starting transfers between devices  35.8 us (30%)
  waiting for transfers between devices  26.3 us (22%)
  local copies, waits for them, and re-layouts  8.99 us (8%)
  other arithmetic  5.29 us (4%)
    pallas_call x1, Pallas kernels, main(): pl.pallas_call(functools.partial(main_kernel, n_q, n_w, n_g), out_shape=(...  16.8 us
    pallas_call x3, Pallas kernels, rebuild(): pl.pallas_call(functools.partial(rebuild_kernel, n_t, n_b), out_shape=(ja...  16 us
    ppermute x1, waiting for transfers between devices, compute(): part = move(part, 'shard', ring(n_sh, 2 * j))  10.1 us
    ppermute x3, starting transfers between devices, compute(): q_pieces.append(q if t == a == 0 else move(q, ('shard', 'dp'), pairs))  8.09 us
    unnamed x18, local copies, waits for them, and re-layouts  7.28 us
    ppermute x3, starting transfers between devices, compute(): move(encoder_weight, 'shard', ring(n_sh, k))  6.14 us
    ppermute x3, waiting for transfers between devices, compute(): moved = move(summed[i, j], ('dom', 'shard'), pairs)  5.88 us
    pallas_call x2, Pallas kernels, word_grads(): pl.pallas_call(functools.partial(words_kernel, words), out_shape=jax.Shap...  5.57 us
  transfers between devices with their start and end apart: 27, of which 6 were waited for; matrix products, arithmetic and copies ran while one was open for 5% of the time, Pallas kernels for 15%

commit v1 on v0

--- a/solution.py
+++ b/solution.py
@@ -29,12 +29,16 @@
     return pl.CostEstimate(flops=flops, bytes_accessed=bytes_accessed, transcendentals=0)
 
 
-def rebuild_kernel(n_t, n_b, place_ref, *refs):
-    code_refs, books, (out_ref, codes_ref, table) = refs[:n_t], refs[n_t : n_t + n_b], refs[n_t + n_b :]
+def rebuild_kernel(n_t, n_b, place_ref, blocks_ref, *refs):
+    code_refs, books = refs[:n_t], refs[n_t : n_t + n_b]
+    out_ref, kept_ref, codes_ref, table = refs[n_t + n_b :]
     held, sub, words = books[0].shape
     columns = code_refs[0].shape[1]
+    kept = kept_ref.shape[2]
     for i, code_ref in enumerate(code_refs):
         codes_ref[i] = code_ref[...].astype(I32)
+        for b in range(kept_ref.shape[1]):
+            kept_ref[i, b] = codes_ref[i, pl.ds(pl.multiple_of(blocks_ref[b] * kept, kept), kept), :]
     for piece, book_ref in enumerate(books):
         table[pl.ds(place_ref[piece] * held, held)] = book_ref[...].astype(F32)
 
@@ -66,7 +70,7 @@
     lax.fori_loop(0, n_t * n_b, body, 0)
 
 
-def rebuild(place, codes, books):
+def rebuild(place, blocks, kept, codes, books):
     n_t, n_b = len(codes), len(books)
     subspaces, columns = codes[0].shape
     _, sub, words = books[0].shape
@@ -74,22 +78,25 @@
         functools.partial(rebuild_kernel, n_t, n_b),
         out_shape=(
             jax.ShapeDtypeStruct((n_t, subspaces * sub, columns), BF16),
-            jax.ShapeDtypeStruct((n_t, subspaces, columns), I32),
+            jax.ShapeDtypeStruct((n_t, blocks.shape[0], kept, columns), I32),
         ),
-        in_specs=[SMEM] + [VMEM] * (n_t + n_b),
+        in_specs=[SMEM, SMEM] + [VMEM] * (n_t + n_b),
         out_specs=(VMEM, VMEM),
-        scratch_shapes=[pltpu.VMEM((subspaces, sub, words), F32)],
+        scratch_shapes=[
+            pltpu.VMEM((n_t, subspaces, columns), I32),
+            pltpu.VMEM((subspaces, sub, words), F32),
+        ],
         compiler_params=pltpu.CompilerParams(vmem_limit_bytes=(6 + n_t) * MIB),
         cost_estimate=cost(n_t * 10**9, n_t * 2 * 10**6),
-    )(place, *codes, *books)
-
-
-def main_kernel(n_q, n_w, n_g, woff_ref, tbase_ref, frow_ref, pos_ref, wt_ref, *refs):
+    )(place, blocks, *codes, *books)
+
+
+def main_kernel(n_q, n_w, n_g, woff_ref, tbase_ref, blocks_ref, frow_ref, pos_ref, wt_ref, *refs):
     q_refs, refs = refs[:n_q], refs[n_q:]
     w_refs, refs = refs[:n_w], refs[n_w:]
     g_refs, refs = refs[:n_g], refs[n_g:]
-    gs_ref, nt_ref, own_ref, other_ref = refs[:4]
-    w, q, exps, normed, total, gn = refs[4:]
+    own_ref, other_ref, grads_refs, refs = refs[0], refs[1], refs[2:-8], refs[-8:]
+    w, q, exps, normed, total, gn, nt, some = refs
     for i, w_ref in enumerate(w_refs):
         blocks, rows = w_ref.shape[0], w_ref.shape[1]
         for k in range(blocks):
@@ -106,7 +113,11 @@
     normed[...] = encoded * inv_rms
     low = normed[...].astype(BF16)
     q[...] = low
-    nt_ref[...] = low.T
+    nt[...] = low.T
+    features = grads_refs[0].shape[0]
+    for i in range(len(grads_refs)):
+        at = pl.ds(pl.multiple_of(blocks_ref[i] * features, features), features)
+        some[i * features : (i + 1) * features, :] = nt[at, :]
     total[...] = jnp.zeros_like(total)
     first = 0
     for tiles in g_refs:
@@ -129,7 +140,10 @@
             ids = tbase_ref[first + j] + lax.broadcasted_iota(I32, (1, width), 1)
             target = (pos_ref[...] == ids).astype(F32)
             gs = (wt_ref[...] * (exps[first + j] * scale - target)).astype(BF16)
-            gs_ref[first + j] = gs
+            grads = jnp.dot(some[...], gs, preferred_element_type=F32)
+            span = pl.ds(pl.multiple_of((first + j) * width, width), width)
+            for i, grads_ref in enumerate(grads_refs):
+                grads_ref[:, span] = grads[i * features : (i + 1) * features]
             gn[...] += lax.dot_general(gs, tiles[j], NT, preferred_element_type=F32)
             return 0
 
@@ -142,7 +156,7 @@
     other_ref[...] = jnp.dot(picked[half:], grad, preferred_element_type=F32)
 
 
-def main(woff, tbase, frow, pos, wt, q_pieces, w_pieces, groups):
+def main(woff, tbase, blocks, rows, frow, pos, wt, q_pieces, w_pieces, groups):
     n_q, n_w, n_g = len(q_pieces), len(w_pieces), len(groups)
     own, depth = q_pieces[0].shape
     queries = own * n_q
@@ -151,14 +165,10 @@
     half = frow.shape[0] // 2
     return pl.pallas_call(
         functools.partial(main_kernel, n_q, n_w, n_g),
-        out_shape=(
-            jax.ShapeDtypeStruct((n_t, queries, width), BF16),
-            jax.ShapeDtypeStruct((features, queries), BF16),
-            jax.ShapeDtypeStruct((half, features), F32),
-            jax.ShapeDtypeStruct((half, features), F32),
-        ),
-        in_specs=[SMEM, SMEM, VMEM, VMEM, VMEM] + [VMEM] * (n_q + n_w + n_g),
-        out_specs=(VMEM,) * 4,
+        out_shape=(jax.ShapeDtypeStruct((half, features), F32),) * 2
+        + (jax.ShapeDtypeStruct((rows, n_t * width), F32),) * blocks.shape[0],
+        in_specs=[SMEM, SMEM, SMEM, VMEM, VMEM, VMEM] + [VMEM] * (n_q + n_w + n_g),
+        out_specs=(VMEM,) * (2 + blocks.shape[0]),
         scratch_shapes=[
             pltpu.VMEM((depth, features), BF16),
             pltpu.VMEM((queries, depth), BF16),
@@ -166,45 +176,22 @@
             pltpu.VMEM((queries, features), F32),
             pltpu.VMEM((queries, 1), F32),
             pltpu.VMEM((queries, features), F32),
+            pltpu.VMEM((features, queries), BF16),
+            pltpu.VMEM((rows * blocks.shape[0], queries), BF16),
         ],
         compiler_params=pltpu.CompilerParams(vmem_limit_bytes=(28 if n_t * queries * width * 4 <= 8 * MIB else 60) * MIB),
         cost_estimate=cost(20 * 10**9, 20 * 10**6),
-    )(woff, tbase, frow, pos, wt, *q_pieces, *w_pieces, *groups)
-
-
-def dots_kernel(blocks_ref, nt_ref, gs_ref, *out_refs):
-    rows = out_refs[0].shape[0]
-    n_t, width = gs_ref.shape[0], gs_ref.shape[2]
-    picked = [nt_ref[pl.ds(pl.multiple_of(blocks_ref[i] * rows, rows), rows), :] for i in range(len(out_refs))]
-    picked = jnp.concatenate(picked, 0)
-    for j in range(n_t):
-        grads = jnp.dot(picked, gs_ref[j], preferred_element_type=F32)
-        for i, out_ref in enumerate(out_refs):
-            out_ref[:, j * width : (j + 1) * width] = grads[i * rows : (i + 1) * rows]
-
-
-def passage_grads(blocks, rows, nt, gs):
-    n_t, _, width = gs.shape
-    n = blocks.shape[0]
-    return pl.pallas_call(
-        dots_kernel,
-        out_shape=(jax.ShapeDtypeStruct((rows, n_t * width), F32),) * n,
-        in_specs=[SMEM, VMEM, VMEM],
-        out_specs=(VMEM,) * n,
-        compiler_params=pltpu.CompilerParams(vmem_limit_bytes=12 * MIB),
-        cost_estimate=cost(3 * 10**9, 8 * 10**6),
-    )(blocks, nt, gs)
-
-
-def words_kernel(words, block_ref, grads_ref, *refs):
+    )(woff, tbase, blocks, frow, pos, wt, *q_pieces, *w_pieces, *groups)
+
+
+def words_kernel(words, block, grads_ref, *refs):
     code_refs, (out_ref, codes) = refs[:-2], refs[-2:]
     held, sub = out_ref.shape[0], out_ref.shape[1]
     column = 0
     for code_ref in code_refs:
-        width = code_ref.shape[2]
+        width = code_ref.shape[3]
         for j in range(code_ref.shape[0]):
-            rows = pl.ds(pl.multiple_of(block_ref[0] * held, held), held)
-            codes[:, column : column + width] = code_ref[j, rows, :]
+            codes[:, column : column + width] = code_ref[j, block]
             column += width
     low = words // SPLIT
     shift = low.bit_length() - 1
@@ -244,20 +231,21 @@
     columns = grads.shape[1]
     sub = grads.shape[0] // held
     return pl.pallas_call(
-        functools.partial(words_kernel, words),
+        functools.partial(words_kernel, words, block),
         out_shape=jax.ShapeDtypeStruct((held, sub, words), F32),
-        in_specs=[SMEM, VMEM] + [VMEM] * len(codes),
+        in_specs=[VMEM] * (1 + len(codes)),
         out_specs=VMEM,
         scratch_shapes=[pltpu.VMEM((held, columns), I32)],
         compiler_params=pltpu.CompilerParams(vmem_limit_bytes=8 * MIB),
         cost_estimate=cost(3 * 10**9, 4 * 10**6),
-    )(block, grads, *codes)
+    )(grads, *codes)
 
 
 def compute(n_dom, n_sh, n_dp, queries_in, encoder_weight, codebook, codes, positive_ids, loss_weight):
     dom, z, x = (lax.axis_index(a) for a in ("dom", "shard", "dp"))
     n_dev = n_dom * n_sh * n_dp
-    n_zp = n_sh // 2
+    group = min(n_sh, 4)
+    n_zp, zp, zi = n_sh // group, z // group, lax.rem(z, group)
     evens = range(0, n_dom, 2)
     shards = [lax.rem(z - k + n_sh, n_sh) for k in range(n_sh)]
     lanes = [lax.rem(x - t + n_dp, n_dp) for t in range(n_dp)]
@@ -266,21 +254,17 @@
     w_rows, depth = encoder_weight.shape
     w_z = jnp.stack([encoder_weight] + [move(encoder_weight, "shard", ring(n_sh, k)) for k in range(1, n_sh)])
 
-    q = queries_in[0]
-    own = q.shape[0]
-    q_pieces, q_from = [], []
-    for t in range(n_dp):
-        for a in range(2):
-            pairs = []
-            for s in range(n_sh):
-                for d in range(n_dp):
-                    pairs.append((s * n_dp + d, (s ^ a) * n_dp + (d + t) % n_dp))
-            q_pieces.append(q if t == a == 0 else move(q, ("shard", "dp"), pairs))
-            q_from.append((z ^ a) * n_dp + lanes[t])
-
     book = codebook[0].astype(BF16)
     words = book.shape[2]
-    books = [book] + [move(book, "shard", ring(n_sh, k)) for k in range(1, n_sh)]
+    held_words = book.shape[0] // n_dp
+    book_share = [lax.dynamic_slice_in_dim(book, lanes[t] * held_words, held_words, 0) for t in range(n_dp)]
+    moved = [move(book_share[0], "shard", ring(n_sh, k)) for k in range(1, n_sh)]
+    books = [book_share[0]] + moved
+    moved = jnp.concatenate(moved)
+    for t in range(1, n_dp):
+        books += [book_share[t]] + jnp.split(move(moved, "dp", ring(n_dp, t)), n_sh - 1)
+    place = jnp.stack([shards[k] * n_dp + lanes[t] for t in range(n_dp) for k in range(n_sh)]).astype(I32)
+
     codes_t = codes[0].T.astype(BF16)
     subspaces, pass_rows = codes_t.shape
     width = pass_rows // n_dp
@@ -292,6 +276,11 @@
         tiles[t, 0] = share[t]
         for k in range(1, n_sh):
             tiles[t, k] = move(tiles[0, k], "dp", ring(n_dp, t))
+
+    q = queries_in[0]
+    own = q.shape[0]
+    q_pieces = [q] + [move(q, "shard", flip(n_sh, a)) for a in range(1, group)]
+    q_from = [(z ^ a) * n_dp + x for a in range(group)]
 
     w_x = [w_z] + [move(w_z, "dp", ring(n_dp, t)) for t in range(1, n_dp)]
     w_pieces, w_places = [], []
@@ -313,10 +302,18 @@
     else:
         w_offsets = w_places * w_rows
 
-    place = jnp.stack(shards).astype(I32)
+    held = subspaces // (n_sh * n_dp)
+    owners = []
+    for j in range(n_zp):
+        for t in range(n_dp):
+            owners.append((lax.rem(zp + j, n_zp) * group + zi) * n_dp + lax.rem(x + t, n_dp))
+    blocks = jnp.stack(owners).astype(I32)
+
     order = [[(t, 0) for t in range(n_dp)]] + [[(t, k) for k in range(1, n_sh)] for t in range(n_dp)]
-    bases = [shards[k] * pass_rows + lanes[t] * width for group in order for t, k in group]
-    built = [rebuild(place, [tiles[key] for key in group], books) for group in order]
+    bases = [shards[k] * pass_rows + lanes[t] * width for part in order for t, k in part]
+    built = []
+    for part in order:
+        built.append(rebuild(place, blocks, held, [tiles[key] for key in part], books))
     passages = [b[0] for b in built]
     tile_codes = [b[1] for b in built]
 
@@ -324,18 +321,18 @@
         return jnp.concatenate([lax.dynamic_slice_in_dim(array, f * own, own, 0) for f in q_from])[:, None]
 
     out_rows = depth // n_dev
-    zp, zi = z // 2, z % 2
-    blocks = []
+    firsts = []
     for core in range(2):
         for e in evens:
-            for j in range(n_zp):
-                to_z = lax.rem(zp + j, n_zp) * 2 + zi
-                blocks.append((((dom ^ (e | core)) * n_sh + to_z) * n_dp + x) * out_rows)
-    frow = (jnp.stack(blocks).astype(I32)[:, None] + jnp.arange(out_rows, dtype=I32)[None, :]).reshape(-1, 1)
-
-    gs, low_t, own_part, other_part = main(
+            for owner in owners:
+                firsts.append(((dom ^ (e | core)) * n_sh * n_dp + owner) * out_rows)
+    frow = (jnp.stack(firsts).astype(I32)[:, None] + jnp.arange(out_rows, dtype=I32)[None, :]).reshape(-1, 1)
+
+    own_part, other_part, *grads = main(
         w_offsets,
         jnp.stack(bases).astype(I32),
+        blocks,
+        held * (depth // subspaces),
         frow,
         rows_of(positive_ids[0]),
         rows_of(loss_weight[0].astype(F32)),
@@ -344,32 +341,33 @@
         passages,
     )
 
-    held = subspaces // (n_sh * n_dp)
-    owners = [lax.rem(zp + j, n_zp) * 2 + zi for j in range(n_zp)]
-    blocks = jnp.stack([o * n_dp + x for o in owners]).astype(I32)
-    grads = passage_grads(blocks, low_t.shape[0] // (n_sh * n_dp), low_t, gs)
-
     summed = own_part + move(other_part, "dom", flip(n_dom, 1))
-    summed, grads = lax.optimization_barrier((summed, grads))
-    summed = summed.reshape(len(evens), n_zp, out_rows, depth)
+    summed = summed.reshape(len(evens), len(owners), out_rows, depth)
     weight_grad = summed[0, 0]
+    book_grad = None
+    for o in reversed(range(len(owners))):
+        j, t = o // n_dp, o % n_dp
+        part = word_grads(o, held, words, grads[o], tile_codes)
+        if o:
+            pairs = []
+            for s in range(n_sh):
+                for d in range(n_dp):
+                    pairs.append((s * n_dp + d, (s + group * j) % n_sh * n_dp + (d + t) % n_dp))
+            part = move(part, ("shard", "dp"), pairs)
+        book_grad = part if book_grad is None else book_grad + part
     for i, e in enumerate(evens):
-        for j in range(n_zp):
-            if i == j == 0:
+        for o in range(len(owners)):
+            if i == o == 0:
                 continue
+            j, t = o // n_dp, o % n_dp
             pairs = []
             for d in range(n_dom):
                 for s in range(n_sh):
-                    pairs.append((d * n_sh + s, (d ^ e) * n_sh + (s + 2 * j) % n_sh))
-            moved = move(summed[i, j], ("dom", "shard"), pairs)
+                    for c in range(n_dp):
+                        to = ((d ^ e) * n_sh + (s + group * j) % n_sh) * n_dp + (c + t) % n_dp
+                        pairs.append(((d * n_sh + s) * n_dp + c, to))
+            moved = move(summed[i, o], ("dom", "shard", "dp"), pairs)
             weight_grad = weight_grad + moved
-
-    book_grad = None
-    for j in reversed(range(n_zp)):
-        part = word_grads(blocks[j : j + 1], held, words, grads[j], tile_codes)
-        if j:
-            part = move(part, "shard", ring(n_sh, 2 * j))
-        book_grad = part if book_grad is None else book_grad + part
     return (weight_grad, book_grad[None])
 
 

time: 118 us -> 102 us (0.86)
  waiting for transfers between devices: 26.3 us -> 16.2 us
  local copies, waits for them, and re-layouts: 8.99 us -> 1.83 us
  Pallas kernels: 40.2 us -> 42.4 us
    ppermute x10 -> x11, waiting for transfers between devices: 21.1 us -> 6.59 us  [the longest x3 5.62 us: compute(): moved = move(summed[i, o], ('dom', 'shard', 'dp'), pairs)]
    ppermute x3, waiting for transfers between devices: 0.01 us -> 9.62 us  [compute(): tiles[0, k] = move(share[0], 'shard', ring(n_sh, k))]
    unnamed x18 -> x4, local copies, waits for them, and re-layouts: 7.28 us -> 0.01 us
    ppermute x3, waiting for transfers between devices: 5.13 us -> 0.01 us  [compute(): tiles[t, k] = move(tiles[0, k], 'dp', ring(n_dp, t))]
    pallas_call x3, Pallas kernels: 16 us -> 18.3 us  [rebuild(): pl.pallas_call(functools.partial(rebuild_kernel, n_t, n_b), out_shape=(ja...]
    ppermute x10 -> x11, starting transfers between devices: 17.8 us -> 20 us  [the longest x3 10.1 us: compute(): q_pieces = [q] + [move(q, 'shard', flip(n_sh, a)) for a in range(1, group)]]
    pallas_call x1, Pallas kernels: 16.8 us -> 18.5 us  [main(): pl.pallas_call(functools.partial(main_kernel, n_q, n_w, n_g), out_shape=(...]
    pallas_call x3 -> x2, Pallas kernels: 7.36 us -> 5.58 us  [word_grads(): pl.pallas_call(functools.partial(words_kernel, words, block), out_shape=j...]
  transfers between devices with their start and end apart: 27 -> 28, of which waited for: 6 -> 6; matrix products, arithmetic and copies ran while one was open for 5% -> 5% of each run, Pallas kernels for 15% -> 23%
where the time goes in v1:
time: 102 us
  Pallas kernels  42.4 us (42%)
  starting transfers between devices  36.2 us (35%)
  waiting for transfers between devices  16.2 us (16%)
  other arithmetic  4.4 us (4%)
  local copies, waits for them, and re-layouts  1.83 us (2%)
    pallas_call x1, Pallas kernels, main(): pl.pallas_call(functools.partial(main_kernel, n_q, n_w, n_g), out_shape=(...  18.5 us
    pallas_call x3, Pallas kernels, rebuild(): pl.pallas_call(functools.partial(rebuild_kernel, n_t, n_b), out_shape=(ja...  18.3 us
    ppermute x3, starting transfers between devices, compute(): q_pieces = [q] + [move(q, 'shard', flip(n_sh, a)) for a in range(1, group)]  10.1 us
    ppermute x3, waiting for transfers between devices, compute(): tiles[0, k] = move(share[0], 'shard', ring(n_sh, k))  9.62 us
    ppermute x3, starting transfers between devices, compute(): move(encoder_weight, 'shard', ring(n_sh, k))  7.24 us
    ppermute x3, waiting for transfers between devices, compute(): moved = move(summed[i, o], ('dom', 'shard', 'dp'), pairs)  5.62 us
    pallas_call x2, Pallas kernels, word_grads(): pl.pallas_call(functools.partial(words_kernel, words, block), out_shape=j...  5.58 us
    ppermute x3, starting transfers between devices, compute(): moved = move(summed[i, o], ('dom', 'shard', 'dp'), pairs)  3.55 us
  transfers between devices with their start and end apart: 28, of which 6 were waited for; matrix products, arithmetic and copies ran while one was open for 5% of the time, Pallas kernels for 23%

profile of v1, /device:TPU:0, one launch (start us, length us, event | category | flops | bytes accessed | tf_op | source)
XLA Modules:
  0.0 102.1 jit_solution(16542717878679442138)
XLA Ops:
  0.6 3.1 %collective-permute-start.3 = (bf16[32,1024]{1,0:T(8,128)(2,1)}, bf16[32,1024]{1,0:T(8,128)(2,1)S(1)}, u32[]{:S(2)}, u32[]{:S(2)}) collective-permute-start(bf16[32,1024]{1,0:T(8,128)(2,1)} %param.7), channel_id=1, source_target_pairs={{0,2},{2,4},{4,6},{6,0},{1,3},{3,5},{5,7},{7,1},{8,10},{10,12},{12... | collective-permute-start | bytes 196616 | tf_op jit(solution)/shard_map/ppermute | solution.py:255
  3.7 2.1 %collective-permute-start.5 = (bf16[32,1024]{1,0:T(8,128)(2,1)}, bf16[32,1024]{1,0:T(8,128)(2,1)S(1)}, u32[]{:S(2)}, u32[]{:S(2)}) collective-permute-start(bf16[32,1024]{1,0:T(8,128)(2,1)} %param.7), channel_id=1, source_target_pairs={{0,6},{2,0},{4,2},{6,4},{1,7},{3,1},{5,3},{7,5},{8,14},{10,8},{12,... | collective-permute-start | bytes 196616 | tf_op jit(solution)/shard_map/ppermute | solution.py:255
  5.8 1.0 convert_element_type.15
  6.8 2.0 %collective-permute-start.15 = (bf16[16,8,256]{2,1,0:T(8,128)(2,1)S(1)}, bf16[16,8,256]{2,1,0:T(8,128)(2,1)S(1)}, u32[]{:S(2)}, u32[]{:S(2)}) collective-permute-start(bf16[16,8,256]{2,1,0:T(8,128)(2,1)S(1)} %get-tuple-element.31.refs_2_.refs_3_), channel_id=1, source_target_pairs={{0,6},{2,0},{4,2},{6,4},{1,7},{3,1},{5,3},{7,5},{8,14},{10,8},{12,... | collective-permute-start | bytes 196616 | tf_op jit(solution)/shard_map/ppermute | solution.py:261
  8.9 1.0 collective-permute-start.13
  9.9 0.1 stack.236
  10.2 0.7 convert_element_type.13
  10.9 0.7 fusion.3
  11.6 1.1 %convert_element_type.14 = bf16[1,1024,128]{2,1,0:T(8,128)(2,1)S(1)} convert(s32[1,1024,128]{2,1,0:T(8,128)} %param.9) | non-fusion elementwise | flops 131072 | bytes 786432 | tf_op jit(solution)/shard_map/convert_element_type | solution.py:268
  12.7 0.1 copy.10
  12.9 2.0 %collective-permute-start.4 = (bf16[32,1024]{1,0:T(8,128)(2,1)S(1)}, bf16[32,1024]{1,0:T(8,128)(2,1)S(1)}, u32[]{:S(2)}, u32[]{:S(2)}) collective-permute-start(bf16[32,1024]{1,0:T(8,128)(2,1)S(1)} %copy-done.1), channel_id=1, source_target_pairs={{0,4},{2,6},{4,0},{6,2},{1,5},{3,7},{5,1},{7,3},{8,12},{10,14},{12... | collective-permute-start | bytes 196616 | tf_op jit(solution)/shard_map/ppermute | solution.py:255
  14.9 1.0 collective-permute-done.14.refs_4_.refs_5_
  15.9 1.9 %collective-permute-start.19 = (bf16[128,512]{1,0:T(8,128)(2,1)S(1)}, bf16[128,512]{1,0:T(8,128)(2,1)S(1)}, u32[]{:S(2)}, u32[]{:S(2)}) collective-permute-start(bf16[128,512]{1,0:T(8,128)(2,1)S(1)} %bitcast.108), channel_id=1, source_target_pairs={{0,6},{2,0},{4,2},{6,4},{1,7},{3,1},{5,3},{7,5},{8,14},{10,8},{12,... | collective-permute-start | bytes 393224 | tf_op jit(solution)/shard_map/ppermute | solution.py:274
  17.8 0.7 collective-permute-start.17
  18.5 1.5 %collective-permute-start.16 = (bf16[48,8,256]{2,1,0:T(8,128)(2,1)S(1)}, bf16[48,8,256]{2,1,0:T(8,128)(2,1)S(1)}, u32[]{:S(2)}, u32[]{:S(2)}) collective-permute-start(bf16[48,8,256]{2,1,0:T(8,128)(2,1)S(1)} %pad_maximum_fusion.1), channel_id=1, source_target_pairs={{0,1},{1,0},{2,3},{3,2},{4,5},{5,4},{6,7},{7,6},{8,9},{9,8},{10,11... | collective-permute-start | bytes 589832 | tf_op jit(solution)/shard_map/ppermute | solution.py:265
  20.0 0.6 collective-permute-start.6
  20.7 0.1 add.451.frow_ref
  20.8 0.1 copy.14.wt_ref
  21.0 0.1 copy.13.pos_ref
  21.2 0.1 copy.11
  21.5 0.2 collective-permute-done.19.refs_2_
  21.7 8.0 %collective-permute-start.2 = (bf16[128,1024]{1,0:T(8,128)(2,1)S(1)}, bf16[128,1024]{1,0:T(8,128)(2,1)S(1)}, u32[]{:S(2)}, u32[]{:S(2)}) collective-permute-start(bf16[128,1024]{1,0:T(8,128)(2,1)S(1)} %bitcast.113), channel_id=1, source_target_pairs={{0,6},{2,4},{4,2},{6,0},{1,7},{3,5},{5,3},{7,1},{8,14},{10,12},{12... | collective-permute-start | bytes 786440 | tf_op jit(solution)/shard_map/ppermute | solution.py:282
  29.7 0.5 collective-permute-start.22
  30.2 9.4 %collective-permute-done.18.refs_1_ = bf16[128,512]{1,0:T(8,128)(2,1)S(1)} collective-permute-done((bf16[128,512]{1,0:T(8,128)(2,1)S(1)}, bf16[128,512]{1,0:T(8,128)(2,1)S(1)}, u32[]{:S(2)}, u32[]{:S(2)}) %collective-permute-start.18) | collective-permute-done | bytes 131104 | tf_op jit(solution)/shard_map/ppermute | solution.py:274
  39.7 0.8 collective-permute-start.1
  40.5 1.5 %collective-permute-start.7 = (bf16[4,32,1024]{2,1,0:T(8,128)(2,1)S(1)}, bf16[4,32,1024]{2,1,0:T(8,128)(2,1)S(1)}, u32[]{:S(2)}, u32[]{:S(2)}) collective-permute-start(bf16[4,32,1024]{2,1,0:T(8,128)(2,1)S(1)} %pad_maximum_fusion.refs_4_), channel_id=1, source_target_pairs={{0,16},{8,24},{16,0},{24,8},{1,17},{9,25},{17,1},{25,9},{2,18},{10... | collective-permute-start | bytes 786440 | tf_op jit(solution)/shard_map/ppermute | solution.py:289
  42.0 0.7 collective-permute-start.21
  42.7 0.5 collective-permute-start.8
  43.2 6.9 %shard_map.78 = (bf16[3,1024,512]{2,1,0:T(8,128)(2,1)S(1)}, s32[3,2,16,512]{3,2,1,0:T(8,128)S(1)}) custom-call(s32[8]{0:T(128)S(1)} %stack.271.place_ref, s32[2]{0:T(128)S(1)} %pad_add_fusion.1.blocks_ref, bf16[128,512]{1,0:T(8,128)(2,1)S(1)} %collective-permute-done.17.refs_0_, bf16[128,512]{1,0:T(8,128)(2,1)S(1)} %collective-permute-done.18.refs_1_, ...), custom_call_target="tpu_custom_call" | custom-call | flops 3000000000 | bytes 6000000 | tf_op jit(solution)/shard_map/pallas_call | solution.py:77
  50.1 1.4 %collective-permute-start.20 = (bf16[128,512]{1,0:T(8,128)(2,1)S(1)}, bf16[128,512]{1,0:T(8,128)(2,1)S(1)}, u32[]{:S(2)}, u32[]{:S(2)}) collective-permute-start(bf16[128,512]{1,0:T(8,128)(2,1)S(1)} %collective-permute-done.17.refs_0_), channel_id=1, source_target_pairs={{0,1},{1,0},{2,3},{3,2},{4,5},{5,4},{6,7},{7,6},{8,9},{9,8},{10,11... | collective-permute-start | bytes 393224 | tf_op jit(solution)/shard_map/ppermute | solution.py:278
  51.5 4.7 %shard_map.77 = (bf16[2,1024,512]{2,1,0:T(8,128)(2,1)S(1)}, s32[2,2,16,512]{3,2,1,0:T(8,128)S(1)}) custom-call(s32[8]{0:T(128)S(1)} %stack.271.place_ref, s32[2]{0:T(128)S(1)} %pad_add_fusion.1.blocks_ref, bf16[128,512]{1,0:T(8,128)(2,1)S(1)} %bitcast.111, bf16[128,512]{1,0:T(8,128)(2,1)S(1)} %bitcast.112, ...), custom_call_target="tpu_custom_call" | custom-call | flops 2000000000 | bytes 4000000 | tf_op jit(solution)/shard_map/pallas_call | solution.py:77
  56.2 1.2 %collective-permute-start = (bf16[128,1024]{1,0:T(8,128)(2,1)S(1)}, bf16[128,1024]{1,0:T(8,128)(2,1)S(1)}, u32[]{:S(2)}, u32[]{:S(2)}) collective-permute-start(bf16[128,1024]{1,0:T(8,128)(2,1)S(1)} %bitcast.115), channel_id=1, source_target_pairs={{0,2},{2,0},{4,6},{6,4},{1,3},{3,1},{5,7},{7,5},{8,10},{10,8},{12,... | collective-permute-start | bytes 786440 | tf_op jit(solution)/shard_map/ppermute | solution.py:282
  57.4 0.5 collective-permute-start.10
  58.0 0.4 collective-permute-start.12
  58.5 6.7 %shard_map.79 = (bf16[3,1024,512]{2,1,0:T(8,128)(2,1)S(1)}, s32[3,2,16,512]{3,2,1,0:T(8,128)S(1)}) custom-call(s32[8]{0:T(128)S(1)} %stack.271.place_ref, s32[2]{0:T(128)S(1)} %pad_add_fusion.1.blocks_ref, bf16[128,512]{1,0:T(8,128)(2,1)S(1)} %collective-permute-done.20.refs_0_, bf16[128,512]{1,0:T(8,128)(2,1)S(1)} %collective-permute-done.21.refs_1_, ...), custom_call_target="tpu_custom_call" | custom-call | flops 3000000000 | bytes 6000000 | tf_op jit(solution)/shard_map/pallas_call | solution.py:77
  65.2 18.5 %shard_map.80 = (f32[128,1024]{1,0:T(8,128)S(1)}, f32[128,1024]{1,0:T(8,128)S(1)}, f32[128,4096]{1,0:T(8,128)S(1)}, f32[128,4096]{1,0:T(8,128)S(1)}) custom-call(s32[32]{0:T(128)S(1)} %broadcast_multiply_fusion.woff_ref, s32[8]{0:T(128)S(1)} %stack.245.tbase_ref, s32[2]{0:T(128)S(1)} %pad_add_fusion.1.blocks_ref, s32[256,1]{1,0:T(8,128)S(1)} %add.451.frow_ref, ...), custom_call_target="tpu_custom_call" | custom-call | flops 20000000000 | bytes 20000000 | tf_op jit(solution)/shard_map/pallas_call | solution.py:166
  83.8 0.1 collective-permute-start.23
  83.9 2.8 %shard_map.81 = f32[16,8,256]{2,1,0:T(8,128)S(1)} custom-call(f32[128,4096]{1,0:T(8,128)S(1)} %get-tuple-element.17.grads_ref, s32[2,2,16,512]{3,2,1,0:T(8,128)S(1)} %get-tuple-element.18.refs_0_, s32[3,2,16,512]{3,2,1,0:T(8,128)S(1)} %get-tuple-element.19.refs_1_, s32[3,2,16,512]{3,2,1,0:T(8,128)S(1)} %get-tuple-element.20.refs_2_), custom_call_target="tpu_custom_call" | custom-call | flops 3000000000 | bytes 4000000 | tf_op jit(solution)/shard_map/pallas_call | solution.py:233
  86.7 1.9 %collective-permute-start.27 = (f32[16,8,256]{2,1,0:T(8,128)S(1)}, f32[16,8,256]{2,1,0:T(8,128)S(1)}, u32[]{:S(2)}, u32[]{:S(2)}) collective-permute-start(f32[16,8,256]{2,1,0:T(8,128)S(1)} %shard_map.81), channel_id=1, source_target_pairs={{0,1},{1,0},{2,3},{3,2},{4,5},{5,4},{6,7},{7,6},{8,9},{9,8},{10,11... | collective-permute-start | bytes 393224 | tf_op jit(solution)/shard_map/ppermute | solution.py:356
  88.6 2.8 %shard_map.82 = f32[16,8,256]{2,1,0:T(8,128)S(1)} custom-call(f32[128,4096]{1,0:T(8,128)S(1)} %get-tuple-element.21.grads_ref, s32[2,2,16,512]{3,2,1,0:T(8,128)S(1)} %get-tuple-element.18.refs_0_, s32[3,2,16,512]{3,2,1,0:T(8,128)S(1)} %get-tuple-element.19.refs_1_, s32[3,2,16,512]{3,2,1,0:T(8,128)S(1)} %get-tuple-element.20.refs_2_), custom_call_target="tpu_custom_call" | custom-call | flops 3000000000 | bytes 4000000 | tf_op jit(solution)/shard_map/pallas_call | solution.py:233
  91.5 0.3 collective-permute-start.24
  91.8 1.8 %collective-permute-start.26 = (f32[32,1024]{1,0:T(8,128)S(1)}, f32[32,1024]{1,0:T(8,128)S(1)}, u32[]{:S(2)}, u32[]{:S(2)}) collective-permute-start(f32[32,1024]{1,0:T(8,128)S(1)} %get-tuple-element.23), channel_id=1, source_target_pairs={{0,17},{1,16},{2,19},{3,18},{4,21},{5,20},{6,23},{7,22},{8,25},{9,... | collective-permute-start | bytes 393224 | tf_op jit(solution)/shard_map/ppermute | solution.py:369
  93.5 1.5 %collective-permute-start.25 = (f32[32,1024]{1,0:T(8,128)S(1)}, f32[32,1024]{1,0:T(8,128)S(1)}, u32[]{:S(2)}, u32[]{:S(2)}) collective-permute-start(f32[32,1024]{1,0:T(8,128)S(1)} %get-tuple-element.24), channel_id=1, source_target_pairs={{0,16},{1,17},{2,18},{3,19},{4,20},{5,21},{6,22},{7,23},{8,24},{9,... | collective-permute-start | bytes 393224 | tf_op jit(solution)/shard_map/ppermute | solution.py:369
  95.1 0.7 add_bitcast_fusion
  95.7 2.2 %collective-permute-done.24 = f32[32,1024]{1,0:T(8,128)S(1)} collective-permute-done((f32[32,1024]{1,0:T(8,128)S(1)}, f32[32,1024]{1,0:T(8,128)S(1)}, u32[]{:S(2)}, u32[]{:S(2)}) %collective-permute-start.24) | collective-permute-done | bytes 131104 | tf_op jit(solution)/shard_map/ppermute | solution.py:369
  97.9 2.1 %collective-permute-done.26 = f32[32,1024]{1,0:T(8,128)S(1)} collective-permute-done((f32[32,1024]{1,0:T(8,128)S(1)}, f32[32,1024]{1,0:T(8,128)S(1)}, u32[]{:S(2)}, u32[]{:S(2)}) %collective-permute-start.26) | collective-permute-done | bytes 131104 | tf_op jit(solution)/shard_map/ppermute | solution.py:369
  100.0 1.4 %collective-permute-done.25 = f32[32,1024]{1,0:T(8,128)S(1)} collective-permute-done((f32[32,1024]{1,0:T(8,128)S(1)}, f32[32,1024]{1,0:T(8,128)S(1)}, u32[]{:S(2)}, u32[]{:S(2)}) %collective-permute-start.25) | collective-permute-done | bytes 131104 | tf_op jit(solution)/shard_map/ppermute | solution.py:369
  101.4 0.7 fusion.2
  (46 shorter events, 0.8 us)
Async XLA Ops:
  0.6 12.2 %copy-start.1 = (bf16[32,1024]{1,0:T(8,128)(2,1)S(1)}, bf16[32,1024]{1,0:T(8,128)(2,1)}, u32[]{:S(2)}) copy-start(bf16[32,1024]{1,0:T(8,128)(2,1)} %param.7) | copy-start | bytes 196612
  0.6 17.2 %collective-permute-start.3 = (bf16[32,1024]{1,0:T(8,128)(2,1)}, bf16[32,1024]{1,0:T(8,128)(2,1)S(1)}, u32[]{:S(2)}, u32[]{:S(2)}) collective-permute-start(bf16[32,1024]{1,0:T(8,128)(2,1)} %param.7), channel_id=1, source_target_pairs={{0,2},{2,4},{4,6},{6,0},{1,3},{3,5},{5,7},{7,1},{8,10},{10,12},{12... | collective-permute-start | bytes 196616 | tf_op jit(solution)/shard_map/ppermute | solution.py:255
  3.7 14.8 %collective-permute-start.5 = (bf16[32,1024]{1,0:T(8,128)(2,1)}, bf16[32,1024]{1,0:T(8,128)(2,1)S(1)}, u32[]{:S(2)}, u32[]{:S(2)}) collective-permute-start(bf16[32,1024]{1,0:T(8,128)(2,1)} %param.7), channel_id=1, source_target_pairs={{0,6},{2,0},{4,2},{6,4},{1,7},{3,1},{5,3},{7,5},{8,14},{10,8},{12,... | collective-permute-start | bytes 196616 | tf_op jit(solution)/shard_map/ppermute | solution.py:255
  6.8 14.8 %copy-start = (bf16[1,128,1024]{2,1,0:T(8,128)(2,1)S(1)}, bf16[1,128,1024]{2,1,0:T(8,128)(2,1)}, u32[]{:S(2)}) copy-start(bf16[1,128,1024]{2,1,0:T(8,128)(2,1)} %param.6) | copy-start | bytes 786436
  6.8 6.0 %collective-permute-start.15 = (bf16[16,8,256]{2,1,0:T(8,128)(2,1)S(1)}, bf16[16,8,256]{2,1,0:T(8,128)(2,1)S(1)}, u32[]{:S(2)}, u32[]{:S(2)}) collective-permute-start(bf16[16,8,256]{2,1,0:T(8,128)(2,1)S(1)} %get-tuple-element.31.refs_2_.refs_3_), channel_id=1, source_target_pairs={{0,6},{2,0},{4,2},{6,4},{1,7},{3,1},{5,3},{7,5},{8,14},{10,8},{12,... | collective-permute-start | bytes 196616 | tf_op jit(solution)/shard_map/ppermute | solution.py:261
  8.9 7.0 %collective-permute-start.14 = (bf16[16,8,256]{2,1,0:T(8,128)(2,1)S(1)}, bf16[16,8,256]{2,1,0:T(8,128)(2,1)S(1)}, u32[]{:S(2)}, u32[]{:S(2)}) collective-permute-start(bf16[16,8,256]{2,1,0:T(8,128)(2,1)S(1)} %get-tuple-element.31.refs_2_.refs_3_), channel_id=1, source_target_pairs={{0,4},{2,6},{4,0},{6,2},{1,5},{3,7},{5,1},{7,3},{8,12},{10,14},{12... | collective-permute-start | bytes 196616 | tf_op jit(solution)/shard_map/ppermute | solution.py:261
  8.9 8.9 %collective-permute-start.13 = (bf16[16,8,256]{2,1,0:T(8,128)(2,1)S(1)}, bf16[16,8,256]{2,1,0:T(8,128)(2,1)S(1)}, u32[]{:S(2)}, u32[]{:S(2)}) collective-permute-start(bf16[16,8,256]{2,1,0:T(8,128)(2,1)S(1)} %get-tuple-element.31.refs_2_.refs_3_), channel_id=1, source_target_pairs={{0,2},{2,4},{4,6},{6,0},{1,3},{3,5},{5,7},{7,1},{8,10},{10,12},{12... | collective-permute-start | bytes 196616 | tf_op jit(solution)/shard_map/ppermute | solution.py:261
  12.9 7.1 %collective-permute-start.4 = (bf16[32,1024]{1,0:T(8,128)(2,1)S(1)}, bf16[32,1024]{1,0:T(8,128)(2,1)S(1)}, u32[]{:S(2)}, u32[]{:S(2)}) collective-permute-start(bf16[32,1024]{1,0:T(8,128)(2,1)S(1)} %copy-done.1), channel_id=1, source_target_pairs={{0,4},{2,6},{4,0},{6,2},{1,5},{3,7},{5,1},{7,3},{8,12},{10,14},{12... | collective-permute-start | bytes 196616 | tf_op jit(solution)/shard_map/ppermute | solution.py:255
  15.9 5.8 %collective-permute-start.19 = (bf16[128,512]{1,0:T(8,128)(2,1)S(1)}, bf16[128,512]{1,0:T(8,128)(2,1)S(1)}, u32[]{:S(2)}, u32[]{:S(2)}) collective-permute-start(bf16[128,512]{1,0:T(8,128)(2,1)S(1)} %bitcast.108), channel_id=1, source_target_pairs={{0,6},{2,0},{4,2},{6,4},{1,7},{3,1},{5,3},{7,5},{8,14},{10,8},{12,... | collective-permute-start | bytes 393224 | tf_op jit(solution)/shard_map/ppermute | solution.py:274
  17.8 21.9 %collective-permute-start.18 = (bf16[128,512]{1,0:T(8,128)(2,1)S(1)}, bf16[128,512]{1,0:T(8,128)(2,1)S(1)}, u32[]{:S(2)}, u32[]{:S(2)}) collective-permute-start(bf16[128,512]{1,0:T(8,128)(2,1)S(1)} %bitcast.109), channel_id=1, source_target_pairs={{0,4},{2,6},{4,0},{6,2},{1,5},{3,7},{5,1},{7,3},{8,12},{10,14},{12... | collective-permute-start | bytes 393224 | tf_op jit(solution)/shard_map/ppermute | solution.py:274
  17.8 22.7 %collective-permute-start.17 = (bf16[128,512]{1,0:T(8,128)(2,1)S(1)}, bf16[128,512]{1,0:T(8,128)(2,1)S(1)}, u32[]{:S(2)}, u32[]{:S(2)}) collective-permute-start(bf16[128,512]{1,0:T(8,128)(2,1)S(1)} %bitcast.110), channel_id=1, source_target_pairs={{0,2},{2,4},{4,6},{6,0},{1,3},{3,5},{5,7},{7,1},{8,10},{10,12},{12... | collective-permute-start | bytes 393224 | tf_op jit(solution)/shard_map/ppermute | solution.py:274
  18.5 11.2 %collective-permute-start.16 = (bf16[48,8,256]{2,1,0:T(8,128)(2,1)S(1)}, bf16[48,8,256]{2,1,0:T(8,128)(2,1)S(1)}, u32[]{:S(2)}, u32[]{:S(2)}) collective-permute-start(bf16[48,8,256]{2,1,0:T(8,128)(2,1)S(1)} %pad_maximum_fusion.1), channel_id=1, source_target_pairs={{0,1},{1,0},{2,3},{3,2},{4,5},{5,4},{6,7},{7,6},{8,9},{9,8},{10,11... | collective-permute-start | bytes 589832 | tf_op jit(solution)/shard_map/ppermute | solution.py:265
  20.0 22.7 %collective-permute-start.6 = (bf16[4,32,1024]{2,1,0:T(8,128)(2,1)S(1)}, bf16[4,32,1024]{2,1,0:T(8,128)(2,1)S(1)}, u32[]{:S(2)}, u32[]{:S(2)}) collective-permute-start(bf16[4,32,1024]{2,1,0:T(8,128)(2,1)S(1)} %pad_maximum_fusion.refs_4_), channel_id=1, source_target_pairs={{0,1},{1,0},{2,3},{3,2},{4,5},{5,4},{6,7},{7,6},{8,9},{9,8},{10,11... | collective-permute-start | bytes 786440 | tf_op jit(solution)/shard_map/ppermute | solution.py:285
  21.7 35.8 %collective-permute-start.2 = (bf16[128,1024]{1,0:T(8,128)(2,1)S(1)}, bf16[128,1024]{1,0:T(8,128)(2,1)S(1)}, u32[]{:S(2)}, u32[]{:S(2)}) collective-permute-start(bf16[128,1024]{1,0:T(8,128)(2,1)S(1)} %bitcast.113), channel_id=1, source_target_pairs={{0,6},{2,4},{4,2},{6,0},{1,7},{3,5},{5,3},{7,1},{8,14},{10,12},{12... | collective-permute-start | bytes 786440 | tf_op jit(solution)/shard_map/ppermute | solution.py:282
  29.7 12.3 %collective-permute-start.22 = (bf16[128,512]{1,0:T(8,128)(2,1)S(1)}, bf16[128,512]{1,0:T(8,128)(2,1)S(1)}, u32[]{:S(2)}, u32[]{:S(2)}) collective-permute-start(bf16[128,512]{1,0:T(8,128)(2,1)S(1)} %collective-permute-done.19.refs_2_), channel_id=1, source_target_pairs={{0,1},{1,0},{2,3},{3,2},{4,5},{5,4},{6,7},{7,6},{8,9},{9,8},{10,11... | collective-permute-start | bytes 393224 | tf_op jit(solution)/shard_map/ppermute | solution.py:278
  39.7 17.8 %collective-permute-start.1 = (bf16[128,1024]{1,0:T(8,128)(2,1)S(1)}, bf16[128,1024]{1,0:T(8,128)(2,1)S(1)}, u32[]{:S(2)}, u32[]{:S(2)}) collective-permute-start(bf16[128,1024]{1,0:T(8,128)(2,1)S(1)} %bitcast.114), channel_id=1, source_target_pairs={{0,4},{2,6},{4,0},{6,2},{1,5},{3,7},{5,1},{7,3},{8,12},{10,14},{12... | collective-permute-start | bytes 786440 | tf_op jit(solution)/shard_map/ppermute | solution.py:282
  40.5 17.5 %collective-permute-start.7 = (bf16[4,32,1024]{2,1,0:T(8,128)(2,1)S(1)}, bf16[4,32,1024]{2,1,0:T(8,128)(2,1)S(1)}, u32[]{:S(2)}, u32[]{:S(2)}) collective-permute-start(bf16[4,32,1024]{2,1,0:T(8,128)(2,1)S(1)} %pad_maximum_fusion.refs_4_), channel_id=1, source_target_pairs={{0,16},{8,24},{16,0},{24,8},{1,17},{9,25},{17,1},{25,9},{2,18},{10... | collective-permute-start | bytes 786440 | tf_op jit(solution)/shard_map/ppermute | solution.py:289
  42.0 8.1 %collective-permute-start.21 = (bf16[128,512]{1,0:T(8,128)(2,1)S(1)}, bf16[128,512]{1,0:T(8,128)(2,1)S(1)}, u32[]{:S(2)}, u32[]{:S(2)}) collective-permute-start(bf16[128,512]{1,0:T(8,128)(2,1)S(1)} %collective-permute-done.18.refs_1_), channel_id=1, source_target_pairs={{0,1},{1,0},{2,3},{3,2},{4,5},{5,4},{6,7},{7,6},{8,9},{9,8},{10,11... | collective-permute-start | bytes 393224 | tf_op jit(solution)/shard_map/ppermute | solution.py:278
  42.7 15.3 %collective-permute-start.8 = (bf16[4,32,1024]{2,1,0:T(8,128)(2,1)S(1)}, bf16[4,32,1024]{2,1,0:T(8,128)(2,1)S(1)}, u32[]{:S(2)}, u32[]{:S(2)}) collective-permute-start(bf16[4,32,1024]{2,1,0:T(8,128)(2,1)S(1)} %collective-permute-done.6.refs_5_), channel_id=1, source_target_pairs={{0,16},{8,24},{16,0},{24,8},{1,17},{9,25},{17,1},{25,9},{2,18},{10... | collective-permute-start | bytes 786440 | tf_op jit(solution)/shard_map/ppermute | solution.py:289
  50.1 6.1 %collective-permute-start.20 = (bf16[128,512]{1,0:T(8,128)(2,1)S(1)}, bf16[128,512]{1,0:T(8,128)(2,1)S(1)}, u32[]{:S(2)}, u32[]{:S(2)}) collective-permute-start(bf16[128,512]{1,0:T(8,128)(2,1)S(1)} %collective-permute-done.17.refs_0_), channel_id=1, source_target_pairs={{0,1},{1,0},{2,3},{3,2},{4,5},{5,4},{6,7},{7,6},{8,9},{9,8},{10,11... | collective-permute-start | bytes 393224 | tf_op jit(solution)/shard_map/ppermute | solution.py:278
  56.2 9.0 %collective-permute-start = (bf16[128,1024]{1,0:T(8,128)(2,1)S(1)}, bf16[128,1024]{1,0:T(8,128)(2,1)S(1)}, u32[]{:S(2)}, u32[]{:S(2)}) collective-permute-start(bf16[128,1024]{1,0:T(8,128)(2,1)S(1)} %bitcast.115), channel_id=1, source_target_pairs={{0,2},{2,0},{4,6},{6,4},{1,3},{3,1},{5,7},{7,5},{8,10},{10,8},{12,... | collective-permute-start | bytes 786440 | tf_op jit(solution)/shard_map/ppermute | solution.py:282
  57.4 7.8 %collective-permute-start.9 = (bf16[4,32,1024]{2,1,0:T(8,128)(2,1)S(1)}, bf16[4,32,1024]{2,1,0:T(8,128)(2,1)S(1)}, u32[]{:S(2)}, u32[]{:S(2)}) collective-permute-start(bf16[4,32,1024]{2,1,0:T(8,128)(2,1)S(1)} %pad_maximum_fusion.refs_4_), channel_id=1, source_target_pairs={{0,8},{8,0},{16,24},{24,16},{1,9},{9,1},{17,25},{25,17},{2,10},{10... | collective-permute-start | bytes 786440 | tf_op jit(solution)/shard_map/ppermute | solution.py:290
  57.4 7.8 %collective-permute-start.10 = (bf16[4,32,1024]{2,1,0:T(8,128)(2,1)S(1)}, bf16[4,32,1024]{2,1,0:T(8,128)(2,1)S(1)}, u32[]{:S(2)}, u32[]{:S(2)}) collective-permute-start(bf16[4,32,1024]{2,1,0:T(8,128)(2,1)S(1)} %collective-permute-done.6.refs_5_), channel_id=1, source_target_pairs={{0,8},{8,0},{16,24},{24,16},{1,9},{9,1},{17,25},{25,17},{2,10},{10... | collective-permute-start | bytes 786440 | tf_op jit(solution)/shard_map/ppermute | solution.py:290
  58.0 7.3 %collective-permute-start.11 = (bf16[4,32,1024]{2,1,0:T(8,128)(2,1)S(1)}, bf16[4,32,1024]{2,1,0:T(8,128)(2,1)S(1)}, u32[]{:S(2)}, u32[]{:S(2)}) collective-permute-start(bf16[4,32,1024]{2,1,0:T(8,128)(2,1)S(1)} %collective-permute-done.7.refs_6_), channel_id=1, source_target_pairs={{0,8},{8,0},{16,24},{24,16},{1,9},{9,1},{17,25},{25,17},{2,10},{10... | collective-permute-start | bytes 786440 | tf_op jit(solution)/shard_map/ppermute | solution.py:290
  58.0 7.2 %collective-permute-start.12 = (bf16[4,32,1024]{2,1,0:T(8,128)(2,1)S(1)}, bf16[4,32,1024]{2,1,0:T(8,128)(2,1)S(1)}, u32[]{:S(2)}, u32[]{:S(2)}) collective-permute-start(bf16[4,32,1024]{2,1,0:T(8,128)(2,1)S(1)} %collective-permute-done.8.refs_7_), channel_id=1, source_target_pairs={{0,8},{8,0},{16,24},{24,16},{1,9},{9,1},{17,25},{25,17},{2,10},{10... | collective-permute-start | bytes 786440 | tf_op jit(solution)/shard_map/ppermute | solution.py:290
  83.8 7.6 %collective-permute-start.23 = (f32[128,1024]{1,0:T(8,128)S(1)}, f32[128,1024]{1,0:T(8,128)S(1)}, u32[]{:S(2)}, u32[]{:S(2)}) collective-permute-start(f32[128,1024]{1,0:T(8,128)S(1)} %get-tuple-element.16), channel_id=1, source_target_pairs={{0,8},{8,0},{16,24},{24,16},{1,9},{9,1},{17,25},{25,17},{2,10},{10... | collective-permute-start | bytes 1572872 | tf_op jit(solution)/shard_map/ppermute | solution.py:344
  86.7 8.3 %collective-permute-start.27 = (f32[16,8,256]{2,1,0:T(8,128)S(1)}, f32[16,8,256]{2,1,0:T(8,128)S(1)}, u32[]{:S(2)}, u32[]{:S(2)}) collective-permute-start(f32[16,8,256]{2,1,0:T(8,128)S(1)} %shard_map.81), channel_id=1, source_target_pairs={{0,1},{1,0},{2,3},{3,2},{4,5},{5,4},{6,7},{7,6},{8,9},{9,8},{10,11... | collective-permute-start | bytes 393224 | tf_op jit(solution)/shard_map/ppermute | solution.py:356
  91.5 6.4 %collective-permute-start.24 = (f32[32,1024]{1,0:T(8,128)S(1)}, f32[32,1024]{1,0:T(8,128)S(1)}, u32[]{:S(2)}, u32[]{:S(2)}) collective-permute-start(f32[32,1024]{1,0:T(8,128)S(1)} %get-tuple-element.22), channel_id=1, source_target_pairs={{0,1},{1,0},{2,3},{3,2},{4,5},{5,4},{6,7},{7,6},{8,9},{9,8},{10,11... | collective-permute-start | bytes 393224 | tf_op jit(solution)/shard_map/ppermute | solution.py:369
  91.8 8.2 %collective-permute-start.26 = (f32[32,1024]{1,0:T(8,128)S(1)}, f32[32,1024]{1,0:T(8,128)S(1)}, u32[]{:S(2)}, u32[]{:S(2)}) collective-permute-start(f32[32,1024]{1,0:T(8,128)S(1)} %get-tuple-element.23), channel_id=1, source_target_pairs={{0,17},{1,16},{2,19},{3,18},{4,21},{5,20},{6,23},{7,22},{8,25},{9,... | collective-permute-start | bytes 393224 | tf_op jit(solution)/shard_map/ppermute | solution.py:369
  93.5 7.8 %collective-permute-start.25 = (f32[32,1024]{1,0:T(8,128)S(1)}, f32[32,1024]{1,0:T(8,128)S(1)}, u32[]{:S(2)}, u32[]{:S(2)}) collective-permute-start(f32[32,1024]{1,0:T(8,128)S(1)} %get-tuple-element.24), channel_id=1, source_target_pairs={{0,16},{1,17},{2,18},{3,19},{4,20},{5,21},{6,22},{7,23},{8,24},{9,... | collective-permute-start | bytes 393224 | tf_op jit(solution)/shard_map/ppermute | solution.py:369

commit v2 on v1

--- a/solution.py
+++ b/solution.py
@@ -14,6 +14,7 @@
 ANY = pl.BlockSpec(memory_space=pl.ANY)
 VMEM = pl.BlockSpec(memory_space=pltpu.VMEM)
 SMEM = pl.BlockSpec(memory_space=pltpu.SMEM)
+SPAN = 32
 MIB = 2**20
 
 
@@ -42,9 +43,13 @@
     for piece, book_ref in enumerate(books):
         table[pl.ds(place_ref[piece] * held, held)] = book_ref[...].astype(F32)
 
+    subspaces = code_refs[0].shape[0]
+    span = min(subspaces, SPAN)
+    steps = subspaces // span
+
     def body(i, _):
-        tile, first = i // n_b, lax.rem(i, n_b) * held
-        for j in range(held // 8):
+        tile, first = i // steps, lax.rem(i, steps) * span
+        for j in range(span // 8):
             rows = pl.multiple_of(first + 8 * j, 8)
             codes = codes_ref[tile, pl.ds(rows, 8), :]
             for pair in range(4):
@@ -67,7 +72,7 @@
                     out_ref[tile, out_rows, t : t + LANES] = jnp.concatenate(parts, 0).astype(BF16)
         return 0
 
-    lax.fori_loop(0, n_t * n_b, body, 0)
+    lax.fori_loop(0, n_t * steps, body, 0)
 
 
 def rebuild(place, blocks, kept, codes, books):
@@ -125,13 +130,16 @@
         def score(j, _, tiles=tiles, first=first):
             e = jnp.exp(jnp.dot(q[...], tiles[j], preferred_element_type=F32))
             exps[first + j] = e
-            total[...] += jnp.sum(e, axis=1, keepdims=True)
+            part = total[...]
+            for c in range(0, e.shape[1], LANES):
+                part = part + e[:, c : c + LANES]
+            total[...] = part
             return 0
 
         lax.fori_loop(0, tiles.shape[0], score, 0)
         first += tiles.shape[0]
     gn[...] = jnp.zeros_like(gn)
-    scale = 1.0 / total[...]
+    scale = 1.0 / jnp.sum(total[...], axis=1, keepdims=True)
     first = 0
     for tiles in g_refs:
         width = tiles.shape[2]
@@ -174,7 +182,7 @@
             pltpu.VMEM((queries, depth), BF16),
             pltpu.VMEM((n_t, queries, width), F32),
             pltpu.VMEM((queries, features), F32),
-            pltpu.VMEM((queries, 1), F32),
+            pltpu.VMEM((queries, LANES), F32),
             pltpu.VMEM((queries, features), F32),
             pltpu.VMEM((features, queries), BF16),
             pltpu.VMEM((rows * blocks.shape[0], queries), BF16),
@@ -262,7 +270,8 @@
     books = [book_share[0]] + moved
     moved = jnp.concatenate(moved)
     for t in range(1, n_dp):
-        books += [book_share[t]] + jnp.split(move(moved, "dp", ring(n_dp, t)), n_sh - 1)
+        across = move(moved, "dp", ring(n_dp, t))
+        books += [book_share[t]] + jnp.split(across, n_sh - 1)
     place = jnp.stack([shards[k] * n_dp + lanes[t] for t in range(n_dp) for k in range(n_sh)]).astype(I32)
 
     codes_t = codes[0].T.astype(BF16)
@@ -282,11 +291,14 @@
     q_pieces = [q] + [move(q, "shard", flip(n_sh, a)) for a in range(1, group)]
     q_from = [(z ^ a) * n_dp + x for a in range(group)]
 
-    w_x = [w_z] + [move(w_z, "dp", ring(n_dp, t)) for t in range(1, n_dp)]
     w_pieces, w_places = [], []
     for e in evens:
         for t in range(n_dp):
-            w_pieces.append(w_x[t] if e == 0 else move(w_x[t], "dom", flip(n_dom, e)))
+            pairs = []
+            for d in range(n_dom):
+                for c in range(n_dp):
+                    pairs.append((d * n_dp + c, (d ^ e) * n_dp + (c + t) % n_dp))
+            w_pieces.append(w_z if e == t == 0 else move(w_z, ("dom", "dp"), pairs))
     w_pieces += [move(piece, "dom", flip(n_dom, 1)) for piece in w_pieces]
     for core in range(2):
         for e in evens:

time: 102 us -> 103 us (level)
  starting transfers between devices: 36.2 us -> 43.2 us
  waiting for transfers between devices: 16.2 us -> 12.6 us
  Pallas kernels: 42.4 us -> 39.5 us
    ppermute x3, waiting for transfers between devices: 9.62 us -> 3.27 us  [compute(): tiles[0, k] = move(share[0], 'shard', ring(n_sh, k))]
    ppermute x3, starting transfers between devices: 10.1 us -> 15.6 us  [compute(): q_pieces = [q] + [move(q, 'shard', flip(n_sh, a)) for a in range(1, group)]]
    pallas_call x3, Pallas kernels: 18.3 us -> 16.1 us  [rebuild(): pl.pallas_call(functools.partial(rebuild_kernel, n_t, n_b), out_shape=(ja...]
    ppermute x4, waiting for transfers between devices: 0.01 us -> 2.15 us  [the longest x3 2.15 us: compute(): w_pieces.append(w_z if e == t == 0 else move(w_z, ('dom', 'dp'), pairs))]
    ppermute x4, starting transfers between devices: 4.12 us -> 5.3 us  [the longest x3 3.81 us: compute(): w_pieces.append(w_z if e == t == 0 else move(w_z, ('dom', 'dp'), pairs))]
  transfers between devices with their start and end apart: 28 -> 28, of which waited for: 6 -> 8; matrix products, arithmetic and copies ran while one was open for 5% -> 5% of each run, Pallas kernels for 23% -> 21%
where the time goes in v2:
time: 103 us
  starting transfers between devices  43.2 us (42%)
  Pallas kernels  39.5 us (38%)
  waiting for transfers between devices  12.6 us (12%)
  other arithmetic  4.43 us (4%)
  local copies, waits for them, and re-layouts  1.83 us (2%)
    pallas_call x1, Pallas kernels, main(): pl.pallas_call(functools.partial(main_kernel, n_q, n_w, n_g), out_shape=(...  17.9 us
    pallas_call x3, Pallas kernels, rebuild(): pl.pallas_call(functools.partial(rebuild_kernel, n_t, n_b), out_shape=(ja...  16.1 us
    ppermute x3, starting transfers between devices, compute(): q_pieces = [q] + [move(q, 'shard', flip(n_sh, a)) for a in range(1, group)]  15.6 us
    ppermute x3, starting transfers between devices, compute(): move(encoder_weight, 'shard', ring(n_sh, k))  7.24 us
    ppermute x3, waiting for transfers between devices, compute(): moved = move(summed[i, o], ('dom', 'shard', 'dp'), pairs)  6.17 us
    pallas_call x2, Pallas kernels, word_grads(): pl.pallas_call(functools.partial(words_kernel, words, block), out_shape=j...  5.58 us
    ppermute x3, starting transfers between devices, compute(): w_pieces.append(w_z if e == t == 0 else move(w_z, ('dom', 'dp'), pairs))  3.81 us
    ppermute x3, starting transfers between devices, compute(): moved = move(summed[i, o], ('dom', 'shard', 'dp'), pairs)  3.55 us
  transfers between devices with their start and end apart: 28, of which 8 were waited for; matrix products, arithmetic and copies ran while one was open for 5% of the time, Pallas kernels for 21%

profile of v2, /device:TPU:0, one launch (start us, length us, event | category | flops | bytes accessed | tf_op | source)
XLA Modules:
  0.0 102.6 jit_solution(13685052084530415872)
XLA Ops:
  0.6 3.1 %collective-permute-start.3 = (bf16[32,1024]{1,0:T(8,128)(2,1)}, bf16[32,1024]{1,0:T(8,128)(2,1)S(1)}, u32[]{:S(2)}, u32[]{:S(2)}) collective-permute-start(bf16[32,1024]{1,0:T(8,128)(2,1)} %param.7), channel_id=1, source_target_pairs={{0,2},{2,4},{4,6},{6,0},{1,3},{3,5},{5,7},{7,1},{8,10},{10,12},{12... | collective-permute-start | bytes 196616 | tf_op jit(solution)/shard_map/ppermute | solution.py:263
  3.7 2.1 %collective-permute-start.5 = (bf16[32,1024]{1,0:T(8,128)(2,1)}, bf16[32,1024]{1,0:T(8,128)(2,1)S(1)}, u32[]{:S(2)}, u32[]{:S(2)}) collective-permute-start(bf16[32,1024]{1,0:T(8,128)(2,1)} %param.7), channel_id=1, source_target_pairs={{0,6},{2,0},{4,2},{6,4},{1,7},{3,1},{5,3},{7,5},{8,14},{10,8},{12,... | collective-permute-start | bytes 196616 | tf_op jit(solution)/shard_map/ppermute | solution.py:263
  5.8 1.0 convert_element_type.15
  6.9 2.0 %collective-permute-start.15 = (bf16[16,8,256]{2,1,0:T(8,128)(2,1)S(1)}, bf16[16,8,256]{2,1,0:T(8,128)(2,1)S(1)}, u32[]{:S(2)}, u32[]{:S(2)}) collective-permute-start(bf16[16,8,256]{2,1,0:T(8,128)(2,1)S(1)} %get-tuple-element.31.refs_2_.refs_3_), channel_id=1, source_target_pairs={{0,6},{2,0},{4,2},{6,4},{1,7},{3,1},{5,3},{7,5},{8,14},{10,8},{12,... | collective-permute-start | bytes 196616 | tf_op jit(solution)/shard_map/ppermute | solution.py:269
  8.9 1.0 collective-permute-start.13
  10.2 0.7 convert_element_type.13
  10.9 0.7 fusion.3
  11.6 1.1 %convert_element_type.14 = bf16[1,1024,128]{2,1,0:T(8,128)(2,1)S(1)} convert(s32[1,1024,128]{2,1,0:T(8,128)} %param.9) | non-fusion elementwise | flops 131072 | bytes 786432 | tf_op jit(solution)/shard_map/convert_element_type | solution.py:277
  12.7 0.1 copy.10
  12.9 2.0 %collective-permute-start.4 = (bf16[32,1024]{1,0:T(8,128)(2,1)S(1)}, bf16[32,1024]{1,0:T(8,128)(2,1)S(1)}, u32[]{:S(2)}, u32[]{:S(2)}) collective-permute-start(bf16[32,1024]{1,0:T(8,128)(2,1)S(1)} %copy-done.1), channel_id=1, source_target_pairs={{0,4},{2,6},{4,0},{6,2},{1,5},{3,7},{5,1},{7,3},{8,12},{10,14},{12... | collective-permute-start | bytes 196616 | tf_op jit(solution)/shard_map/ppermute | solution.py:263
  14.9 1.0 collective-permute-done.14.refs_4_.refs_5_
  15.9 1.9 %collective-permute-start.19 = (bf16[128,512]{1,0:T(8,128)(2,1)S(1)}, bf16[128,512]{1,0:T(8,128)(2,1)S(1)}, u32[]{:S(2)}, u32[]{:S(2)}) collective-permute-start(bf16[128,512]{1,0:T(8,128)(2,1)S(1)} %bitcast.108), channel_id=1, source_target_pairs={{0,6},{2,0},{4,2},{6,4},{1,7},{3,1},{5,3},{7,5},{8,14},{10,8},{12,... | collective-permute-start | bytes 393224 | tf_op jit(solution)/shard_map/ppermute | solution.py:283
  17.8 0.7 collective-permute-start.17
  18.5 1.5 %collective-permute-start.16 = (bf16[48,8,256]{2,1,0:T(8,128)(2,1)S(1)}, bf16[48,8,256]{2,1,0:T(8,128)(2,1)S(1)}, u32[]{:S(2)}, u32[]{:S(2)}) collective-permute-start(bf16[48,8,256]{2,1,0:T(8,128)(2,1)S(1)} %pad_maximum_fusion.1), channel_id=1, source_target_pairs={{0,1},{1,0},{2,3},{3,2},{4,5},{5,4},{6,7},{7,6},{8,9},{9,8},{10,11... | collective-permute-start | bytes 589832 | tf_op jit(solution)/shard_map/ppermute | solution.py:273
  20.1 0.1 add.451.frow_ref
  20.2 0.1 copy.14.wt_ref
  20.4 0.1 copy.13.pos_ref
  20.5 0.1 copy.11
  20.9 6.4 %collective-permute-start.2 = (bf16[128,1024]{1,0:T(8,128)(2,1)S(1)}, bf16[128,1024]{1,0:T(8,128)(2,1)S(1)}, u32[]{:S(2)}, u32[]{:S(2)}) collective-permute-start(bf16[128,1024]{1,0:T(8,128)(2,1)S(1)} %bitcast.113), channel_id=1, source_target_pairs={{0,6},{2,4},{4,2},{6,0},{1,7},{3,5},{5,3},{7,1},{8,14},{10,12},{12... | collective-permute-start | bytes 786440 | tf_op jit(solution)/shard_map/ppermute | solution.py:291
  27.3 9.2 %collective-permute-start.1 = (bf16[128,1024]{1,0:T(8,128)(2,1)S(1)}, bf16[128,1024]{1,0:T(8,128)(2,1)S(1)}, u32[]{:S(2)}, u32[]{:S(2)}) collective-permute-start(bf16[128,1024]{1,0:T(8,128)(2,1)S(1)} %bitcast.114), channel_id=1, source_target_pairs={{0,4},{2,6},{4,0},{6,2},{1,5},{3,7},{5,1},{7,3},{8,12},{10,14},{12... | collective-permute-start | bytes 786440 | tf_op jit(solution)/shard_map/ppermute | solution.py:291
  36.4 3.3 %collective-permute-done.18.refs_1_ = bf16[128,512]{1,0:T(8,128)(2,1)S(1)} collective-permute-done((bf16[128,512]{1,0:T(8,128)(2,1)S(1)}, bf16[128,512]{1,0:T(8,128)(2,1)S(1)}, u32[]{:S(2)}, u32[]{:S(2)}) %collective-permute-start.18) | collective-permute-done | bytes 131104 | tf_op jit(solution)/shard_map/ppermute | solution.py:283
  39.7 1.5 %collective-permute-start.22 = (bf16[128,512]{1,0:T(8,128)(2,1)S(1)}, bf16[128,512]{1,0:T(8,128)(2,1)S(1)}, u32[]{:S(2)}, u32[]{:S(2)}) collective-permute-start(bf16[128,512]{1,0:T(8,128)(2,1)S(1)} %collective-permute-done.19.refs_2_), channel_id=1, source_target_pairs={{0,1},{1,0},{2,3},{3,2},{4,5},{5,4},{6,7},{7,6},{8,9},{9,8},{10,11... | collective-permute-start | bytes 393224 | tf_op jit(solution)/shard_map/ppermute | solution.py:287
  41.2 0.5 collective-permute-start.21
  41.7 1.5 %collective-permute-start.20 = (bf16[128,512]{1,0:T(8,128)(2,1)S(1)}, bf16[128,512]{1,0:T(8,128)(2,1)S(1)}, u32[]{:S(2)}, u32[]{:S(2)}) collective-permute-start(bf16[128,512]{1,0:T(8,128)(2,1)S(1)} %collective-permute-done.17.refs_0_), channel_id=1, source_target_pairs={{0,1},{1,0},{2,3},{3,2},{4,5},{5,4},{6,7},{7,6},{8,9},{9,8},{10,11... | collective-permute-start | bytes 393224 | tf_op jit(solution)/shard_map/ppermute | solution.py:287
  43.2 4.3 %shard_map.77 = (bf16[2,1024,512]{2,1,0:T(8,128)(2,1)S(1)}, s32[2,2,16,512]{3,2,1,0:T(8,128)S(1)}) custom-call(s32[8]{0:T(128)S(1)} %stack.271.place_ref, s32[2]{0:T(128)S(1)} %pad_add_fusion.1.blocks_ref, bf16[128,512]{1,0:T(8,128)(2,1)S(1)} %bitcast.111, bf16[128,512]{1,0:T(8,128)(2,1)S(1)} %bitcast.112, ...), custom_call_target="tpu_custom_call" | custom-call | flops 2000000000 | bytes 4000000 | tf_op jit(solution)/shard_map/pallas_call | solution.py:82
  47.6 1.6 %collective-permute-start.8 = (bf16[4,32,1024]{2,1,0:T(8,128)(2,1)S(1)}, bf16[4,32,1024]{2,1,0:T(8,128)(2,1)S(1)}, u32[]{:S(2)}, u32[]{:S(2)}) collective-permute-start(bf16[4,32,1024]{2,1,0:T(8,128)(2,1)S(1)} %pad_maximum_fusion.refs_4_), channel_id=1, source_target_pairs={{0,17},{1,16},{8,25},{9,24},{16,1},{17,0},{24,9},{25,8},{2,19},{3,... | collective-permute-start | bytes 786440 | tf_op jit(solution)/shard_map/ppermute | solution.py:301
  49.1 0.5 collective-permute-start.7
  49.6 1.7 %collective-permute-start.6 = (bf16[4,32,1024]{2,1,0:T(8,128)(2,1)S(1)}, bf16[4,32,1024]{2,1,0:T(8,128)(2,1)S(1)}, u32[]{:S(2)}, u32[]{:S(2)}) collective-permute-start(bf16[4,32,1024]{2,1,0:T(8,128)(2,1)S(1)} %pad_maximum_fusion.refs_4_), channel_id=1, source_target_pairs={{0,1},{1,0},{8,9},{9,8},{16,17},{17,16},{24,25},{25,24},{2,3},{3,2... | collective-permute-start | bytes 786440 | tf_op jit(solution)/shard_map/ppermute | solution.py:301
  51.4 5.9 %shard_map.78 = (bf16[3,1024,512]{2,1,0:T(8,128)(2,1)S(1)}, s32[3,2,16,512]{3,2,1,0:T(8,128)S(1)}) custom-call(s32[8]{0:T(128)S(1)} %stack.271.place_ref, s32[2]{0:T(128)S(1)} %pad_add_fusion.1.blocks_ref, bf16[128,512]{1,0:T(8,128)(2,1)S(1)} %collective-permute-done.17.refs_0_, bf16[128,512]{1,0:T(8,128)(2,1)S(1)} %collective-permute-done.18.refs_1_, ...), custom_call_target="tpu_custom_call" | custom-call | flops 3000000000 | bytes 6000000 | tf_op jit(solution)/shard_map/pallas_call | solution.py:82
  57.5 0.3 collective-permute-done.8.refs_7_
  57.7 0.2 collective-permute-start.12
  58.0 1.6 %collective-permute-done.7.refs_6_ = bf16[4,32,1024]{2,1,0:T(8,128)(2,1)S(1)} collective-permute-done((bf16[4,32,1024]{2,1,0:T(8,128)(2,1)S(1)}, bf16[4,32,1024]{2,1,0:T(8,128)(2,1)S(1)}, u32[]{:S(2)}, u32[]{:S(2)}) %collective-permute-start.7) | collective-permute-done | bytes 262176 | tf_op jit(solution)/shard_map/ppermute | solution.py:301
  59.5 0.3 collective-permute-done.6.refs_5_
  59.8 0.2 collective-permute-start.10
  60.0 5.9 %shard_map.79 = (bf16[3,1024,512]{2,1,0:T(8,128)(2,1)S(1)}, s32[3,2,16,512]{3,2,1,0:T(8,128)S(1)}) custom-call(s32[8]{0:T(128)S(1)} %stack.271.place_ref, s32[2]{0:T(128)S(1)} %pad_add_fusion.1.blocks_ref, bf16[128,512]{1,0:T(8,128)(2,1)S(1)} %collective-permute-done.20.refs_0_, bf16[128,512]{1,0:T(8,128)(2,1)S(1)} %collective-permute-done.21.refs_1_, ...), custom_call_target="tpu_custom_call" | custom-call | flops 3000000000 | bytes 6000000 | tf_op jit(solution)/shard_map/pallas_call | solution.py:82
  66.0 17.9 %shard_map.80 = (f32[128,1024]{1,0:T(8,128)S(1)}, f32[128,1024]{1,0:T(8,128)S(1)}, f32[128,4096]{1,0:T(8,128)S(1)}, f32[128,4096]{1,0:T(8,128)S(1)}) custom-call(s32[32]{0:T(128)S(1)} %broadcast_multiply_fusion.woff_ref, s32[8]{0:T(128)S(1)} %stack.245.tbase_ref, s32[2]{0:T(128)S(1)} %pad_add_fusion.1.blocks_ref, s32[256,1]{1,0:T(8,128)S(1)} %add.451.frow_ref, ...), custom_call_target="tpu_custom_call" | custom-call | flops 20000000000 | bytes 20000000 | tf_op jit(solution)/shard_map/pallas_call | solution.py:174
  83.9 0.4 collective-permute-start.23
  84.2 2.8 %shard_map.81 = f32[16,8,256]{2,1,0:T(8,128)S(1)} custom-call(f32[128,4096]{1,0:T(8,128)S(1)} %get-tuple-element.17.grads_ref, s32[2,2,16,512]{3,2,1,0:T(8,128)S(1)} %get-tuple-element.18.refs_0_, s32[3,2,16,512]{3,2,1,0:T(8,128)S(1)} %get-tuple-element.19.refs_1_, s32[3,2,16,512]{3,2,1,0:T(8,128)S(1)} %get-tuple-element.20.refs_2_), custom_call_target="tpu_custom_call" | custom-call | flops 3000000000 | bytes 4000000 | tf_op jit(solution)/shard_map/pallas_call | solution.py:241
  87.0 1.5 %collective-permute-start.27 = (f32[16,8,256]{2,1,0:T(8,128)S(1)}, f32[16,8,256]{2,1,0:T(8,128)S(1)}, u32[]{:S(2)}, u32[]{:S(2)}) collective-permute-start(f32[16,8,256]{2,1,0:T(8,128)S(1)} %shard_map.81), channel_id=1, source_target_pairs={{0,1},{1,0},{2,3},{3,2},{4,5},{5,4},{6,7},{7,6},{8,9},{9,8},{10,11... | collective-permute-start | bytes 393224 | tf_op jit(solution)/shard_map/ppermute | solution.py:368
  88.6 2.8 %shard_map.82 = f32[16,8,256]{2,1,0:T(8,128)S(1)} custom-call(f32[128,4096]{1,0:T(8,128)S(1)} %get-tuple-element.21.grads_ref, s32[2,2,16,512]{3,2,1,0:T(8,128)S(1)} %get-tuple-element.18.refs_0_, s32[3,2,16,512]{3,2,1,0:T(8,128)S(1)} %get-tuple-element.19.refs_1_, s32[3,2,16,512]{3,2,1,0:T(8,128)S(1)} %get-tuple-element.20.refs_2_), custom_call_target="tpu_custom_call" | custom-call | flops 3000000000 | bytes 4000000 | tf_op jit(solution)/shard_map/pallas_call | solution.py:241
  91.5 0.6 collective-permute-start.24
  92.1 2.4 %collective-permute-start.26 = (f32[32,1024]{1,0:T(8,128)S(1)}, f32[32,1024]{1,0:T(8,128)S(1)}, u32[]{:S(2)}, u32[]{:S(2)}) collective-permute-start(f32[32,1024]{1,0:T(8,128)S(1)} %get-tuple-element.23), channel_id=1, source_target_pairs={{0,17},{1,16},{2,19},{3,18},{4,21},{5,20},{6,23},{7,22},{8,25},{9,... | collective-permute-start | bytes 393224 | tf_op jit(solution)/shard_map/ppermute | solution.py:381
  94.5 0.5 collective-permute-start.25
  95.0 0.7 add_bitcast_fusion
  95.7 2.2 %collective-permute-done.24 = f32[32,1024]{1,0:T(8,128)S(1)} collective-permute-done((f32[32,1024]{1,0:T(8,128)S(1)}, f32[32,1024]{1,0:T(8,128)S(1)}, u32[]{:S(2)}, u32[]{:S(2)}) %collective-permute-start.24) | collective-permute-done | bytes 131104 | tf_op jit(solution)/shard_map/ppermute | solution.py:381
  97.9 2.6 %collective-permute-done.26 = f32[32,1024]{1,0:T(8,128)S(1)} collective-permute-done((f32[32,1024]{1,0:T(8,128)S(1)}, f32[32,1024]{1,0:T(8,128)S(1)}, u32[]{:S(2)}, u32[]{:S(2)}) %collective-permute-start.26) | collective-permute-done | bytes 131104 | tf_op jit(solution)/shard_map/ppermute | solution.py:381
  100.5 1.4 %collective-permute-done.25 = f32[32,1024]{1,0:T(8,128)S(1)} collective-permute-done((f32[32,1024]{1,0:T(8,128)S(1)}, f32[32,1024]{1,0:T(8,128)S(1)}, u32[]{:S(2)}, u32[]{:S(2)}) %collective-permute-start.25) | collective-permute-done | bytes 131104 | tf_op jit(solution)/shard_map/ppermute | solution.py:381
  101.9 0.7 fusion.2
  (46 shorter events, 1.0 us)
Async XLA Ops:
  0.6 12.3 %copy-start.1 = (bf16[32,1024]{1,0:T(8,128)(2,1)S(1)}, bf16[32,1024]{1,0:T(8,128)(2,1)}, u32[]{:S(2)}) copy-start(bf16[32,1024]{1,0:T(8,128)(2,1)} %param.7) | copy-start | bytes 196612
  0.6 17.2 %collective-permute-start.3 = (bf16[32,1024]{1,0:T(8,128)(2,1)}, bf16[32,1024]{1,0:T(8,128)(2,1)S(1)}, u32[]{:S(2)}, u32[]{:S(2)}) collective-permute-start(bf16[32,1024]{1,0:T(8,128)(2,1)} %param.7), channel_id=1, source_target_pairs={{0,2},{2,4},{4,6},{6,0},{1,3},{3,5},{5,7},{7,1},{8,10},{10,12},{12... | collective-permute-start | bytes 196616 | tf_op jit(solution)/shard_map/ppermute | solution.py:263
  3.7 14.8 %collective-permute-start.5 = (bf16[32,1024]{1,0:T(8,128)(2,1)}, bf16[32,1024]{1,0:T(8,128)(2,1)S(1)}, u32[]{:S(2)}, u32[]{:S(2)}) collective-permute-start(bf16[32,1024]{1,0:T(8,128)(2,1)} %param.7), channel_id=1, source_target_pairs={{0,6},{2,0},{4,2},{6,4},{1,7},{3,1},{5,3},{7,5},{8,14},{10,8},{12,... | collective-permute-start | bytes 196616 | tf_op jit(solution)/shard_map/ppermute | solution.py:263
  5.8 15.0 %copy-start = (bf16[1,128,1024]{2,1,0:T(8,128)(2,1)S(1)}, bf16[1,128,1024]{2,1,0:T(8,128)(2,1)}, u32[]{:S(2)}) copy-start(bf16[1,128,1024]{2,1,0:T(8,128)(2,1)} %param.6) | copy-start | bytes 786436
  6.9 6.0 %collective-permute-start.15 = (bf16[16,8,256]{2,1,0:T(8,128)(2,1)S(1)}, bf16[16,8,256]{2,1,0:T(8,128)(2,1)S(1)}, u32[]{:S(2)}, u32[]{:S(2)}) collective-permute-start(bf16[16,8,256]{2,1,0:T(8,128)(2,1)S(1)} %get-tuple-element.31.refs_2_.refs_3_), channel_id=1, source_target_pairs={{0,6},{2,0},{4,2},{6,4},{1,7},{3,1},{5,3},{7,5},{8,14},{10,8},{12,... | collective-permute-start | bytes 196616 | tf_op jit(solution)/shard_map/ppermute | solution.py:269
  8.9 7.0 %collective-permute-start.14 = (bf16[16,8,256]{2,1,0:T(8,128)(2,1)S(1)}, bf16[16,8,256]{2,1,0:T(8,128)(2,1)S(1)}, u32[]{:S(2)}, u32[]{:S(2)}) collective-permute-start(bf16[16,8,256]{2,1,0:T(8,128)(2,1)S(1)} %get-tuple-element.31.refs_2_.refs_3_), channel_id=1, source_target_pairs={{0,4},{2,6},{4,0},{6,2},{1,5},{3,7},{5,1},{7,3},{8,12},{10,14},{12... | collective-permute-start | bytes 196616 | tf_op jit(solution)/shard_map/ppermute | solution.py:269
  8.9 8.9 %collective-permute-start.13 = (bf16[16,8,256]{2,1,0:T(8,128)(2,1)S(1)}, bf16[16,8,256]{2,1,0:T(8,128)(2,1)S(1)}, u32[]{:S(2)}, u32[]{:S(2)}) collective-permute-start(bf16[16,8,256]{2,1,0:T(8,128)(2,1)S(1)} %get-tuple-element.31.refs_2_.refs_3_), channel_id=1, source_target_pairs={{0,2},{2,4},{4,6},{6,0},{1,3},{3,5},{5,7},{7,1},{8,10},{10,12},{12... | collective-permute-start | bytes 196616 | tf_op jit(solution)/shard_map/ppermute | solution.py:269
  12.9 8.0 %collective-permute-start.4 = (bf16[32,1024]{1,0:T(8,128)(2,1)S(1)}, bf16[32,1024]{1,0:T(8,128)(2,1)S(1)}, u32[]{:S(2)}, u32[]{:S(2)}) collective-permute-start(bf16[32,1024]{1,0:T(8,128)(2,1)S(1)} %copy-done.1), channel_id=1, source_target_pairs={{0,4},{2,6},{4,0},{6,2},{1,5},{3,7},{5,1},{7,3},{8,12},{10,14},{12... | collective-permute-start | bytes 196616 | tf_op jit(solution)/shard_map/ppermute | solution.py:263
  15.9 11.4 %collective-permute-start.19 = (bf16[128,512]{1,0:T(8,128)(2,1)S(1)}, bf16[128,512]{1,0:T(8,128)(2,1)S(1)}, u32[]{:S(2)}, u32[]{:S(2)}) collective-permute-start(bf16[128,512]{1,0:T(8,128)(2,1)S(1)} %bitcast.108), channel_id=1, source_target_pairs={{0,6},{2,0},{4,2},{6,4},{1,7},{3,1},{5,3},{7,5},{8,14},{10,8},{12,... | collective-permute-start | bytes 393224 | tf_op jit(solution)/shard_map/ppermute | solution.py:283
  17.8 21.9 %collective-permute-start.18 = (bf16[128,512]{1,0:T(8,128)(2,1)S(1)}, bf16[128,512]{1,0:T(8,128)(2,1)S(1)}, u32[]{:S(2)}, u32[]{:S(2)}) collective-permute-start(bf16[128,512]{1,0:T(8,128)(2,1)S(1)} %bitcast.109), channel_id=1, source_target_pairs={{0,4},{2,6},{4,0},{6,2},{1,5},{3,7},{5,1},{7,3},{8,12},{10,14},{12... | collective-permute-start | bytes 393224 | tf_op jit(solution)/shard_map/ppermute | solution.py:283
  17.8 23.3 %collective-permute-start.17 = (bf16[128,512]{1,0:T(8,128)(2,1)S(1)}, bf16[128,512]{1,0:T(8,128)(2,1)S(1)}, u32[]{:S(2)}, u32[]{:S(2)}) collective-permute-start(bf16[128,512]{1,0:T(8,128)(2,1)S(1)} %bitcast.110), channel_id=1, source_target_pairs={{0,2},{2,4},{4,6},{6,0},{1,3},{3,5},{5,7},{7,1},{8,10},{10,12},{12... | collective-permute-start | bytes 393224 | tf_op jit(solution)/shard_map/ppermute | solution.py:283
  18.5 23.2 %collective-permute-start.16 = (bf16[48,8,256]{2,1,0:T(8,128)(2,1)S(1)}, bf16[48,8,256]{2,1,0:T(8,128)(2,1)S(1)}, u32[]{:S(2)}, u32[]{:S(2)}) collective-permute-start(bf16[48,8,256]{2,1,0:T(8,128)(2,1)S(1)} %pad_maximum_fusion.1), channel_id=1, source_target_pairs={{0,1},{1,0},{2,3},{3,2},{4,5},{5,4},{6,7},{7,6},{8,9},{9,8},{10,11... | collective-permute-start | bytes 589832 | tf_op jit(solution)/shard_map/ppermute | solution.py:273
  20.9 36.4 %collective-permute-start.2 = (bf16[128,1024]{1,0:T(8,128)(2,1)S(1)}, bf16[128,1024]{1,0:T(8,128)(2,1)S(1)}, u32[]{:S(2)}, u32[]{:S(2)}) collective-permute-start(bf16[128,1024]{1,0:T(8,128)(2,1)S(1)} %bitcast.113), channel_id=1, source_target_pairs={{0,6},{2,4},{4,2},{6,0},{1,7},{3,5},{5,3},{7,1},{8,14},{10,12},{12... | collective-permute-start | bytes 786440 | tf_op jit(solution)/shard_map/ppermute | solution.py:291
  27.3 30.1 %collective-permute-start.1 = (bf16[128,1024]{1,0:T(8,128)(2,1)S(1)}, bf16[128,1024]{1,0:T(8,128)(2,1)S(1)}, u32[]{:S(2)}, u32[]{:S(2)}) collective-permute-start(bf16[128,1024]{1,0:T(8,128)(2,1)S(1)} %bitcast.114), channel_id=1, source_target_pairs={{0,4},{2,6},{4,0},{6,2},{1,5},{3,7},{5,1},{7,3},{8,12},{10,14},{12... | collective-permute-start | bytes 786440 | tf_op jit(solution)/shard_map/ppermute | solution.py:291
  39.7 7.9 %collective-permute-start.22 = (bf16[128,512]{1,0:T(8,128)(2,1)S(1)}, bf16[128,512]{1,0:T(8,128)(2,1)S(1)}, u32[]{:S(2)}, u32[]{:S(2)}) collective-permute-start(bf16[128,512]{1,0:T(8,128)(2,1)S(1)} %collective-permute-done.19.refs_2_), channel_id=1, source_target_pairs={{0,1},{1,0},{2,3},{3,2},{4,5},{5,4},{6,7},{7,6},{8,9},{9,8},{10,11... | collective-permute-start | bytes 393224 | tf_op jit(solution)/shard_map/ppermute | solution.py:287
  41.2 7.9 %collective-permute-start.21 = (bf16[128,512]{1,0:T(8,128)(2,1)S(1)}, bf16[128,512]{1,0:T(8,128)(2,1)S(1)}, u32[]{:S(2)}, u32[]{:S(2)}) collective-permute-start(bf16[128,512]{1,0:T(8,128)(2,1)S(1)} %collective-permute-done.18.refs_1_), channel_id=1, source_target_pairs={{0,1},{1,0},{2,3},{3,2},{4,5},{5,4},{6,7},{7,6},{8,9},{9,8},{10,11... | collective-permute-start | bytes 393224 | tf_op jit(solution)/shard_map/ppermute | solution.py:287
  41.7 7.9 %collective-permute-start.20 = (bf16[128,512]{1,0:T(8,128)(2,1)S(1)}, bf16[128,512]{1,0:T(8,128)(2,1)S(1)}, u32[]{:S(2)}, u32[]{:S(2)}) collective-permute-start(bf16[128,512]{1,0:T(8,128)(2,1)S(1)} %collective-permute-done.17.refs_0_), channel_id=1, source_target_pairs={{0,1},{1,0},{2,3},{3,2},{4,5},{5,4},{6,7},{7,6},{8,9},{9,8},{10,11... | collective-permute-start | bytes 393224 | tf_op jit(solution)/shard_map/ppermute | solution.py:287
  47.6 10.1 %collective-permute-start.8 = (bf16[4,32,1024]{2,1,0:T(8,128)(2,1)S(1)}, bf16[4,32,1024]{2,1,0:T(8,128)(2,1)S(1)}, u32[]{:S(2)}, u32[]{:S(2)}) collective-permute-start(bf16[4,32,1024]{2,1,0:T(8,128)(2,1)S(1)} %pad_maximum_fusion.refs_4_), channel_id=1, source_target_pairs={{0,17},{1,16},{8,25},{9,24},{16,1},{17,0},{24,9},{25,8},{2,19},{3,... | collective-permute-start | bytes 786440 | tf_op jit(solution)/shard_map/ppermute | solution.py:301
  49.1 10.4 %collective-permute-start.7 = (bf16[4,32,1024]{2,1,0:T(8,128)(2,1)S(1)}, bf16[4,32,1024]{2,1,0:T(8,128)(2,1)S(1)}, u32[]{:S(2)}, u32[]{:S(2)}) collective-permute-start(bf16[4,32,1024]{2,1,0:T(8,128)(2,1)S(1)} %pad_maximum_fusion.refs_4_), channel_id=1, source_target_pairs={{0,16},{1,17},{8,24},{9,25},{16,0},{17,1},{24,8},{25,9},{2,18},{3,... | collective-permute-start | bytes 786440 | tf_op jit(solution)/shard_map/ppermute | solution.py:301
  49.6 10.2 %collective-permute-start.6 = (bf16[4,32,1024]{2,1,0:T(8,128)(2,1)S(1)}, bf16[4,32,1024]{2,1,0:T(8,128)(2,1)S(1)}, u32[]{:S(2)}, u32[]{:S(2)}) collective-permute-start(bf16[4,32,1024]{2,1,0:T(8,128)(2,1)S(1)} %pad_maximum_fusion.refs_4_), channel_id=1, source_target_pairs={{0,1},{1,0},{8,9},{9,8},{16,17},{17,16},{24,25},{25,24},{2,3},{3,2... | collective-permute-start | bytes 786440 | tf_op jit(solution)/shard_map/ppermute | solution.py:301
  57.3 8.6 %collective-permute-start = (bf16[128,1024]{1,0:T(8,128)(2,1)S(1)}, bf16[128,1024]{1,0:T(8,128)(2,1)S(1)}, u32[]{:S(2)}, u32[]{:S(2)}) collective-permute-start(bf16[128,1024]{1,0:T(8,128)(2,1)S(1)} %bitcast.115), channel_id=1, source_target_pairs={{0,2},{2,0},{4,6},{6,4},{1,3},{3,1},{5,7},{7,5},{8,10},{10,8},{12,... | collective-permute-start | bytes 786440 | tf_op jit(solution)/shard_map/ppermute | solution.py:291
  57.4 8.6 %collective-permute-start.9 = (bf16[4,32,1024]{2,1,0:T(8,128)(2,1)S(1)}, bf16[4,32,1024]{2,1,0:T(8,128)(2,1)S(1)}, u32[]{:S(2)}, u32[]{:S(2)}) collective-permute-start(bf16[4,32,1024]{2,1,0:T(8,128)(2,1)S(1)} %pad_maximum_fusion.refs_4_), channel_id=1, source_target_pairs={{0,8},{8,0},{16,24},{24,16},{1,9},{9,1},{17,25},{25,17},{2,10},{10... | collective-permute-start | bytes 786440 | tf_op jit(solution)/shard_map/ppermute | solution.py:302
  57.7 8.2 %collective-permute-start.12 = (bf16[4,32,1024]{2,1,0:T(8,128)(2,1)S(1)}, bf16[4,32,1024]{2,1,0:T(8,128)(2,1)S(1)}, u32[]{:S(2)}, u32[]{:S(2)}) collective-permute-start(bf16[4,32,1024]{2,1,0:T(8,128)(2,1)S(1)} %collective-permute-done.8.refs_7_), channel_id=1, source_target_pairs={{0,8},{8,0},{16,24},{24,16},{1,9},{9,1},{17,25},{25,17},{2,10},{10... | collective-permute-start | bytes 786440 | tf_op jit(solution)/shard_map/ppermute | solution.py:302
  59.5 6.4 %collective-permute-start.11 = (bf16[4,32,1024]{2,1,0:T(8,128)(2,1)S(1)}, bf16[4,32,1024]{2,1,0:T(8,128)(2,1)S(1)}, u32[]{:S(2)}, u32[]{:S(2)}) collective-permute-start(bf16[4,32,1024]{2,1,0:T(8,128)(2,1)S(1)} %collective-permute-done.7.refs_6_), channel_id=1, source_target_pairs={{0,8},{8,0},{16,24},{24,16},{1,9},{9,1},{17,25},{25,17},{2,10},{10... | collective-permute-start | bytes 786440 | tf_op jit(solution)/shard_map/ppermute | solution.py:302
  59.8 6.1 %collective-permute-start.10 = (bf16[4,32,1024]{2,1,0:T(8,128)(2,1)S(1)}, bf16[4,32,1024]{2,1,0:T(8,128)(2,1)S(1)}, u32[]{:S(2)}, u32[]{:S(2)}) collective-permute-start(bf16[4,32,1024]{2,1,0:T(8,128)(2,1)S(1)} %collective-permute-done.6.refs_5_), channel_id=1, source_target_pairs={{0,8},{8,0},{16,24},{24,16},{1,9},{9,1},{17,25},{25,17},{2,10},{10... | collective-permute-start | bytes 786440 | tf_op jit(solution)/shard_map/ppermute | solution.py:302
  83.9 7.5 %collective-permute-start.23 = (f32[128,1024]{1,0:T(8,128)S(1)}, f32[128,1024]{1,0:T(8,128)S(1)}, u32[]{:S(2)}, u32[]{:S(2)}) collective-permute-start(f32[128,1024]{1,0:T(8,128)S(1)} %get-tuple-element.16), channel_id=1, source_target_pairs={{0,8},{8,0},{16,24},{24,16},{1,9},{9,1},{17,25},{25,17},{2,10},{10... | collective-permute-start | bytes 1572872 | tf_op jit(solution)/shard_map/ppermute | solution.py:356
  87.0 8.0 %collective-permute-start.27 = (f32[16,8,256]{2,1,0:T(8,128)S(1)}, f32[16,8,256]{2,1,0:T(8,128)S(1)}, u32[]{:S(2)}, u32[]{:S(2)}) collective-permute-start(f32[16,8,256]{2,1,0:T(8,128)S(1)} %shard_map.81), channel_id=1, source_target_pairs={{0,1},{1,0},{2,3},{3,2},{4,5},{5,4},{6,7},{7,6},{8,9},{9,8},{10,11... | collective-permute-start | bytes 393224 | tf_op jit(solution)/shard_map/ppermute | solution.py:368
  91.5 6.4 %collective-permute-start.24 = (f32[32,1024]{1,0:T(8,128)S(1)}, f32[32,1024]{1,0:T(8,128)S(1)}, u32[]{:S(2)}, u32[]{:S(2)}) collective-permute-start(f32[32,1024]{1,0:T(8,128)S(1)} %get-tuple-element.22), channel_id=1, source_target_pairs={{0,1},{1,0},{2,3},{3,2},{4,5},{5,4},{6,7},{7,6},{8,9},{9,8},{10,11... | collective-permute-start | bytes 393224 | tf_op jit(solution)/shard_map/ppermute | solution.py:381
  92.1 8.4 %collective-permute-start.26 = (f32[32,1024]{1,0:T(8,128)S(1)}, f32[32,1024]{1,0:T(8,128)S(1)}, u32[]{:S(2)}, u32[]{:S(2)}) collective-permute-start(f32[32,1024]{1,0:T(8,128)S(1)} %get-tuple-element.23), channel_id=1, source_target_pairs={{0,17},{1,16},{2,19},{3,18},{4,21},{5,20},{6,23},{7,22},{8,25},{9,... | collective-permute-start | bytes 393224 | tf_op jit(solution)/shard_map/ppermute | solution.py:381
  94.5 7.4 %collective-permute-start.25 = (f32[32,1024]{1,0:T(8,128)S(1)}, f32[32,1024]{1,0:T(8,128)S(1)}, u32[]{:S(2)}, u32[]{:S(2)}) collective-permute-start(f32[32,1024]{1,0:T(8,128)S(1)} %get-tuple-element.24), channel_id=1, source_target_pairs={{0,16},{1,17},{2,18},{3,19},{4,20},{5,21},{6,22},{7,23},{8,24},{9,... | collective-permute-start | bytes 393224 | tf_op jit(solution)/shard_map/ppermute | solution.py:381

commit v3 on v2

--- a/solution.py
+++ b/solution.py
@@ -14,7 +14,7 @@
 ANY = pl.BlockSpec(memory_space=pl.ANY)
 VMEM = pl.BlockSpec(memory_space=pltpu.VMEM)
 SMEM = pl.BlockSpec(memory_space=pltpu.SMEM)
-SPAN = 32
+SPAN = 64
 MIB = 2**20
 
 
@@ -33,7 +33,7 @@
 def rebuild_kernel(n_t, n_b, place_ref, blocks_ref, *refs):
     code_refs, books = refs[:n_t], refs[n_t : n_t + n_b]
     out_ref, kept_ref, codes_ref, table = refs[n_t + n_b :]
-    held, sub, words = books[0].shape
+    sub, words = table.shape[1:]
     columns = code_refs[0].shape[1]
     kept = kept_ref.shape[2]
     for i, code_ref in enumerate(code_refs):
@@ -41,7 +41,11 @@
         for b in range(kept_ref.shape[1]):
             kept_ref[i, b] = codes_ref[i, pl.ds(pl.multiple_of(blocks_ref[b] * kept, kept), kept), :]
     for piece, book_ref in enumerate(books):
-        table[pl.ds(place_ref[piece] * held, held)] = book_ref[...].astype(F32)
+        some = book_ref.shape[0] // sub
+        blocks = book_ref.shape[1] // words
+        for c in range(blocks):
+            part = book_ref[:, c * words : (c + 1) * words].astype(F32).reshape(some, sub, words)
+            table[pl.ds((place_ref[piece] * blocks + c) * some, some)] = part
 
     subspaces = code_refs[0].shape[0]
     span = min(subspaces, SPAN)
@@ -75,10 +79,9 @@
     lax.fori_loop(0, n_t * steps, body, 0)
 
 
-def rebuild(place, blocks, kept, codes, books):
+def rebuild(place, blocks, kept, sub, words, codes, books):
     n_t, n_b = len(codes), len(books)
     subspaces, columns = codes[0].shape
-    _, sub, words = books[0].shape
     return pl.pallas_call(
         functools.partial(rebuild_kernel, n_t, n_b),
         out_shape=(
@@ -260,18 +263,24 @@
     move = lax.ppermute
 
     w_rows, depth = encoder_weight.shape
-    w_z = jnp.stack([encoder_weight] + [move(encoder_weight, "shard", ring(n_sh, k)) for k in range(1, n_sh)])
-
     book = codebook[0].astype(BF16)
-    words = book.shape[2]
+    words, sub = book.shape[2], book.shape[1]
     held_words = book.shape[0] // n_dp
-    book_share = [lax.dynamic_slice_in_dim(book, lanes[t] * held_words, held_words, 0) for t in range(n_dp)]
-    moved = [move(book_share[0], "shard", ring(n_sh, k)) for k in range(1, n_sh)]
-    books = [book_share[0]] + moved
-    moved = jnp.concatenate(moved)
+    columns = depth // words
+
+    def packed(t):
+        mine = lax.dynamic_slice_in_dim(book, lanes[t] * held_words, held_words, 0)
+        return jnp.concatenate(jnp.split(mine.reshape(held_words * sub, words), columns), 1)
+
+    packs = [packed(t) for t in range(n_dp)]
+    packet = jnp.concatenate([encoder_weight, packs[0]])
+    moved = [move(packet, "shard", ring(n_sh, k)) for k in range(1, n_sh)]
+    w_z = jnp.stack([encoder_weight] + [m[:w_rows] for m in moved])
+    moved = jnp.concatenate([m[w_rows:] for m in moved])
+    books = [packs[0]] + jnp.split(moved, n_sh - 1)
     for t in range(1, n_dp):
         across = move(moved, "dp", ring(n_dp, t))
-        books += [book_share[t]] + jnp.split(across, n_sh - 1)
+        books += [packs[t]] + jnp.split(across, n_sh - 1)
     place = jnp.stack([shards[k] * n_dp + lanes[t] for t in range(n_dp) for k in range(n_sh)]).astype(I32)
 
     codes_t = codes[0].T.astype(BF16)
@@ -325,7 +334,7 @@
     bases = [shards[k] * pass_rows + lanes[t] * width for part in order for t, k in part]
     built = []
     for part in order:
-        built.append(rebuild(place, blocks, held, [tiles[key] for key in part], books))
+        built.append(rebuild(place, blocks, held, sub, words, [tiles[key] for key in part], books))
     passages = [b[0] for b in built]
     tile_codes = [b[1] for b in built]
 

time: 103 us -> 104 us (level)
  waiting for transfers between devices: 12.6 us -> 23.1 us
  starting transfers between devices: 43.2 us -> 35.4 us
  Pallas kernels: 39.5 us -> 38.2 us
    ppermute x3, waiting for transfers between devices: 3.27 us -> 8.89 us  [compute(): tiles[0, k] = move(share[0], 'shard', ring(n_sh, k))]
    ppermute x3, starting transfers between devices: 15.6 us -> 10.2 us  [compute(): q_pieces = [q] + [move(q, 'shard', flip(n_sh, a)) for a in range(1, group)]]
    ppermute x6 -> x3, waiting for transfers between devices: 0.97 us -> 6.06 us  [compute(): moved = [move(packet, 'shard', ring(n_sh, k)) for k in range(1, n_sh)]]
    ppermute x6 -> x3, starting transfers between devices: 10.3 us -> 6.14 us  [compute(): moved = [move(packet, 'shard', ring(n_sh, k)) for k in range(1, n_sh)]]
    ppermute x3, waiting for transfers between devices: 2.15 us -> 0.01 us  [compute(): w_pieces.append(w_z if e == t == 0 else move(w_z, ('dom', 'dp'), pairs))]
    ppermute x3, waiting for transfers between devices: 0.01 us -> 1.53 us  [compute(): tiles[t, k] = move(tiles[0, k], 'dp', ring(n_dp, t))]
    ppermute x3, starting transfers between devices: 2.59 us -> 4.05 us  [compute(): tiles[0, k] = move(share[0], 'shard', ring(n_sh, k))]
    pallas_call x3, Pallas kernels: 16.1 us -> 14.7 us  [rebuild(): pl.pallas_call(functools.partial(rebuild_kernel, n_t, n_b), out_shape=(ja...]
  transfers between devices with their start and end apart: 28 -> 25, of which waited for: 8 -> 7; matrix products, arithmetic and copies ran while one was open for 5% -> 3% of each run, Pallas kernels for 21% -> 20%
where the time goes in v3:
time: 104 us
  Pallas kernels  38.2 us (37%)
  starting transfers between devices  35.4 us (34%)
  waiting for transfers between devices  23.1 us (22%)
  other arithmetic  4.65 us (4%)
  local copies, waits for them, and re-layouts  1.21 us (1%)
    pallas_call x1, Pallas kernels, main(): pl.pallas_call(functools.partial(main_kernel, n_q, n_w, n_g), out_shape=(...  17.9 us
    pallas_call x3, Pallas kernels, rebuild(): pl.pallas_call(functools.partial(rebuild_kernel, n_t, n_b), out_shape=(ja...  14.7 us
    ppermute x3, starting transfers between devices, compute(): q_pieces = [q] + [move(q, 'shard', flip(n_sh, a)) for a in range(1, group)]  10.2 us
    ppermute x3, waiting for transfers between devices, compute(): tiles[0, k] = move(share[0], 'shard', ring(n_sh, k))  8.89 us
    ppermute x3, waiting for transfers between devices, compute(): moved = move(summed[i, o], ('dom', 'shard', 'dp'), pairs)  6.59 us
    ppermute x3, starting transfers between devices, compute(): moved = [move(packet, 'shard', ring(n_sh, k)) for k in range(1, n_sh)]  6.14 us
    ppermute x3, waiting for transfers between devices, compute(): moved = [move(packet, 'shard', ring(n_sh, k)) for k in range(1, n_sh)]  6.06 us
    pallas_call x2, Pallas kernels, word_grads(): pl.pallas_call(functools.partial(words_kernel, words, block), out_shape=j...  5.58 us
  transfers between devices with their start and end apart: 25, of which 7 were waited for; matrix products, arithmetic and copies ran while one was open for 3% of the time, Pallas kernels for 20%

profile of v3, /device:TPU:0, one launch (start us, length us, event | category | flops | bytes accessed | tf_op | source)
XLA Modules:
  0.0 103.5 jit_solution(8183494318313216483)
XLA Ops:
  0.7 1.0 convert_element_type.14
  1.7 0.9 maximum_maximum_fusion
  2.6 5.1 %collective-permute-start.5 = (bf16[64,1024]{1,0:T(8,128)(2,1)S(1)}, bf16[64,1024]{1,0:T(8,128)(2,1)S(1)}, u32[]{:S(2)}, u32[]{:S(2)}) collective-permute-start(bf16[64,1024]{1,0:T(8,128)(2,1)S(1)} %maximum_maximum_fusion), channel_id=1, source_target_pairs={{0,6},{2,0},{4,2},{6,4},{1,7},{3,1},{5,3},{7,5},{8,14},{10,8},{12,... | collective-permute-start | bytes 393224 | tf_op jit(solution)/shard_map/ppermute | solution.py:277
  7.7 1.0 collective-permute-start.3
  8.7 1.1 %convert_element_type.15 = bf16[1,1024,128]{2,1,0:T(8,128)(2,1)S(1)} convert(s32[1,1024,128]{2,1,0:T(8,128)} %param.9) | non-fusion elementwise | flops 131072 | bytes 786432 | tf_op jit(solution)/shard_map/convert_element_type | solution.py:286
  9.9 0.1 copy.10
  10.0 2.9 %collective-permute-start.16 = (bf16[128,512]{1,0:T(8,128)(2,1)S(1)}, bf16[128,512]{1,0:T(8,128)(2,1)S(1)}, u32[]{:S(2)}, u32[]{:S(2)}) collective-permute-start(bf16[128,512]{1,0:T(8,128)(2,1)S(1)} %bitcast.123), channel_id=1, source_target_pairs={{0,6},{2,0},{4,2},{6,4},{1,7},{3,1},{5,3},{7,5},{8,14},{10,8},{12,... | collective-permute-start | bytes 393224 | tf_op jit(solution)/shard_map/ppermute | solution.py:292
  12.9 1.1 %collective-permute-start.15 = (bf16[128,512]{1,0:T(8,128)(2,1)S(1)}, bf16[128,512]{1,0:T(8,128)(2,1)S(1)}, u32[]{:S(2)}, u32[]{:S(2)}) collective-permute-start(bf16[128,512]{1,0:T(8,128)(2,1)S(1)} %bitcast.124), channel_id=1, source_target_pairs={{0,4},{2,6},{4,0},{6,2},{1,5},{3,7},{5,1},{7,3},{8,12},{10,14},{12... | collective-permute-start | bytes 393224 | tf_op jit(solution)/shard_map/ppermute | solution.py:292
  14.0 0.1 stack.236
  14.1 0.1 stack.257
  14.5 6.1 %collective-permute-done.4 = bf16[64,1024]{1,0:T(8,128)(2,1)S(1)} collective-permute-done((bf16[64,1024]{1,0:T(8,128)(2,1)S(1)}, bf16[64,1024]{1,0:T(8,128)(2,1)S(1)}, u32[]{:S(2)}, u32[]{:S(2)}) %collective-permute-start.4) | collective-permute-done | bytes 131104 | tf_op jit(solution)/shard_map/ppermute | solution.py:277
  20.5 1.0 collective-permute-start.2
  21.6 1.6 %collective-permute-start.13 = (bf16[96,1024]{1,0:T(8,128)(2,1)S(1)}, bf16[96,1024]{1,0:T(8,128)(2,1)S(1)}, u32[]{:S(2)}, u32[]{:S(2)}) collective-permute-start(bf16[96,1024]{1,0:T(8,128)(2,1)S(1)} %pad_maximum_fusion.1), channel_id=1, source_target_pairs={{0,1},{1,0},{2,3},{3,2},{4,5},{5,4},{6,7},{7,6},{8,9},{9,8},{10,11... | collective-permute-start | bytes 589832 | tf_op jit(solution)/shard_map/ppermute | solution.py:282
  23.3 0.1 add.451.frow_ref
  23.4 0.1 copy.14.wt_ref
  23.6 0.1 copy.13.pos_ref
  23.7 0.1 copy.11
  23.8 0.1 stack.271.place_ref
  24.1 9.2 %collective-permute-start.1 = (bf16[128,1024]{1,0:T(8,128)(2,1)S(1)}, bf16[128,1024]{1,0:T(8,128)(2,1)S(1)}, u32[]{:S(2)}, u32[]{:S(2)}) collective-permute-start(bf16[128,1024]{1,0:T(8,128)(2,1)S(1)} %bitcast.129), channel_id=1, source_target_pairs={{0,4},{2,6},{4,0},{6,2},{1,5},{3,7},{5,1},{7,3},{8,12},{10,14},{12... | collective-permute-start | bytes 786440 | tf_op jit(solution)/shard_map/ppermute | solution.py:300
  33.2 8.9 %collective-permute-done.15.refs_1_ = bf16[128,512]{1,0:T(8,128)(2,1)S(1)} collective-permute-done((bf16[128,512]{1,0:T(8,128)(2,1)S(1)}, bf16[128,512]{1,0:T(8,128)(2,1)S(1)}, u32[]{:S(2)}, u32[]{:S(2)}) %collective-permute-start.15) | collective-permute-done | bytes 131104 | tf_op jit(solution)/shard_map/ppermute | solution.py:292
  42.1 1.5 %collective-permute-start.19 = (bf16[128,512]{1,0:T(8,128)(2,1)S(1)}, bf16[128,512]{1,0:T(8,128)(2,1)S(1)}, u32[]{:S(2)}, u32[]{:S(2)}) collective-permute-start(bf16[128,512]{1,0:T(8,128)(2,1)S(1)} %collective-permute-done.16.refs_2_), channel_id=1, source_target_pairs={{0,1},{1,0},{2,3},{3,2},{4,5},{5,4},{6,7},{7,6},{8,9},{9,8},{10,11... | collective-permute-start | bytes 393224 | tf_op jit(solution)/shard_map/ppermute | solution.py:296
  43.6 0.5 collective-permute-start.18
  44.1 1.5 %collective-permute-start.17 = (bf16[128,512]{1,0:T(8,128)(2,1)S(1)}, bf16[128,512]{1,0:T(8,128)(2,1)S(1)}, u32[]{:S(2)}, u32[]{:S(2)}) collective-permute-start(bf16[128,512]{1,0:T(8,128)(2,1)S(1)} %collective-permute-done.14.refs_0_), channel_id=1, source_target_pairs={{0,1},{1,0},{2,3},{3,2},{4,5},{5,4},{6,7},{7,6},{8,9},{9,8},{10,11... | collective-permute-start | bytes 393224 | tf_op jit(solution)/shard_map/ppermute | solution.py:296
  45.6 3.8 %shard_map.77 = (bf16[2,1024,512]{2,1,0:T(8,128)(2,1)S(1)}, s32[2,2,16,512]{3,2,1,0:T(8,128)S(1)}) custom-call(s32[8]{0:T(128)S(1)} %stack.271.place_ref, s32[2]{0:T(128)S(1)} %pad_add_fusion.1.blocks_ref, bf16[128,512]{1,0:T(8,128)(2,1)S(1)} %bitcast.126, bf16[128,512]{1,0:T(8,128)(2,1)S(1)} %bitcast.127, ...), custom_call_target="tpu_custom_call" | custom-call | flops 2000000000 | bytes 4000000 | tf_op jit(solution)/shard_map/pallas_call | solution.py:85
  49.5 1.6 %collective-permute-start.8 = (bf16[4,32,1024]{2,1,0:T(8,128)(2,1)S(1)}, bf16[4,32,1024]{2,1,0:T(8,128)(2,1)S(1)}, u32[]{:S(2)}, u32[]{:S(2)}) collective-permute-start(bf16[4,32,1024]{2,1,0:T(8,128)(2,1)S(1)} %pad_maximum_fusion.refs_4_), channel_id=1, source_target_pairs={{0,17},{1,16},{8,25},{9,24},{16,1},{17,0},{24,9},{25,8},{2,19},{3,... | collective-permute-start | bytes 786440 | tf_op jit(solution)/shard_map/ppermute | solution.py:310
  51.0 0.2 collective-permute-done.18.refs_1_
  51.3 1.5 %collective-permute-start.7 = (bf16[4,32,1024]{2,1,0:T(8,128)(2,1)S(1)}, bf16[4,32,1024]{2,1,0:T(8,128)(2,1)S(1)}, u32[]{:S(2)}, u32[]{:S(2)}) collective-permute-start(bf16[4,32,1024]{2,1,0:T(8,128)(2,1)S(1)} %pad_maximum_fusion.refs_4_), channel_id=1, source_target_pairs={{0,16},{1,17},{8,24},{9,25},{16,0},{17,1},{24,8},{25,9},{2,18},{3,... | collective-permute-start | bytes 786440 | tf_op jit(solution)/shard_map/ppermute | solution.py:310
  52.8 1.3 %collective-permute-done.17.refs_0_ = bf16[128,512]{1,0:T(8,128)(2,1)S(1)} collective-permute-done((bf16[128,512]{1,0:T(8,128)(2,1)S(1)}, bf16[128,512]{1,0:T(8,128)(2,1)S(1)}, u32[]{:S(2)}, u32[]{:S(2)}) %collective-permute-start.17) | collective-permute-done | bytes 131104 | tf_op jit(solution)/shard_map/ppermute | solution.py:296
  54.1 1.5 %collective-permute-start.6 = (bf16[4,32,1024]{2,1,0:T(8,128)(2,1)S(1)}, bf16[4,32,1024]{2,1,0:T(8,128)(2,1)S(1)}, u32[]{:S(2)}, u32[]{:S(2)}) collective-permute-start(bf16[4,32,1024]{2,1,0:T(8,128)(2,1)S(1)} %pad_maximum_fusion.refs_4_), channel_id=1, source_target_pairs={{0,1},{1,0},{8,9},{9,8},{16,17},{17,16},{24,25},{25,24},{2,3},{3,2... | collective-permute-start | bytes 786440 | tf_op jit(solution)/shard_map/ppermute | solution.py:310
  55.6 5.4 %shard_map.78 = (bf16[3,1024,512]{2,1,0:T(8,128)(2,1)S(1)}, s32[3,2,16,512]{3,2,1,0:T(8,128)S(1)}) custom-call(s32[8]{0:T(128)S(1)} %stack.271.place_ref, s32[2]{0:T(128)S(1)} %pad_add_fusion.1.blocks_ref, bf16[128,512]{1,0:T(8,128)(2,1)S(1)} %collective-permute-done.14.refs_0_, bf16[128,512]{1,0:T(8,128)(2,1)S(1)} %collective-permute-done.15.refs_1_, ...), custom_call_target="tpu_custom_call" | custom-call | flops 3000000000 | bytes 6000000 | tf_op jit(solution)/shard_map/pallas_call | solution.py:85
  61.2 0.5 collective-permute-start.12
  61.7 0.1 collective-permute-start.11
  61.8 0.4 collective-permute-start.10
  62.2 5.4 %shard_map.79 = (bf16[3,1024,512]{2,1,0:T(8,128)(2,1)S(1)}, s32[3,2,16,512]{3,2,1,0:T(8,128)S(1)}) custom-call(s32[8]{0:T(128)S(1)} %stack.271.place_ref, s32[2]{0:T(128)S(1)} %pad_add_fusion.1.blocks_ref, bf16[128,512]{1,0:T(8,128)(2,1)S(1)} %collective-permute-done.17.refs_0_, bf16[128,512]{1,0:T(8,128)(2,1)S(1)} %collective-permute-done.18.refs_1_, ...), custom_call_target="tpu_custom_call" | custom-call | flops 3000000000 | bytes 6000000 | tf_op jit(solution)/shard_map/pallas_call | solution.py:85
  67.7 17.9 %shard_map.80 = (f32[128,1024]{1,0:T(8,128)S(1)}, f32[128,1024]{1,0:T(8,128)S(1)}, f32[128,4096]{1,0:T(8,128)S(1)}, f32[128,4096]{1,0:T(8,128)S(1)}) custom-call(s32[32]{0:T(128)S(1)} %broadcast_multiply_fusion.woff_ref, s32[8]{0:T(128)S(1)} %stack.245.tbase_ref, s32[2]{0:T(128)S(1)} %pad_add_fusion.1.blocks_ref, s32[256,1]{1,0:T(8,128)S(1)} %add.451.frow_ref, ...), custom_call_target="tpu_custom_call" | custom-call | flops 20000000000 | bytes 20000000 | tf_op jit(solution)/shard_map/pallas_call | solution.py:177
  85.6 0.2 collective-permute-start.20
  85.7 2.8 %shard_map.81 = f32[16,8,256]{2,1,0:T(8,128)S(1)} custom-call(f32[128,4096]{1,0:T(8,128)S(1)} %get-tuple-element.17.grads_ref, s32[2,2,16,512]{3,2,1,0:T(8,128)S(1)} %get-tuple-element.18.refs_0_, s32[3,2,16,512]{3,2,1,0:T(8,128)S(1)} %get-tuple-element.19.refs_1_, s32[3,2,16,512]{3,2,1,0:T(8,128)S(1)} %get-tuple-element.20.refs_2_), custom_call_target="tpu_custom_call" | custom-call | flops 3000000000 | bytes 4000000 | tf_op jit(solution)/shard_map/pallas_call | solution.py:244
  88.5 0.6 collective-permute-start.24
  89.1 2.8 %shard_map.82 = f32[16,8,256]{2,1,0:T(8,128)S(1)} custom-call(f32[128,4096]{1,0:T(8,128)S(1)} %get-tuple-element.21.grads_ref, s32[2,2,16,512]{3,2,1,0:T(8,128)S(1)} %get-tuple-element.18.refs_0_, s32[3,2,16,512]{3,2,1,0:T(8,128)S(1)} %get-tuple-element.19.refs_1_, s32[3,2,16,512]{3,2,1,0:T(8,128)S(1)} %get-tuple-element.20.refs_2_), custom_call_target="tpu_custom_call" | custom-call | flops 3000000000 | bytes 4000000 | tf_op jit(solution)/shard_map/pallas_call | solution.py:244
  91.9 0.1 add.446
  92.0 1.6 %collective-permute-start.21 = (f32[32,1024]{1,0:T(8,128)S(1)}, f32[32,1024]{1,0:T(8,128)S(1)}, u32[]{:S(2)}, u32[]{:S(2)}) collective-permute-start(f32[32,1024]{1,0:T(8,128)S(1)} %get-tuple-element.22), channel_id=1, source_target_pairs={{0,1},{1,0},{2,3},{3,2},{4,5},{5,4},{6,7},{7,6},{8,9},{9,8},{10,11... | collective-permute-start | bytes 393224 | tf_op jit(solution)/shard_map/ppermute | solution.py:390
  93.6 1.5 %collective-permute-start.23 = (f32[32,1024]{1,0:T(8,128)S(1)}, f32[32,1024]{1,0:T(8,128)S(1)}, u32[]{:S(2)}, u32[]{:S(2)}) collective-permute-start(f32[32,1024]{1,0:T(8,128)S(1)} %get-tuple-element.23), channel_id=1, source_target_pairs={{0,17},{1,16},{2,19},{3,18},{4,21},{5,20},{6,23},{7,22},{8,25},{9,... | collective-permute-start | bytes 393224 | tf_op jit(solution)/shard_map/ppermute | solution.py:390
  95.1 0.5 collective-permute-start.22
  95.6 0.7 add_bitcast_fusion
  96.3 2.2 %collective-permute-done.21 = f32[32,1024]{1,0:T(8,128)S(1)} collective-permute-done((f32[32,1024]{1,0:T(8,128)S(1)}, f32[32,1024]{1,0:T(8,128)S(1)}, u32[]{:S(2)}, u32[]{:S(2)}) %collective-permute-start.21) | collective-permute-done | bytes 131104 | tf_op jit(solution)/shard_map/ppermute | solution.py:390
  98.5 3.0 %collective-permute-done.23 = f32[32,1024]{1,0:T(8,128)S(1)} collective-permute-done((f32[32,1024]{1,0:T(8,128)S(1)}, f32[32,1024]{1,0:T(8,128)S(1)}, u32[]{:S(2)}, u32[]{:S(2)}) %collective-permute-start.23) | collective-permute-done | bytes 131104 | tf_op jit(solution)/shard_map/ppermute | solution.py:390
  101.5 1.4 %collective-permute-done.22 = f32[32,1024]{1,0:T(8,128)S(1)} collective-permute-done((f32[32,1024]{1,0:T(8,128)S(1)}, f32[32,1024]{1,0:T(8,128)S(1)}, u32[]{:S(2)}, u32[]{:S(2)}) %collective-permute-start.22) | collective-permute-done | bytes 131104 | tf_op jit(solution)/shard_map/ppermute | solution.py:390
  102.9 0.7 fusion.2
  (49 shorter events, 0.8 us)
Async XLA Ops:
  0.6 13.6 %copy-start.2 = (bf16[1,1024]{1,0:T(2,128)(2,1)S(1)}, bf16[1,1024]{1,0:T(2,128)(2,1)}, u32[]{:S(2)}) copy-start(bf16[1,1024]{1,0:T(2,128)(2,1)} %param.11) | copy-start | bytes 6148
  0.6 13.6 %copy-start.3 = (s32[1,1024]{1,0:T(1,128)S(1)}, s32[1,1024]{1,0:T(1,128)}, u32[]{:S(2)}) copy-start(s32[1,1024]{1,0:T(1,128)} %param.10) | copy-start | bytes 12292
  0.7 19.9 %copy-start = (bf16[1,128,1024]{2,1,0:T(8,128)(2,1)S(1)}, bf16[1,128,1024]{2,1,0:T(8,128)(2,1)}, u32[]{:S(2)}) copy-start(bf16[1,128,1024]{2,1,0:T(8,128)(2,1)} %param.6) | copy-start | bytes 786436
  2.6 11.8 %collective-permute-start.5 = (bf16[64,1024]{1,0:T(8,128)(2,1)S(1)}, bf16[64,1024]{1,0:T(8,128)(2,1)S(1)}, u32[]{:S(2)}, u32[]{:S(2)}) collective-permute-start(bf16[64,1024]{1,0:T(8,128)(2,1)S(1)} %maximum_maximum_fusion), channel_id=1, source_target_pairs={{0,6},{2,0},{4,2},{6,4},{1,7},{3,1},{5,3},{7,5},{8,14},{10,8},{12,... | collective-permute-start | bytes 393224 | tf_op jit(solution)/shard_map/ppermute | solution.py:277
  7.7 12.8 %collective-permute-start.4 = (bf16[64,1024]{1,0:T(8,128)(2,1)S(1)}, bf16[64,1024]{1,0:T(8,128)(2,1)S(1)}, u32[]{:S(2)}, u32[]{:S(2)}) collective-permute-start(bf16[64,1024]{1,0:T(8,128)(2,1)S(1)} %maximum_maximum_fusion), channel_id=1, source_target_pairs={{0,4},{2,6},{4,0},{6,2},{1,5},{3,7},{5,1},{7,3},{8,12},{10,14},{12... | collective-permute-start | bytes 393224 | tf_op jit(solution)/shard_map/ppermute | solution.py:277
  7.7 13.9 %collective-permute-start.3 = (bf16[64,1024]{1,0:T(8,128)(2,1)S(1)}, bf16[64,1024]{1,0:T(8,128)(2,1)S(1)}, u32[]{:S(2)}, u32[]{:S(2)}) collective-permute-start(bf16[64,1024]{1,0:T(8,128)(2,1)S(1)} %maximum_maximum_fusion), channel_id=1, source_target_pairs={{0,2},{2,4},{4,6},{6,0},{1,3},{3,5},{5,7},{7,1},{8,10},{10,12},{12... | collective-permute-start | bytes 393224 | tf_op jit(solution)/shard_map/ppermute | solution.py:277
  8.7 15.3 %copy-start.1 = (bf16[32,1024]{1,0:T(8,128)(2,1)S(1)}, bf16[32,1024]{1,0:T(8,128)(2,1)}, u32[]{:S(2)}) copy-start(bf16[32,1024]{1,0:T(8,128)(2,1)} %param.7) | copy-start | bytes 196612
  10.0 14.1 %collective-permute-start.16 = (bf16[128,512]{1,0:T(8,128)(2,1)S(1)}, bf16[128,512]{1,0:T(8,128)(2,1)S(1)}, u32[]{:S(2)}, u32[]{:S(2)}) collective-permute-start(bf16[128,512]{1,0:T(8,128)(2,1)S(1)} %bitcast.123), channel_id=1, source_target_pairs={{0,6},{2,0},{4,2},{6,4},{1,7},{3,1},{5,3},{7,5},{8,14},{10,8},{12,... | collective-permute-start | bytes 393224 | tf_op jit(solution)/shard_map/ppermute | solution.py:292
  12.9 29.2 %collective-permute-start.15 = (bf16[128,512]{1,0:T(8,128)(2,1)S(1)}, bf16[128,512]{1,0:T(8,128)(2,1)S(1)}, u32[]{:S(2)}, u32[]{:S(2)}) collective-permute-start(bf16[128,512]{1,0:T(8,128)(2,1)S(1)} %bitcast.124), channel_id=1, source_target_pairs={{0,4},{2,6},{4,0},{6,2},{1,5},{3,7},{5,1},{7,3},{8,12},{10,14},{12... | collective-permute-start | bytes 393224 | tf_op jit(solution)/shard_map/ppermute | solution.py:292
  14.4 29.2 %collective-permute-start.14 = (bf16[128,512]{1,0:T(8,128)(2,1)S(1)}, bf16[128,512]{1,0:T(8,128)(2,1)S(1)}, u32[]{:S(2)}, u32[]{:S(2)}) collective-permute-start(bf16[128,512]{1,0:T(8,128)(2,1)S(1)} %bitcast.125), channel_id=1, source_target_pairs={{0,2},{2,4},{4,6},{6,0},{1,3},{3,5},{5,7},{7,1},{8,10},{10,12},{12... | collective-permute-start | bytes 393224 | tf_op jit(solution)/shard_map/ppermute | solution.py:292
  20.5 40.5 %collective-permute-start.2 = (bf16[128,1024]{1,0:T(8,128)(2,1)S(1)}, bf16[128,1024]{1,0:T(8,128)(2,1)S(1)}, u32[]{:S(2)}, u32[]{:S(2)}) collective-permute-start(bf16[128,1024]{1,0:T(8,128)(2,1)S(1)} %bitcast.128), channel_id=1, source_target_pairs={{0,6},{2,4},{4,2},{6,0},{1,7},{3,5},{5,3},{7,1},{8,14},{10,12},{12... | collective-permute-start | bytes 786440 | tf_op jit(solution)/shard_map/ppermute | solution.py:300
  21.6 22.5 %collective-permute-start.13 = (bf16[96,1024]{1,0:T(8,128)(2,1)S(1)}, bf16[96,1024]{1,0:T(8,128)(2,1)S(1)}, u32[]{:S(2)}, u32[]{:S(2)}) collective-permute-start(bf16[96,1024]{1,0:T(8,128)(2,1)S(1)} %pad_maximum_fusion.1), channel_id=1, source_target_pairs={{0,1},{1,0},{2,3},{3,2},{4,5},{5,4},{6,7},{7,6},{8,9},{9,8},{10,11... | collective-permute-start | bytes 589832 | tf_op jit(solution)/shard_map/ppermute | solution.py:282
  24.1 37.0 %collective-permute-start.1 = (bf16[128,1024]{1,0:T(8,128)(2,1)S(1)}, bf16[128,1024]{1,0:T(8,128)(2,1)S(1)}, u32[]{:S(2)}, u32[]{:S(2)}) collective-permute-start(bf16[128,1024]{1,0:T(8,128)(2,1)S(1)} %bitcast.129), channel_id=1, source_target_pairs={{0,4},{2,6},{4,0},{6,2},{1,5},{3,7},{5,1},{7,3},{8,12},{10,14},{12... | collective-permute-start | bytes 786440 | tf_op jit(solution)/shard_map/ppermute | solution.py:300
  42.1 7.4 %collective-permute-start.19 = (bf16[128,512]{1,0:T(8,128)(2,1)S(1)}, bf16[128,512]{1,0:T(8,128)(2,1)S(1)}, u32[]{:S(2)}, u32[]{:S(2)}) collective-permute-start(bf16[128,512]{1,0:T(8,128)(2,1)S(1)} %collective-permute-done.16.refs_2_), channel_id=1, source_target_pairs={{0,1},{1,0},{2,3},{3,2},{4,5},{5,4},{6,7},{7,6},{8,9},{9,8},{10,11... | collective-permute-start | bytes 393224 | tf_op jit(solution)/shard_map/ppermute | solution.py:296
  43.6 7.7 %collective-permute-start.18 = (bf16[128,512]{1,0:T(8,128)(2,1)S(1)}, bf16[128,512]{1,0:T(8,128)(2,1)S(1)}, u32[]{:S(2)}, u32[]{:S(2)}) collective-permute-start(bf16[128,512]{1,0:T(8,128)(2,1)S(1)} %collective-permute-done.15.refs_1_), channel_id=1, source_target_pairs={{0,1},{1,0},{2,3},{3,2},{4,5},{5,4},{6,7},{7,6},{8,9},{9,8},{10,11... | collective-permute-start | bytes 393224 | tf_op jit(solution)/shard_map/ppermute | solution.py:296
  44.1 10.0 %collective-permute-start.17 = (bf16[128,512]{1,0:T(8,128)(2,1)S(1)}, bf16[128,512]{1,0:T(8,128)(2,1)S(1)}, u32[]{:S(2)}, u32[]{:S(2)}) collective-permute-start(bf16[128,512]{1,0:T(8,128)(2,1)S(1)} %collective-permute-done.14.refs_0_), channel_id=1, source_target_pairs={{0,1},{1,0},{2,3},{3,2},{4,5},{5,4},{6,7},{7,6},{8,9},{9,8},{10,11... | collective-permute-start | bytes 393224 | tf_op jit(solution)/shard_map/ppermute | solution.py:296
  49.5 11.7 %collective-permute-start.8 = (bf16[4,32,1024]{2,1,0:T(8,128)(2,1)S(1)}, bf16[4,32,1024]{2,1,0:T(8,128)(2,1)S(1)}, u32[]{:S(2)}, u32[]{:S(2)}) collective-permute-start(bf16[4,32,1024]{2,1,0:T(8,128)(2,1)S(1)} %pad_maximum_fusion.refs_4_), channel_id=1, source_target_pairs={{0,17},{1,16},{8,25},{9,24},{16,1},{17,0},{24,9},{25,8},{2,19},{3,... | collective-permute-start | bytes 786440 | tf_op jit(solution)/shard_map/ppermute | solution.py:310
  51.3 10.4 %collective-permute-start.7 = (bf16[4,32,1024]{2,1,0:T(8,128)(2,1)S(1)}, bf16[4,32,1024]{2,1,0:T(8,128)(2,1)S(1)}, u32[]{:S(2)}, u32[]{:S(2)}) collective-permute-start(bf16[4,32,1024]{2,1,0:T(8,128)(2,1)S(1)} %pad_maximum_fusion.refs_4_), channel_id=1, source_target_pairs={{0,16},{1,17},{8,24},{9,25},{16,0},{17,1},{24,8},{25,9},{2,18},{3,... | collective-permute-start | bytes 786440 | tf_op jit(solution)/shard_map/ppermute | solution.py:310
  54.1 7.7 %collective-permute-start.6 = (bf16[4,32,1024]{2,1,0:T(8,128)(2,1)S(1)}, bf16[4,32,1024]{2,1,0:T(8,128)(2,1)S(1)}, u32[]{:S(2)}, u32[]{:S(2)}) collective-permute-start(bf16[4,32,1024]{2,1,0:T(8,128)(2,1)S(1)} %pad_maximum_fusion.refs_4_), channel_id=1, source_target_pairs={{0,1},{1,0},{8,9},{9,8},{16,17},{17,16},{24,25},{25,24},{2,3},{3,2... | collective-permute-start | bytes 786440 | tf_op jit(solution)/shard_map/ppermute | solution.py:310
  61.0 6.6 %collective-permute-start = (bf16[128,1024]{1,0:T(8,128)(2,1)S(1)}, bf16[128,1024]{1,0:T(8,128)(2,1)S(1)}, u32[]{:S(2)}, u32[]{:S(2)}) collective-permute-start(bf16[128,1024]{1,0:T(8,128)(2,1)S(1)} %bitcast.130), channel_id=1, source_target_pairs={{0,2},{2,0},{4,6},{6,4},{1,3},{3,1},{5,7},{7,5},{8,10},{10,8},{12,... | collective-permute-start | bytes 786440 | tf_op jit(solution)/shard_map/ppermute | solution.py:300
  61.1 6.6 %collective-permute-start.9 = (bf16[4,32,1024]{2,1,0:T(8,128)(2,1)S(1)}, bf16[4,32,1024]{2,1,0:T(8,128)(2,1)S(1)}, u32[]{:S(2)}, u32[]{:S(2)}) collective-permute-start(bf16[4,32,1024]{2,1,0:T(8,128)(2,1)S(1)} %pad_maximum_fusion.refs_4_), channel_id=1, source_target_pairs={{0,8},{8,0},{16,24},{24,16},{1,9},{9,1},{17,25},{25,17},{2,10},{10... | collective-permute-start | bytes 786440 | tf_op jit(solution)/shard_map/ppermute | solution.py:311
  61.2 6.5 %collective-permute-start.12 = (bf16[4,32,1024]{2,1,0:T(8,128)(2,1)S(1)}, bf16[4,32,1024]{2,1,0:T(8,128)(2,1)S(1)}, u32[]{:S(2)}, u32[]{:S(2)}) collective-permute-start(bf16[4,32,1024]{2,1,0:T(8,128)(2,1)S(1)} %collective-permute-done.8.refs_7_), channel_id=1, source_target_pairs={{0,8},{8,0},{16,24},{24,16},{1,9},{9,1},{17,25},{25,17},{2,10},{10... | collective-permute-start | bytes 786440 | tf_op jit(solution)/shard_map/ppermute | solution.py:311
  61.7 6.0 %collective-permute-start.11 = (bf16[4,32,1024]{2,1,0:T(8,128)(2,1)S(1)}, bf16[4,32,1024]{2,1,0:T(8,128)(2,1)S(1)}, u32[]{:S(2)}, u32[]{:S(2)}) collective-permute-start(bf16[4,32,1024]{2,1,0:T(8,128)(2,1)S(1)} %collective-permute-done.7.refs_6_), channel_id=1, source_target_pairs={{0,8},{8,0},{16,24},{24,16},{1,9},{9,1},{17,25},{25,17},{2,10},{10... | collective-permute-start | bytes 786440 | tf_op jit(solution)/shard_map/ppermute | solution.py:311
  61.8 5.9 %collective-permute-start.10 = (bf16[4,32,1024]{2,1,0:T(8,128)(2,1)S(1)}, bf16[4,32,1024]{2,1,0:T(8,128)(2,1)S(1)}, u32[]{:S(2)}, u32[]{:S(2)}) collective-permute-start(bf16[4,32,1024]{2,1,0:T(8,128)(2,1)S(1)} %collective-permute-done.6.refs_5_), channel_id=1, source_target_pairs={{0,8},{8,0},{16,24},{24,16},{1,9},{9,1},{17,25},{25,17},{2,10},{10... | collective-permute-start | bytes 786440 | tf_op jit(solution)/shard_map/ppermute | solution.py:311
  85.6 6.3 %collective-permute-start.20 = (f32[128,1024]{1,0:T(8,128)S(1)}, f32[128,1024]{1,0:T(8,128)S(1)}, u32[]{:S(2)}, u32[]{:S(2)}) collective-permute-start(f32[128,1024]{1,0:T(8,128)S(1)} %get-tuple-element.16), channel_id=1, source_target_pairs={{0,8},{8,0},{16,24},{24,16},{1,9},{9,1},{17,25},{25,17},{2,10},{10... | collective-permute-start | bytes 1572872 | tf_op jit(solution)/shard_map/ppermute | solution.py:365
  88.5 7.1 %collective-permute-start.24 = (f32[16,8,256]{2,1,0:T(8,128)S(1)}, f32[16,8,256]{2,1,0:T(8,128)S(1)}, u32[]{:S(2)}, u32[]{:S(2)}) collective-permute-start(f32[16,8,256]{2,1,0:T(8,128)S(1)} %shard_map.81), channel_id=1, source_target_pairs={{0,1},{1,0},{2,3},{3,2},{4,5},{5,4},{6,7},{7,6},{8,9},{9,8},{10,11... | collective-permute-start | bytes 393224 | tf_op jit(solution)/shard_map/ppermute | solution.py:377
  92.0 6.4 %collective-permute-start.21 = (f32[32,1024]{1,0:T(8,128)S(1)}, f32[32,1024]{1,0:T(8,128)S(1)}, u32[]{:S(2)}, u32[]{:S(2)}) collective-permute-start(f32[32,1024]{1,0:T(8,128)S(1)} %get-tuple-element.22), channel_id=1, source_target_pairs={{0,1},{1,0},{2,3},{3,2},{4,5},{5,4},{6,7},{7,6},{8,9},{9,8},{10,11... | collective-permute-start | bytes 393224 | tf_op jit(solution)/shard_map/ppermute | solution.py:390
  93.6 7.9 %collective-permute-start.23 = (f32[32,1024]{1,0:T(8,128)S(1)}, f32[32,1024]{1,0:T(8,128)S(1)}, u32[]{:S(2)}, u32[]{:S(2)}) collective-permute-start(f32[32,1024]{1,0:T(8,128)S(1)} %get-tuple-element.23), channel_id=1, source_target_pairs={{0,17},{1,16},{2,19},{3,18},{4,21},{5,20},{6,23},{7,22},{8,25},{9,... | collective-permute-start | bytes 393224 | tf_op jit(solution)/shard_map/ppermute | solution.py:390
  95.1 7.8 %collective-permute-start.22 = (f32[32,1024]{1,0:T(8,128)S(1)}, f32[32,1024]{1,0:T(8,128)S(1)}, u32[]{:S(2)}, u32[]{:S(2)}) collective-permute-start(f32[32,1024]{1,0:T(8,128)S(1)} %get-tuple-element.24), channel_id=1, source_target_pairs={{0,16},{1,17},{2,18},{3,19},{4,20},{5,21},{6,22},{7,23},{8,24},{9,... | collective-permute-start | bytes 393224 | tf_op jit(solution)/shard_map/ppermute | solution.py:390

commit v4 on v3

--- a/solution.py
+++ b/solution.py
@@ -24,6 +24,10 @@
 
 def flip(n, k):
     return [(i, i ^ k) for i in range(n)]
+
+
+def relay(n):
+    return list(range(1, n // 2 + 1)) + list(range(n - 1, n // 2, -1))
 
 
 def cost(flops, bytes_accessed):
@@ -288,8 +292,10 @@
     width = pass_rows // n_dp
     share = [lax.dynamic_slice_in_dim(codes_t, lanes[t] * width, width, 1) for t in range(n_dp)]
     tiles = {(0, 0): share[0]}
-    for k in range(1, n_sh):
-        tiles[0, k] = move(share[0], "shard", ring(n_sh, k))
+    for k in relay(n_sh):
+        step = 1 if 2 * k <= n_sh else n_sh - 1
+        source = tiles[0, (k - step) % n_sh]
+        tiles[0, k] = move(source, "shard", ring(n_sh, step))
     for t in range(1, n_dp):
         tiles[t, 0] = share[t]
         for k in range(1, n_sh):
@@ -297,8 +303,13 @@
 
     q = queries_in[0]
     own = q.shape[0]
-    q_pieces = [q] + [move(q, "shard", flip(n_sh, a)) for a in range(1, group)]
-    q_from = [(z ^ a) * n_dp + x for a in range(group)]
+    q_held = {0: q}
+    for k in relay(group):
+        step = 1 if 2 * k <= group else group - 1
+        pairs = [(s, s // group * group + (s + step) % group) for s in range(n_sh)]
+        q_held[k] = move(q_held[(k - step) % group], "shard", pairs)
+    q_pieces = [q_held[k] for k in range(group)]
+    q_from = [(zp * group + lax.rem(zi - k + group, group)) * n_dp + x for k in range(group)]
 
     w_pieces, w_places = [], []
     for e in evens:

time: 104 us -> 100 us (0.962)
  waiting for transfers between devices: 23.1 us -> 17 us
  starting transfers between devices: 35.4 us -> 37.9 us
    ppermute x6, waiting for transfers between devices: 8.89 us -> 1.58 us  [the longest x3 0.79 us: compute(): tiles[0, k] = move(source, 'shard', ring(n_sh, step))]
    ppermute x6, starting transfers between devices: 14.3 us -> 17.9 us  [the longest x3 10.8 us: compute(): tiles[0, k] = move(source, 'shard', ring(n_sh, step))]
    ppermute x3, waiting for transfers between devices: 1.53 us -> 4.93 us  [compute(): tiles[t, k] = move(tiles[0, k], 'dp', ring(n_dp, t))]
    ppermute x3, waiting for transfers between devices: 6.06 us -> 3.4 us  [compute(): moved = [move(packet, 'shard', ring(n_sh, k)) for k in range(1, n_sh)]]
  transfers between devices with their start and end apart: 25 -> 25, of which waited for: 7 -> 8; matrix products, arithmetic and copies ran while one was open for 3% -> 3% of each run, Pallas kernels for 20% -> 20%
where the time goes in v4:
time: 100 us; the launch traced here: 99.9 us
  Pallas kernels  38.2 us (38%)
  starting transfers between devices  37.9 us (38%)
  waiting for transfers between devices  17 us (17%)
  other arithmetic  4.59 us (5%)
  local copies, waits for them, and re-layouts  1.21 us (1%)
    pallas_call x1, Pallas kernels, main(): pl.pallas_call(functools.partial(main_kernel, n_q, n_w, n_g), out_shape=(...  17.9 us
    pallas_call x3, Pallas kernels, rebuild(): pl.pallas_call(functools.partial(rebuild_kernel, n_t, n_b), out_shape=(ja...  14.7 us
    ppermute x3, starting transfers between devices, compute(): tiles[0, k] = move(source, 'shard', ring(n_sh, step))  10.8 us
    ppermute x3, waiting for transfers between devices, compute(): moved = move(summed[i, o], ('dom', 'shard', 'dp'), pairs)  7.12 us
    ppermute x3, starting transfers between devices, compute(): q_held[k] = move(q_held[(k - step) % group], 'shard', pairs)  7.05 us
    ppermute x3, starting transfers between devices, compute(): moved = [move(packet, 'shard', ring(n_sh, k)) for k in range(1, n_sh)]  6.14 us
    pallas_call x2, Pallas kernels, word_grads(): pl.pallas_call(functools.partial(words_kernel, words, block), out_shape=j...  5.59 us
    ppermute x3, waiting for transfers between devices, compute(): tiles[t, k] = move(tiles[0, k], 'dp', ring(n_dp, t))  4.93 us
  transfers between devices with their start and end apart: 25, of which 8 were waited for; matrix products, arithmetic and copies ran while one was open for 3% of the time, Pallas kernels for 20%

profile of v4, /device:TPU:0, one launch (start us, length us, event | category | flops | bytes accessed | tf_op | source)
XLA Modules:
  0.0 99.9 jit_solution(7414752528852504343)
XLA Ops:
  0.7 1.0 %convert_element_type.14 = bf16[1,32,8,256]{3,2,1,0:T(8,128)(2,1)S(1)} convert(f32[1,32,8,256]{3,2,1,0:T(8,128)} %param.8) | non-fusion elementwise | flops 65536 | bytes 393216 | tf_op jit(solution)/shard_map/convert_element_type | solution.py:270
  1.7 0.9 maximum_maximum_fusion
  2.6 5.1 %collective-permute-start.5 = (bf16[64,1024]{1,0:T(8,128)(2,1)S(1)}, bf16[64,1024]{1,0:T(8,128)(2,1)S(1)}, u32[]{:S(2)}, u32[]{:S(2)}) collective-permute-start(bf16[64,1024]{1,0:T(8,128)(2,1)S(1)} %maximum_maximum_fusion), channel_id=1, source_target_pairs={{0,6},{2,0},{4,2},{6,4},{1,7},{3,1},{5,3},{7,5},{8,14},{10,8},{12,... | collective-permute-start | bytes 393224 | tf_op jit(solution)/shard_map/ppermute | solution.py:281
  7.7 1.0 %collective-permute-start.3 = (bf16[64,1024]{1,0:T(8,128)(2,1)S(1)}, bf16[64,1024]{1,0:T(8,128)(2,1)S(1)}, u32[]{:S(2)}, u32[]{:S(2)}) collective-permute-start(bf16[64,1024]{1,0:T(8,128)(2,1)S(1)} %maximum_maximum_fusion), channel_id=1, source_target_pairs={{0,2},{2,4},{4,6},{6,0},{1,3},{3,5},{5,7},{7,1},{8,10},{10,12},{12... | collective-permute-start | bytes 393224 | tf_op jit(solution)/shard_map/ppermute | solution.py:281
  8.7 1.1 %convert_element_type.15 = bf16[1,1024,128]{2,1,0:T(8,128)(2,1)S(1)} convert(s32[1,1024,128]{2,1,0:T(8,128)} %param.9) | non-fusion elementwise | flops 131072 | bytes 786432 | tf_op jit(solution)/shard_map/convert_element_type | solution.py:290
  9.9 0.1 copy.10
  10.0 2.9 %collective-permute-start.16 = (bf16[128,512]{1,0:T(8,128)(2,1)S(1)}, bf16[128,512]{1,0:T(8,128)(2,1)S(1)}, u32[]{:S(2)}, u32[]{:S(2)}) collective-permute-start(bf16[128,512]{1,0:T(8,128)(2,1)S(1)} %bitcast.123), channel_id=1, source_target_pairs={{0,6},{2,0},{4,2},{6,4},{1,7},{3,1},{5,3},{7,5},{8,14},{10,8},{12,... | collective-permute-start | bytes 393224 | tf_op jit(solution)/shard_map/ppermute | solution.py:298
  12.8 0.1 stack.236
  13.0 0.1 stack.257
  13.1 0.1 iota_add_fusion
  13.3 3.9 %collective-permute-start.2 = (bf16[128,1024]{1,0:T(8,128)(2,1)S(1)}, bf16[128,1024]{1,0:T(8,128)(2,1)S(1)}, u32[]{:S(2)}, u32[]{:S(2)}) collective-permute-start(bf16[128,1024]{1,0:T(8,128)(2,1)S(1)} %bitcast.127), channel_id=1, source_target_pairs={{0,6},{2,0},{4,2},{6,4},{1,7},{3,1},{5,3},{7,5},{8,14},{10,8},{12,... | collective-permute-start | bytes 786440 | tf_op jit(solution)/shard_map/ppermute | solution.py:310
  17.2 3.4 %collective-permute-done.4 = bf16[64,1024]{1,0:T(8,128)(2,1)S(1)} collective-permute-done((bf16[64,1024]{1,0:T(8,128)(2,1)S(1)}, bf16[64,1024]{1,0:T(8,128)(2,1)S(1)}, u32[]{:S(2)}, u32[]{:S(2)}) %collective-permute-start.4) | collective-permute-done | bytes 131104 | tf_op jit(solution)/shard_map/ppermute | solution.py:281
  20.6 1.6 %collective-permute-start.13 = (bf16[96,1024]{1,0:T(8,128)(2,1)S(1)}, bf16[96,1024]{1,0:T(8,128)(2,1)S(1)}, u32[]{:S(2)}, u32[]{:S(2)}) collective-permute-start(bf16[96,1024]{1,0:T(8,128)(2,1)S(1)} %pad_maximum_fusion.1), channel_id=1, source_target_pairs={{0,1},{1,0},{2,3},{3,2},{4,5},{5,4},{6,7},{7,6},{8,9},{9,8},{10,11... | collective-permute-start | bytes 589832 | tf_op jit(solution)/shard_map/ppermute | solution.py:286
  22.2 0.1 pad_add_fusion.1.blocks_ref
  22.2 0.1 add.492.frow_ref
  22.4 0.1 copy.14.wt_ref
  22.5 0.1 copy.13.pos_ref
  22.7 0.1 copy.11
  22.8 0.1 stack.271.place_ref
  22.9 0.1 stack.245.tbase_ref
  23.0 0.8 collective-permute-done.14.refs_0_
  23.8 1.5 %collective-permute-start.17 = (bf16[128,512]{1,0:T(8,128)(2,1)S(1)}, bf16[128,512]{1,0:T(8,128)(2,1)S(1)}, u32[]{:S(2)}, u32[]{:S(2)}) collective-permute-start(bf16[128,512]{1,0:T(8,128)(2,1)S(1)} %collective-permute-done.14.refs_0_), channel_id=1, source_target_pairs={{0,1},{1,0},{2,3},{3,2},{4,5},{5,4},{6,7},{7,6},{8,9},{9,8},{10,11... | collective-permute-start | bytes 393224 | tf_op jit(solution)/shard_map/ppermute | solution.py:302
  25.3 8.0 %collective-permute-start.15 = (bf16[128,512]{1,0:T(8,128)(2,1)S(1)}, bf16[128,512]{1,0:T(8,128)(2,1)S(1)}, u32[]{:S(2)}, u32[]{:S(2)}) collective-permute-start(bf16[128,512]{1,0:T(8,128)(2,1)S(1)} %collective-permute-done.14.refs_0_), channel_id=1, source_target_pairs={{0,2},{2,4},{4,6},{6,0},{1,3},{3,5},{5,7},{7,1},{8,10},{10,12},{12... | collective-permute-start | bytes 393224 | tf_op jit(solution)/shard_map/ppermute | solution.py:298
  33.3 0.5 collective-permute-start.19
  33.8 4.4 %collective-permute-done.19.refs_2_ = bf16[128,512]{1,0:T(8,128)(2,1)S(1)} collective-permute-done((bf16[128,512]{1,0:T(8,128)(2,1)S(1)}, bf16[128,512]{1,0:T(8,128)(2,1)S(1)}, u32[]{:S(2)}, u32[]{:S(2)}) %collective-permute-start.19) | collective-permute-done | bytes 131104 | tf_op jit(solution)/shard_map/ppermute | solution.py:302
  38.3 2.3 %collective-permute-start.8 = (bf16[4,32,1024]{2,1,0:T(8,128)(2,1)S(1)}, bf16[4,32,1024]{2,1,0:T(8,128)(2,1)S(1)}, u32[]{:S(2)}, u32[]{:S(2)}) collective-permute-start(bf16[4,32,1024]{2,1,0:T(8,128)(2,1)S(1)} %pad_maximum_fusion.refs_4_), channel_id=1, source_target_pairs={{0,17},{1,16},{8,25},{9,24},{16,1},{17,0},{24,9},{25,8},{2,19},{3,... | collective-permute-start | bytes 786440 | tf_op jit(solution)/shard_map/ppermute | solution.py:321
  40.6 1.5 %collective-permute-start.6 = (bf16[4,32,1024]{2,1,0:T(8,128)(2,1)S(1)}, bf16[4,32,1024]{2,1,0:T(8,128)(2,1)S(1)}, u32[]{:S(2)}, u32[]{:S(2)}) collective-permute-start(bf16[4,32,1024]{2,1,0:T(8,128)(2,1)S(1)} %pad_maximum_fusion.refs_4_), channel_id=1, source_target_pairs={{0,1},{1,0},{8,9},{9,8},{16,17},{17,16},{24,25},{25,24},{2,3},{3,2... | collective-permute-start | bytes 786440 | tf_op jit(solution)/shard_map/ppermute | solution.py:321
  42.2 5.4 %shard_map.78 = (bf16[3,1024,512]{2,1,0:T(8,128)(2,1)S(1)}, s32[3,2,16,512]{3,2,1,0:T(8,128)S(1)}) custom-call(s32[8]{0:T(128)S(1)} %stack.271.place_ref, s32[2]{0:T(128)S(1)} %pad_add_fusion.1.blocks_ref, bf16[128,512]{1,0:T(8,128)(2,1)S(1)} %collective-permute-done.14.refs_0_, bf16[128,512]{1,0:T(8,128)(2,1)S(1)} %collective-permute-done.15.refs_1_, ...), custom_call_target="tpu_custom_call" | custom-call | flops 3000000000 | bytes 6000000 | tf_op jit(solution)/shard_map/pallas_call | solution.py:89
  47.6 0.6 collective-permute-start.18
  48.2 3.8 %shard_map.77 = (bf16[2,1024,512]{2,1,0:T(8,128)(2,1)S(1)}, s32[2,2,16,512]{3,2,1,0:T(8,128)S(1)}) custom-call(s32[8]{0:T(128)S(1)} %stack.271.place_ref, s32[2]{0:T(128)S(1)} %pad_add_fusion.1.blocks_ref, bf16[128,512]{1,0:T(8,128)(2,1)S(1)} %bitcast.125, bf16[128,512]{1,0:T(8,128)(2,1)S(1)} %bitcast.126, ...), custom_call_target="tpu_custom_call" | custom-call | flops 2000000000 | bytes 4000000 | tf_op jit(solution)/shard_map/pallas_call | solution.py:89
  52.1 0.1 collective-permute-start.9
  52.1 0.5 collective-permute-done.18.refs_1_
  52.6 3.2 %collective-permute-start.1 = (bf16[128,1024]{1,0:T(8,128)(2,1)S(1)}, bf16[128,1024]{1,0:T(8,128)(2,1)S(1)}, u32[]{:S(2)}, u32[]{:S(2)}) collective-permute-start(bf16[128,1024]{1,0:T(8,128)(2,1)S(1)} %collective-permute-done.refs_1_), channel_id=1, source_target_pairs={{0,2},{2,4},{4,6},{6,0},{1,3},{3,5},{5,7},{7,1},{8,10},{10,12},{12... | collective-permute-start | bytes 786440 | tf_op jit(solution)/shard_map/ppermute | solution.py:310
  55.8 0.5 collective-permute-start.11
  56.4 5.4 %shard_map.79 = (bf16[3,1024,512]{2,1,0:T(8,128)(2,1)S(1)}, s32[3,2,16,512]{3,2,1,0:T(8,128)S(1)}) custom-call(s32[8]{0:T(128)S(1)} %stack.271.place_ref, s32[2]{0:T(128)S(1)} %pad_add_fusion.1.blocks_ref, bf16[128,512]{1,0:T(8,128)(2,1)S(1)} %collective-permute-done.17.refs_0_, bf16[128,512]{1,0:T(8,128)(2,1)S(1)} %collective-permute-done.18.refs_1_, ...), custom_call_target="tpu_custom_call" | custom-call | flops 3000000000 | bytes 6000000 | tf_op jit(solution)/shard_map/pallas_call | solution.py:89
  61.9 0.8 collective-permute-done.1.refs_2_
  62.7 17.9 %shard_map.80 = (f32[128,1024]{1,0:T(8,128)S(1)}, f32[128,1024]{1,0:T(8,128)S(1)}, f32[128,4096]{1,0:T(8,128)S(1)}, f32[128,4096]{1,0:T(8,128)S(1)}) custom-call(s32[32]{0:T(128)S(1)} %broadcast_multiply_fusion.woff_ref, s32[8]{0:T(128)S(1)} %stack.245.tbase_ref, s32[2]{0:T(128)S(1)} %pad_add_fusion.1.blocks_ref, s32[256,1]{1,0:T(8,128)S(1)} %add.492.frow_ref, ...), custom_call_target="tpu_custom_call" | custom-call | flops 20000000000 | bytes 20000000 | tf_op jit(solution)/shard_map/pallas_call | solution.py:181
  80.5 0.1 collective-permute-start.20
  80.6 2.8 %shard_map.81 = f32[16,8,256]{2,1,0:T(8,128)S(1)} custom-call(f32[128,4096]{1,0:T(8,128)S(1)} %get-tuple-element.17.grads_ref, s32[2,2,16,512]{3,2,1,0:T(8,128)S(1)} %get-tuple-element.18.refs_0_, s32[3,2,16,512]{3,2,1,0:T(8,128)S(1)} %get-tuple-element.19.refs_1_, s32[3,2,16,512]{3,2,1,0:T(8,128)S(1)} %get-tuple-element.20.refs_2_), custom_call_target="tpu_custom_call" | custom-call | flops 3000000000 | bytes 4000000 | tf_op jit(solution)/shard_map/pallas_call | solution.py:248
  83.4 1.5 %collective-permute-start.24 = (f32[16,8,256]{2,1,0:T(8,128)S(1)}, f32[16,8,256]{2,1,0:T(8,128)S(1)}, u32[]{:S(2)}, u32[]{:S(2)}) collective-permute-start(f32[16,8,256]{2,1,0:T(8,128)S(1)} %shard_map.81), channel_id=1, source_target_pairs={{0,1},{1,0},{2,3},{3,2},{4,5},{5,4},{6,7},{7,6},{8,9},{9,8},{10,11... | collective-permute-start | bytes 393224 | tf_op jit(solution)/shard_map/ppermute | solution.py:388
  84.9 2.8 %shard_map.82 = f32[16,8,256]{2,1,0:T(8,128)S(1)} custom-call(f32[128,4096]{1,0:T(8,128)S(1)} %get-tuple-element.21.grads_ref, s32[2,2,16,512]{3,2,1,0:T(8,128)S(1)} %get-tuple-element.18.refs_0_, s32[3,2,16,512]{3,2,1,0:T(8,128)S(1)} %get-tuple-element.19.refs_1_, s32[3,2,16,512]{3,2,1,0:T(8,128)S(1)} %get-tuple-element.20.refs_2_), custom_call_target="tpu_custom_call" | custom-call | flops 3000000000 | bytes 4000000 | tf_op jit(solution)/shard_map/pallas_call | solution.py:248
  87.8 0.6 collective-permute-start.21
  88.5 2.9 %collective-permute-start.23 = (f32[32,1024]{1,0:T(8,128)S(1)}, f32[32,1024]{1,0:T(8,128)S(1)}, u32[]{:S(2)}, u32[]{:S(2)}) collective-permute-start(f32[32,1024]{1,0:T(8,128)S(1)} %get-tuple-element.23), channel_id=1, source_target_pairs={{0,17},{1,16},{2,19},{3,18},{4,21},{5,20},{6,23},{7,22},{8,25},{9,... | collective-permute-start | bytes 393224 | tf_op jit(solution)/shard_map/ppermute | solution.py:401
  91.4 0.7 add_bitcast_fusion
  92.1 2.2 %collective-permute-done.21 = f32[32,1024]{1,0:T(8,128)S(1)} collective-permute-done((f32[32,1024]{1,0:T(8,128)S(1)}, f32[32,1024]{1,0:T(8,128)S(1)}, u32[]{:S(2)}, u32[]{:S(2)}) %collective-permute-start.21) | collective-permute-done | bytes 131104 | tf_op jit(solution)/shard_map/ppermute | solution.py:401
  94.3 3.5 %collective-permute-done.23 = f32[32,1024]{1,0:T(8,128)S(1)} collective-permute-done((f32[32,1024]{1,0:T(8,128)S(1)}, f32[32,1024]{1,0:T(8,128)S(1)}, u32[]{:S(2)}, u32[]{:S(2)}) %collective-permute-start.23) | collective-permute-done | bytes 131104 | tf_op jit(solution)/shard_map/ppermute | solution.py:401
  97.8 1.4 %collective-permute-done.22 = f32[32,1024]{1,0:T(8,128)S(1)} collective-permute-done((f32[32,1024]{1,0:T(8,128)S(1)}, f32[32,1024]{1,0:T(8,128)S(1)}, u32[]{:S(2)}, u32[]{:S(2)}) %collective-permute-start.22) | collective-permute-done | bytes 131104 | tf_op jit(solution)/shard_map/ppermute | solution.py:401
  99.2 0.7 fusion.2
  (49 shorter events, 0.6 us)
Async XLA Ops:
  0.6 12.5 %copy-start.2 = (bf16[1,1024]{1,0:T(2,128)(2,1)S(1)}, bf16[1,1024]{1,0:T(2,128)(2,1)}, u32[]{:S(2)}) copy-start(bf16[1,1024]{1,0:T(2,128)(2,1)} %param.11) | copy-start | bytes 6148
  0.6 12.5 %copy-start.3 = (s32[1,1024]{1,0:T(1,128)S(1)}, s32[1,1024]{1,0:T(1,128)}, u32[]{:S(2)}) copy-start(s32[1,1024]{1,0:T(1,128)} %param.10) | copy-start | bytes 12292
  0.7 12.6 %copy-start = (bf16[1,128,1024]{2,1,0:T(8,128)(2,1)S(1)}, bf16[1,128,1024]{2,1,0:T(8,128)(2,1)}, u32[]{:S(2)}) copy-start(bf16[1,128,1024]{2,1,0:T(8,128)(2,1)} %param.6) | copy-start | bytes 786436
  2.6 10.7 %collective-permute-start.5 = (bf16[64,1024]{1,0:T(8,128)(2,1)S(1)}, bf16[64,1024]{1,0:T(8,128)(2,1)S(1)}, u32[]{:S(2)}, u32[]{:S(2)}) collective-permute-start(bf16[64,1024]{1,0:T(8,128)(2,1)S(1)} %maximum_maximum_fusion), channel_id=1, source_target_pairs={{0,6},{2,0},{4,2},{6,4},{1,7},{3,1},{5,3},{7,5},{8,14},{10,8},{12,... | collective-permute-start | bytes 393224 | tf_op jit(solution)/shard_map/ppermute | solution.py:281
  7.7 12.8 %collective-permute-start.4 = (bf16[64,1024]{1,0:T(8,128)(2,1)S(1)}, bf16[64,1024]{1,0:T(8,128)(2,1)S(1)}, u32[]{:S(2)}, u32[]{:S(2)}) collective-permute-start(bf16[64,1024]{1,0:T(8,128)(2,1)S(1)} %maximum_maximum_fusion), channel_id=1, source_target_pairs={{0,4},{2,6},{4,0},{6,2},{1,5},{3,7},{5,1},{7,3},{8,12},{10,14},{12... | collective-permute-start | bytes 393224 | tf_op jit(solution)/shard_map/ppermute | solution.py:281
  7.7 12.9 %collective-permute-start.3 = (bf16[64,1024]{1,0:T(8,128)(2,1)S(1)}, bf16[64,1024]{1,0:T(8,128)(2,1)S(1)}, u32[]{:S(2)}, u32[]{:S(2)}) collective-permute-start(bf16[64,1024]{1,0:T(8,128)(2,1)S(1)} %maximum_maximum_fusion), channel_id=1, source_target_pairs={{0,2},{2,4},{4,6},{6,0},{1,3},{3,5},{5,7},{7,1},{8,10},{10,12},{12... | collective-permute-start | bytes 393224 | tf_op jit(solution)/shard_map/ppermute | solution.py:281
  9.8 15.5 %copy-start.1 = (bf16[32,1024]{1,0:T(8,128)(2,1)S(1)}, bf16[32,1024]{1,0:T(8,128)(2,1)}, u32[]{:S(2)}) copy-start(bf16[32,1024]{1,0:T(8,128)(2,1)} %param.7) | copy-start | bytes 196612
  10.0 15.3 %collective-permute-start.16 = (bf16[128,512]{1,0:T(8,128)(2,1)S(1)}, bf16[128,512]{1,0:T(8,128)(2,1)S(1)}, u32[]{:S(2)}, u32[]{:S(2)}) collective-permute-start(bf16[128,512]{1,0:T(8,128)(2,1)S(1)} %bitcast.123), channel_id=1, source_target_pairs={{0,6},{2,0},{4,2},{6,4},{1,7},{3,1},{5,3},{7,5},{8,14},{10,8},{12,... | collective-permute-start | bytes 393224 | tf_op jit(solution)/shard_map/ppermute | solution.py:298
  12.8 10.9 %collective-permute-start.14 = (bf16[128,512]{1,0:T(8,128)(2,1)S(1)}, bf16[128,512]{1,0:T(8,128)(2,1)S(1)}, u32[]{:S(2)}, u32[]{:S(2)}) collective-permute-start(bf16[128,512]{1,0:T(8,128)(2,1)S(1)} %bitcast.124), channel_id=1, source_target_pairs={{0,2},{2,4},{4,6},{6,0},{1,3},{3,5},{5,7},{7,1},{8,10},{10,12},{12... | collective-permute-start | bytes 393224 | tf_op jit(solution)/shard_map/ppermute | solution.py:298
  13.3 34.3 %collective-permute-start.2 = (bf16[128,1024]{1,0:T(8,128)(2,1)S(1)}, bf16[128,1024]{1,0:T(8,128)(2,1)S(1)}, u32[]{:S(2)}, u32[]{:S(2)}) collective-permute-start(bf16[128,1024]{1,0:T(8,128)(2,1)S(1)} %bitcast.127), channel_id=1, source_target_pairs={{0,6},{2,0},{4,2},{6,4},{1,7},{3,1},{5,3},{7,5},{8,14},{10,8},{12,... | collective-permute-start | bytes 786440 | tf_op jit(solution)/shard_map/ppermute | solution.py:310
  20.5 31.5 %collective-permute-start = (bf16[128,1024]{1,0:T(8,128)(2,1)S(1)}, bf16[128,1024]{1,0:T(8,128)(2,1)S(1)}, u32[]{:S(2)}, u32[]{:S(2)}) collective-permute-start(bf16[128,1024]{1,0:T(8,128)(2,1)S(1)} %bitcast.128), channel_id=1, source_target_pairs={{0,2},{2,4},{4,6},{6,0},{1,3},{3,5},{5,7},{7,1},{8,10},{10,12},{12... | collective-permute-start | bytes 786440 | tf_op jit(solution)/shard_map/ppermute | solution.py:310
  20.6 12.7 %collective-permute-start.13 = (bf16[96,1024]{1,0:T(8,128)(2,1)S(1)}, bf16[96,1024]{1,0:T(8,128)(2,1)S(1)}, u32[]{:S(2)}, u32[]{:S(2)}) collective-permute-start(bf16[96,1024]{1,0:T(8,128)(2,1)S(1)} %pad_maximum_fusion.1), channel_id=1, source_target_pairs={{0,1},{1,0},{2,3},{3,2},{4,5},{5,4},{6,7},{7,6},{8,9},{9,8},{10,11... | collective-permute-start | bytes 589832 | tf_op jit(solution)/shard_map/ppermute | solution.py:286
  23.8 16.8 %collective-permute-start.17 = (bf16[128,512]{1,0:T(8,128)(2,1)S(1)}, bf16[128,512]{1,0:T(8,128)(2,1)S(1)}, u32[]{:S(2)}, u32[]{:S(2)}) collective-permute-start(bf16[128,512]{1,0:T(8,128)(2,1)S(1)} %collective-permute-done.14.refs_0_), channel_id=1, source_target_pairs={{0,1},{1,0},{2,3},{3,2},{4,5},{5,4},{6,7},{7,6},{8,9},{9,8},{10,11... | collective-permute-start | bytes 393224 | tf_op jit(solution)/shard_map/ppermute | solution.py:302
  25.3 15.3 %collective-permute-start.15 = (bf16[128,512]{1,0:T(8,128)(2,1)S(1)}, bf16[128,512]{1,0:T(8,128)(2,1)S(1)}, u32[]{:S(2)}, u32[]{:S(2)}) collective-permute-start(bf16[128,512]{1,0:T(8,128)(2,1)S(1)} %collective-permute-done.14.refs_0_), channel_id=1, source_target_pairs={{0,2},{2,4},{4,6},{6,0},{1,3},{3,5},{5,7},{7,1},{8,10},{10,12},{12... | collective-permute-start | bytes 393224 | tf_op jit(solution)/shard_map/ppermute | solution.py:298
  33.3 5.0 %collective-permute-start.19 = (bf16[128,512]{1,0:T(8,128)(2,1)S(1)}, bf16[128,512]{1,0:T(8,128)(2,1)S(1)}, u32[]{:S(2)}, u32[]{:S(2)}) collective-permute-start(bf16[128,512]{1,0:T(8,128)(2,1)S(1)} %collective-permute-done.16.refs_2_), channel_id=1, source_target_pairs={{0,1},{1,0},{2,3},{3,2},{4,5},{5,4},{6,7},{7,6},{8,9},{9,8},{10,11... | collective-permute-start | bytes 393224 | tf_op jit(solution)/shard_map/ppermute | solution.py:302
  38.3 17.6 %collective-permute-start.8 = (bf16[4,32,1024]{2,1,0:T(8,128)(2,1)S(1)}, bf16[4,32,1024]{2,1,0:T(8,128)(2,1)S(1)}, u32[]{:S(2)}, u32[]{:S(2)}) collective-permute-start(bf16[4,32,1024]{2,1,0:T(8,128)(2,1)S(1)} %pad_maximum_fusion.refs_4_), channel_id=1, source_target_pairs={{0,17},{1,16},{8,25},{9,24},{16,1},{17,0},{24,9},{25,8},{2,19},{3,... | collective-permute-start | bytes 786440 | tf_op jit(solution)/shard_map/ppermute | solution.py:321
  40.6 15.2 %collective-permute-start.7 = (bf16[4,32,1024]{2,1,0:T(8,128)(2,1)S(1)}, bf16[4,32,1024]{2,1,0:T(8,128)(2,1)S(1)}, u32[]{:S(2)}, u32[]{:S(2)}) collective-permute-start(bf16[4,32,1024]{2,1,0:T(8,128)(2,1)S(1)} %pad_maximum_fusion.refs_4_), channel_id=1, source_target_pairs={{0,16},{1,17},{8,24},{9,25},{16,0},{17,1},{24,8},{25,9},{2,18},{3,... | collective-permute-start | bytes 786440 | tf_op jit(solution)/shard_map/ppermute | solution.py:321
  40.6 15.7 %collective-permute-start.6 = (bf16[4,32,1024]{2,1,0:T(8,128)(2,1)S(1)}, bf16[4,32,1024]{2,1,0:T(8,128)(2,1)S(1)}, u32[]{:S(2)}, u32[]{:S(2)}) collective-permute-start(bf16[4,32,1024]{2,1,0:T(8,128)(2,1)S(1)} %pad_maximum_fusion.refs_4_), channel_id=1, source_target_pairs={{0,1},{1,0},{8,9},{9,8},{16,17},{17,16},{24,25},{25,24},{2,3},{3,2... | collective-permute-start | bytes 786440 | tf_op jit(solution)/shard_map/ppermute | solution.py:321
  47.6 5.0 %collective-permute-start.18 = (bf16[128,512]{1,0:T(8,128)(2,1)S(1)}, bf16[128,512]{1,0:T(8,128)(2,1)S(1)}, u32[]{:S(2)}, u32[]{:S(2)}) collective-permute-start(bf16[128,512]{1,0:T(8,128)(2,1)S(1)} %collective-permute-done.15.refs_1_), channel_id=1, source_target_pairs={{0,1},{1,0},{2,3},{3,2},{4,5},{5,4},{6,7},{7,6},{8,9},{9,8},{10,11... | collective-permute-start | bytes 393224 | tf_op jit(solution)/shard_map/ppermute | solution.py:302
  52.1 9.8 %collective-permute-start.9 = (bf16[4,32,1024]{2,1,0:T(8,128)(2,1)S(1)}, bf16[4,32,1024]{2,1,0:T(8,128)(2,1)S(1)}, u32[]{:S(2)}, u32[]{:S(2)}) collective-permute-start(bf16[4,32,1024]{2,1,0:T(8,128)(2,1)S(1)} %pad_maximum_fusion.refs_4_), channel_id=1, source_target_pairs={{0,8},{8,0},{16,24},{24,16},{1,9},{9,1},{17,25},{25,17},{2,10},{10... | collective-permute-start | bytes 786440 | tf_op jit(solution)/shard_map/ppermute | solution.py:322
  52.6 10.0 %collective-permute-start.1 = (bf16[128,1024]{1,0:T(8,128)(2,1)S(1)}, bf16[128,1024]{1,0:T(8,128)(2,1)S(1)}, u32[]{:S(2)}, u32[]{:S(2)}) collective-permute-start(bf16[128,1024]{1,0:T(8,128)(2,1)S(1)} %collective-permute-done.refs_1_), channel_id=1, source_target_pairs={{0,2},{2,4},{4,6},{6,0},{1,3},{3,5},{5,7},{7,1},{8,10},{10,12},{12... | collective-permute-start | bytes 786440 | tf_op jit(solution)/shard_map/ppermute | solution.py:310
  55.8 6.8 %collective-permute-start.12 = (bf16[4,32,1024]{2,1,0:T(8,128)(2,1)S(1)}, bf16[4,32,1024]{2,1,0:T(8,128)(2,1)S(1)}, u32[]{:S(2)}, u32[]{:S(2)}) collective-permute-start(bf16[4,32,1024]{2,1,0:T(8,128)(2,1)S(1)} %collective-permute-done.8.refs_7_), channel_id=1, source_target_pairs={{0,8},{8,0},{16,24},{24,16},{1,9},{9,1},{17,25},{25,17},{2,10},{10... | collective-permute-start | bytes 786440 | tf_op jit(solution)/shard_map/ppermute | solution.py:322
  55.8 6.8 %collective-permute-start.11 = (bf16[4,32,1024]{2,1,0:T(8,128)(2,1)S(1)}, bf16[4,32,1024]{2,1,0:T(8,128)(2,1)S(1)}, u32[]{:S(2)}, u32[]{:S(2)}) collective-permute-start(bf16[4,32,1024]{2,1,0:T(8,128)(2,1)S(1)} %collective-permute-done.7.refs_6_), channel_id=1, source_target_pairs={{0,8},{8,0},{16,24},{24,16},{1,9},{9,1},{17,25},{25,17},{2,10},{10... | collective-permute-start | bytes 786440 | tf_op jit(solution)/shard_map/ppermute | solution.py:322
  56.3 6.3 %collective-permute-start.10 = (bf16[4,32,1024]{2,1,0:T(8,128)(2,1)S(1)}, bf16[4,32,1024]{2,1,0:T(8,128)(2,1)S(1)}, u32[]{:S(2)}, u32[]{:S(2)}) collective-permute-start(bf16[4,32,1024]{2,1,0:T(8,128)(2,1)S(1)} %collective-permute-done.6.refs_5_), channel_id=1, source_target_pairs={{0,8},{8,0},{16,24},{24,16},{1,9},{9,1},{17,25},{25,17},{2,10},{10... | collective-permute-start | bytes 786440 | tf_op jit(solution)/shard_map/ppermute | solution.py:322
  80.5 7.2 %collective-permute-start.20 = (f32[128,1024]{1,0:T(8,128)S(1)}, f32[128,1024]{1,0:T(8,128)S(1)}, u32[]{:S(2)}, u32[]{:S(2)}) collective-permute-start(f32[128,1024]{1,0:T(8,128)S(1)} %get-tuple-element.16), channel_id=1, source_target_pairs={{0,8},{8,0},{16,24},{24,16},{1,9},{9,1},{17,25},{25,17},{2,10},{10... | collective-permute-start | bytes 1572872 | tf_op jit(solution)/shard_map/ppermute | solution.py:376
  83.4 8.0 %collective-permute-start.24 = (f32[16,8,256]{2,1,0:T(8,128)S(1)}, f32[16,8,256]{2,1,0:T(8,128)S(1)}, u32[]{:S(2)}, u32[]{:S(2)}) collective-permute-start(f32[16,8,256]{2,1,0:T(8,128)S(1)} %shard_map.81), channel_id=1, source_target_pairs={{0,1},{1,0},{2,3},{3,2},{4,5},{5,4},{6,7},{7,6},{8,9},{9,8},{10,11... | collective-permute-start | bytes 393224 | tf_op jit(solution)/shard_map/ppermute | solution.py:388
  87.8 6.4 %collective-permute-start.21 = (f32[32,1024]{1,0:T(8,128)S(1)}, f32[32,1024]{1,0:T(8,128)S(1)}, u32[]{:S(2)}, u32[]{:S(2)}) collective-permute-start(f32[32,1024]{1,0:T(8,128)S(1)} %get-tuple-element.22), channel_id=1, source_target_pairs={{0,1},{1,0},{2,3},{3,2},{4,5},{5,4},{6,7},{7,6},{8,9},{9,8},{10,11... | collective-permute-start | bytes 393224 | tf_op jit(solution)/shard_map/ppermute | solution.py:401
  88.5 9.4 %collective-permute-start.23 = (f32[32,1024]{1,0:T(8,128)S(1)}, f32[32,1024]{1,0:T(8,128)S(1)}, u32[]{:S(2)}, u32[]{:S(2)}) collective-permute-start(f32[32,1024]{1,0:T(8,128)S(1)} %get-tuple-element.23), channel_id=1, source_target_pairs={{0,17},{1,16},{2,19},{3,18},{4,21},{5,20},{6,23},{7,22},{8,25},{9,... | collective-permute-start | bytes 393224 | tf_op jit(solution)/shard_map/ppermute | solution.py:401
  91.3 7.9 %collective-permute-start.22 = (f32[32,1024]{1,0:T(8,128)S(1)}, f32[32,1024]{1,0:T(8,128)S(1)}, u32[]{:S(2)}, u32[]{:S(2)}) collective-permute-start(f32[32,1024]{1,0:T(8,128)S(1)} %get-tuple-element.24), channel_id=1, source_target_pairs={{0,16},{1,17},{2,18},{3,19},{4,20},{5,21},{6,22},{7,23},{8,24},{9,... | collective-permute-start | bytes 393224 | tf_op jit(solution)/shard_map/ppermute | solution.py:401

commit v5 on v4

--- a/solution.py
+++ b/solution.py
@@ -107,8 +107,8 @@
     q_refs, refs = refs[:n_q], refs[n_q:]
     w_refs, refs = refs[:n_w], refs[n_w:]
     g_refs, refs = refs[:n_g], refs[n_g:]
-    own_ref, other_ref, grads_refs, refs = refs[0], refs[1], refs[2:-8], refs[-8:]
-    w, q, exps, normed, total, gn, nt, some = refs
+    own_ref, other_ref, grads_refs, refs = refs[0], refs[1], refs[2:-12], refs[-12:]
+    w, q, exps, normed, total, gn, nt, some, ahead, places, even, odd = refs
     for i, w_ref in enumerate(w_refs):
         blocks, rows = w_ref.shape[0], w_ref.shape[1]
         for k in range(blocks):
@@ -130,40 +130,46 @@
     for i in range(len(grads_refs)):
         at = pl.ds(pl.multiple_of(blocks_ref[i] * features, features), features)
         some[i * features : (i + 1) * features, :] = nt[at, :]
+    at = [(tiles, j) for tiles in g_refs for j in range(tiles.shape[0])]
+    width = at[0][0].shape[2]
+    spread = [pl.ds(c, LANES) for c in range(0, width, LANES)]
     total[...] = jnp.zeros_like(total)
-    first = 0
-    for tiles in g_refs:
-
-        def score(j, _, tiles=tiles, first=first):
-            e = jnp.exp(jnp.dot(q[...], tiles[j], preferred_element_type=F32))
-            exps[first + j] = e
-            part = total[...]
-            for c in range(0, e.shape[1], LANES):
-                part = part + e[:, c : c + LANES]
-            total[...] = part
-            return 0
-
-        lax.fori_loop(0, tiles.shape[0], score, 0)
-        first += tiles.shape[0]
-    gn[...] = jnp.zeros_like(gn)
-    scale = 1.0 / jnp.sum(total[...], axis=1, keepdims=True)
-    first = 0
-    for tiles in g_refs:
-        width = tiles.shape[2]
-
-        def back(j, _, tiles=tiles, first=first, width=width):
-            ids = tbase_ref[first + j] + lax.broadcasted_iota(I32, (1, width), 1)
-            target = (pos_ref[...] == ids).astype(F32)
-            gs = (wt_ref[...] * (exps[first + j] * scale - target)).astype(BF16)
-            grads = jnp.dot(some[...], gs, preferred_element_type=F32)
-            span = pl.ds(pl.multiple_of((first + j) * width, width), width)
-            for i, grads_ref in enumerate(grads_refs):
-                grads_ref[:, span] = grads[i * features : (i + 1) * features]
-            gn[...] += lax.dot_general(gs, tiles[j], NT, preferred_element_type=F32)
-            return 0
-
-        lax.fori_loop(0, tiles.shape[0], back, 0)
-        first += tiles.shape[0]
+
+    def exponent(n):
+        part = total[...]
+        for c in spread:
+            e = jnp.exp(exps[n, :, c])
+            exps[n, :, c] = e
+            part = part + e
+        total[...] = part
+
+    for n, (tiles, j) in enumerate(at):
+        exps[n] = jnp.dot(q[...], tiles[j], preferred_element_type=F32)
+        if n:
+            exponent(n - 1)
+    exponent(len(at) - 1)
+    scale = wt_ref[...] / jnp.sum(total[...], axis=1, keepdims=True)
+    ahead[0] = jnp.broadcast_to(scale, total.shape)
+    ahead[1] = jnp.broadcast_to(wt_ref[...], total.shape)
+    places[...] = jnp.broadcast_to(pos_ref[...], total.shape)
+    lane = lax.broadcasted_iota(I32, (1, LANES), 1)
+
+    def weigh(n):
+        out = (even, odd)[n % 2]
+        for i, c in enumerate(spread):
+            hit = places[...] == lane + (tbase_ref[n] + i * LANES)
+            out[:, c] = (exps[n, :, c] * ahead[0] - jnp.where(hit, ahead[1], 0.0)).astype(BF16)
+
+    weigh(0)
+    for n, (tiles, j) in enumerate(at):
+        gs = (even, odd)[n % 2]
+        if n + 1 < len(at):
+            weigh(n + 1)
+        more = lax.dot_general(gs[...], tiles[j], NT, preferred_element_type=F32)
+        gn[...] = more if n == 0 else gn[...] + more
+        grads = jnp.dot(some[...], gs[...], preferred_element_type=F32)
+        for i, grads_ref in enumerate(grads_refs):
+            grads_ref[:, n * width : (n + 1) * width] = grads[i * features : (i + 1) * features]
     inner = jnp.mean(gn[...] * normed[...], axis=1, keepdims=True)
     grad = (inv_rms * (gn[...] - normed[...] * inner)).astype(BF16)
     half = rows // 2
@@ -193,6 +199,10 @@
             pltpu.VMEM((queries, features), F32),
             pltpu.VMEM((features, queries), BF16),
             pltpu.VMEM((rows * blocks.shape[0], queries), BF16),
+            pltpu.VMEM((2, queries, LANES), F32),
+            pltpu.VMEM((queries, LANES), I32),
+            pltpu.VMEM((queries, width), BF16),
+            pltpu.VMEM((queries, width), BF16),
         ],
         compiler_params=pltpu.CompilerParams(vmem_limit_bytes=(28 if n_t * queries * width * 4 <= 8 * MIB else 60) * MIB),
         cost_estimate=cost(20 * 10**9, 20 * 10**6),

time: 100 us -> 96.6 us (0.966)
  Pallas kernels: 38.2 us -> 34.7 us
    pallas_call x1, Pallas kernels: 17.9 us -> 14.2 us  [main(): pl.pallas_call(functools.partial(main_kernel, n_q, n_w, n_g), out_shape=(...]
  transfers between devices with their start and end apart: 25 -> 25, of which waited for: 8 -> 8; matrix products, arithmetic and copies ran while one was open for 3% -> 3% of each run, Pallas kernels for 20% -> 21%
where the time goes in v5:
time: 96.6 us; the launch traced here: 96.4 us
  starting transfers between devices  37.9 us (39%)
  Pallas kernels  34.7 us (36%)
  waiting for transfers between devices  17 us (18%)
  other arithmetic  4.59 us (5%)
  local copies, waits for them, and re-layouts  1.21 us (1%)
  between operations  0.98 us (1%)
    pallas_call x3, Pallas kernels, rebuild(): pl.pallas_call(functools.partial(rebuild_kernel, n_t, n_b), out_shape=(ja...  14.7 us
    pallas_call x1, Pallas kernels, main(): pl.pallas_call(functools.partial(main_kernel, n_q, n_w, n_g), out_shape=(...  14.2 us
    ppermute x3, starting transfers between devices, compute(): tiles[0, k] = move(source, 'shard', ring(n_sh, step))  10.8 us
    ppermute x3, waiting for transfers between devices, compute(): moved = move(summed[i, o], ('dom', 'shard', 'dp'), pairs)  7.11 us
    ppermute x3, starting transfers between devices, compute(): q_held[k] = move(q_held[(k - step) % group], 'shard', pairs)  7.05 us
    ppermute x3, starting transfers between devices, compute(): moved = [move(packet, 'shard', ring(n_sh, k)) for k in range(1, n_sh)]  6.14 us
    pallas_call x2, Pallas kernels, word_grads(): pl.pallas_call(functools.partial(words_kernel, words, block), out_shape=j...  5.81 us
    ppermute x3, waiting for transfers between devices, compute(): tiles[t, k] = move(tiles[0, k], 'dp', ring(n_dp, t))  4.93 us
  transfers between devices with their start and end apart: 25, of which 8 were waited for; matrix products, arithmetic and copies ran while one was open for 3% of the time, Pallas kernels for 21%

profile of v5, /device:TPU:0, one launch (start us, length us, event | category | flops | bytes accessed | tf_op | source)
XLA Modules:
  0.0 96.4 jit_solution(5737487049090010188)
XLA Ops:
  0.7 1.0 %convert_element_type.14 = bf16[1,32,8,256]{3,2,1,0:T(8,128)(2,1)S(1)} convert(f32[1,32,8,256]{3,2,1,0:T(8,128)} %param.8) | non-fusion elementwise | flops 65536 | bytes 393216 | tf_op jit(solution)/shard_map/convert_element_type | solution.py:280
  1.7 0.9 maximum_maximum_fusion
  2.6 5.1 %collective-permute-start.5 = (bf16[64,1024]{1,0:T(8,128)(2,1)S(1)}, bf16[64,1024]{1,0:T(8,128)(2,1)S(1)}, u32[]{:S(2)}, u32[]{:S(2)}) collective-permute-start(bf16[64,1024]{1,0:T(8,128)(2,1)S(1)} %maximum_maximum_fusion), channel_id=1, source_target_pairs={{0,6},{2,0},{4,2},{6,4},{1,7},{3,1},{5,3},{7,5},{8,14},{10,8},{12,... | collective-permute-start | bytes 393224 | tf_op jit(solution)/shard_map/ppermute | solution.py:291
  7.7 1.0 %collective-permute-start.3 = (bf16[64,1024]{1,0:T(8,128)(2,1)S(1)}, bf16[64,1024]{1,0:T(8,128)(2,1)S(1)}, u32[]{:S(2)}, u32[]{:S(2)}) collective-permute-start(bf16[64,1024]{1,0:T(8,128)(2,1)S(1)} %maximum_maximum_fusion), channel_id=1, source_target_pairs={{0,2},{2,4},{4,6},{6,0},{1,3},{3,5},{5,7},{7,1},{8,10},{10,12},{12... | collective-permute-start | bytes 393224 | tf_op jit(solution)/shard_map/ppermute | solution.py:291
  8.7 1.1 %convert_element_type.15 = bf16[1,1024,128]{2,1,0:T(8,128)(2,1)S(1)} convert(s32[1,1024,128]{2,1,0:T(8,128)} %param.9) | non-fusion elementwise | flops 131072 | bytes 786432 | tf_op jit(solution)/shard_map/convert_element_type | solution.py:300
  9.9 0.1 copy.10
  10.0 2.9 %collective-permute-start.16 = (bf16[128,512]{1,0:T(8,128)(2,1)S(1)}, bf16[128,512]{1,0:T(8,128)(2,1)S(1)}, u32[]{:S(2)}, u32[]{:S(2)}) collective-permute-start(bf16[128,512]{1,0:T(8,128)(2,1)S(1)} %bitcast.123), channel_id=1, source_target_pairs={{0,6},{2,0},{4,2},{6,4},{1,7},{3,1},{5,3},{7,5},{8,14},{10,8},{12,... | collective-permute-start | bytes 393224 | tf_op jit(solution)/shard_map/ppermute | solution.py:308
  12.8 0.1 stack.236
  13.0 0.1 stack.257
  13.1 0.1 iota_add_fusion
  13.3 3.9 %collective-permute-start.2 = (bf16[128,1024]{1,0:T(8,128)(2,1)S(1)}, bf16[128,1024]{1,0:T(8,128)(2,1)S(1)}, u32[]{:S(2)}, u32[]{:S(2)}) collective-permute-start(bf16[128,1024]{1,0:T(8,128)(2,1)S(1)} %bitcast.127), channel_id=1, source_target_pairs={{0,6},{2,0},{4,2},{6,4},{1,7},{3,1},{5,3},{7,5},{8,14},{10,8},{12,... | collective-permute-start | bytes 786440 | tf_op jit(solution)/shard_map/ppermute | solution.py:320
  17.2 3.4 %collective-permute-done.4 = bf16[64,1024]{1,0:T(8,128)(2,1)S(1)} collective-permute-done((bf16[64,1024]{1,0:T(8,128)(2,1)S(1)}, bf16[64,1024]{1,0:T(8,128)(2,1)S(1)}, u32[]{:S(2)}, u32[]{:S(2)}) %collective-permute-start.4) | collective-permute-done | bytes 131104 | tf_op jit(solution)/shard_map/ppermute | solution.py:291
  20.6 1.6 %collective-permute-start.13 = (bf16[96,1024]{1,0:T(8,128)(2,1)S(1)}, bf16[96,1024]{1,0:T(8,128)(2,1)S(1)}, u32[]{:S(2)}, u32[]{:S(2)}) collective-permute-start(bf16[96,1024]{1,0:T(8,128)(2,1)S(1)} %pad_maximum_fusion.1), channel_id=1, source_target_pairs={{0,1},{1,0},{2,3},{3,2},{4,5},{5,4},{6,7},{7,6},{8,9},{9,8},{10,11... | collective-permute-start | bytes 589832 | tf_op jit(solution)/shard_map/ppermute | solution.py:296
  22.2 0.1 pad_add_fusion.1.blocks_ref
  22.2 0.1 add.492.frow_ref
  22.4 0.1 copy.14.wt_ref
  22.5 0.1 copy.13.pos_ref
  22.7 0.1 copy.11
  22.8 0.1 stack.271.place_ref
  22.9 0.1 stack.245.tbase_ref
  23.0 0.8 collective-permute-done.14.refs_0_
  23.8 1.5 %collective-permute-start.17 = (bf16[128,512]{1,0:T(8,128)(2,1)S(1)}, bf16[128,512]{1,0:T(8,128)(2,1)S(1)}, u32[]{:S(2)}, u32[]{:S(2)}) collective-permute-start(bf16[128,512]{1,0:T(8,128)(2,1)S(1)} %collective-permute-done.14.refs_0_), channel_id=1, source_target_pairs={{0,1},{1,0},{2,3},{3,2},{4,5},{5,4},{6,7},{7,6},{8,9},{9,8},{10,11... | collective-permute-start | bytes 393224 | tf_op jit(solution)/shard_map/ppermute | solution.py:312
  25.3 8.0 %collective-permute-start.15 = (bf16[128,512]{1,0:T(8,128)(2,1)S(1)}, bf16[128,512]{1,0:T(8,128)(2,1)S(1)}, u32[]{:S(2)}, u32[]{:S(2)}) collective-permute-start(bf16[128,512]{1,0:T(8,128)(2,1)S(1)} %collective-permute-done.14.refs_0_), channel_id=1, source_target_pairs={{0,2},{2,4},{4,6},{6,0},{1,3},{3,5},{5,7},{7,1},{8,10},{10,12},{12... | collective-permute-start | bytes 393224 | tf_op jit(solution)/shard_map/ppermute | solution.py:308
  33.3 0.5 collective-permute-start.19
  33.8 4.4 %collective-permute-done.19.refs_2_ = bf16[128,512]{1,0:T(8,128)(2,1)S(1)} collective-permute-done((bf16[128,512]{1,0:T(8,128)(2,1)S(1)}, bf16[128,512]{1,0:T(8,128)(2,1)S(1)}, u32[]{:S(2)}, u32[]{:S(2)}) %collective-permute-start.19) | collective-permute-done | bytes 131104 | tf_op jit(solution)/shard_map/ppermute | solution.py:312
  38.3 2.3 %collective-permute-start.8 = (bf16[4,32,1024]{2,1,0:T(8,128)(2,1)S(1)}, bf16[4,32,1024]{2,1,0:T(8,128)(2,1)S(1)}, u32[]{:S(2)}, u32[]{:S(2)}) collective-permute-start(bf16[4,32,1024]{2,1,0:T(8,128)(2,1)S(1)} %pad_maximum_fusion.refs_4_), channel_id=1, source_target_pairs={{0,17},{1,16},{8,25},{9,24},{16,1},{17,0},{24,9},{25,8},{2,19},{3,... | collective-permute-start | bytes 786440 | tf_op jit(solution)/shard_map/ppermute | solution.py:331
  40.6 1.5 %collective-permute-start.6 = (bf16[4,32,1024]{2,1,0:T(8,128)(2,1)S(1)}, bf16[4,32,1024]{2,1,0:T(8,128)(2,1)S(1)}, u32[]{:S(2)}, u32[]{:S(2)}) collective-permute-start(bf16[4,32,1024]{2,1,0:T(8,128)(2,1)S(1)} %pad_maximum_fusion.refs_4_), channel_id=1, source_target_pairs={{0,1},{1,0},{8,9},{9,8},{16,17},{17,16},{24,25},{25,24},{2,3},{3,2... | collective-permute-start | bytes 786440 | tf_op jit(solution)/shard_map/ppermute | solution.py:331
  42.2 5.4 %shard_map.78 = (bf16[3,1024,512]{2,1,0:T(8,128)(2,1)S(1)}, s32[3,2,16,512]{3,2,1,0:T(8,128)S(1)}) custom-call(s32[8]{0:T(128)S(1)} %stack.271.place_ref, s32[2]{0:T(128)S(1)} %pad_add_fusion.1.blocks_ref, bf16[128,512]{1,0:T(8,128)(2,1)S(1)} %collective-permute-done.14.refs_0_, bf16[128,512]{1,0:T(8,128)(2,1)S(1)} %collective-permute-done.15.refs_1_, ...), custom_call_target="tpu_custom_call" | custom-call | flops 3000000000 | bytes 6000000 | tf_op jit(solution)/shard_map/pallas_call | solution.py:89
  47.6 0.6 collective-permute-start.18
  48.2 3.8 %shard_map.77 = (bf16[2,1024,512]{2,1,0:T(8,128)(2,1)S(1)}, s32[2,2,16,512]{3,2,1,0:T(8,128)S(1)}) custom-call(s32[8]{0:T(128)S(1)} %stack.271.place_ref, s32[2]{0:T(128)S(1)} %pad_add_fusion.1.blocks_ref, bf16[128,512]{1,0:T(8,128)(2,1)S(1)} %bitcast.125, bf16[128,512]{1,0:T(8,128)(2,1)S(1)} %bitcast.126, ...), custom_call_target="tpu_custom_call" | custom-call | flops 2000000000 | bytes 4000000 | tf_op jit(solution)/shard_map/pallas_call | solution.py:89
  52.1 0.1 collective-permute-start.9
  52.1 0.5 collective-permute-done.18.refs_1_
  52.6 3.2 %collective-permute-start.1 = (bf16[128,1024]{1,0:T(8,128)(2,1)S(1)}, bf16[128,1024]{1,0:T(8,128)(2,1)S(1)}, u32[]{:S(2)}, u32[]{:S(2)}) collective-permute-start(bf16[128,1024]{1,0:T(8,128)(2,1)S(1)} %collective-permute-done.refs_1_), channel_id=1, source_target_pairs={{0,2},{2,4},{4,6},{6,0},{1,3},{3,5},{5,7},{7,1},{8,10},{10,12},{12... | collective-permute-start | bytes 786440 | tf_op jit(solution)/shard_map/ppermute | solution.py:320
  55.8 0.5 collective-permute-start.11
  56.4 5.4 %shard_map.79 = (bf16[3,1024,512]{2,1,0:T(8,128)(2,1)S(1)}, s32[3,2,16,512]{3,2,1,0:T(8,128)S(1)}) custom-call(s32[8]{0:T(128)S(1)} %stack.271.place_ref, s32[2]{0:T(128)S(1)} %pad_add_fusion.1.blocks_ref, bf16[128,512]{1,0:T(8,128)(2,1)S(1)} %collective-permute-done.17.refs_0_, bf16[128,512]{1,0:T(8,128)(2,1)S(1)} %collective-permute-done.18.refs_1_, ...), custom_call_target="tpu_custom_call" | custom-call | flops 3000000000 | bytes 6000000 | tf_op jit(solution)/shard_map/pallas_call | solution.py:89
  61.9 0.8 collective-permute-done.1.refs_2_
  62.7 14.2 %shard_map.80 = (f32[128,1024]{1,0:T(8,128)S(1)}, f32[128,1024]{1,0:T(8,128)S(1)}, f32[128,4096]{1,0:T(8,128)S(1)}, f32[128,4096]{1,0:T(8,128)S(1)}) custom-call(s32[32]{0:T(128)S(1)} %broadcast_multiply_fusion.woff_ref, s32[8]{0:T(128)S(1)} %stack.245.tbase_ref, s32[2]{0:T(128)S(1)} %pad_add_fusion.1.blocks_ref, s32[256,1]{1,0:T(8,128)S(1)} %add.492.frow_ref, ...), custom_call_target="tpu_custom_call" | custom-call | flops 20000000000 | bytes 20000000 | tf_op jit(solution)/shard_map/pallas_call | solution.py:187
  76.8 0.1 collective-permute-start.20
  76.9 3.0 %shard_map.81 = f32[16,8,256]{2,1,0:T(8,128)S(1)} custom-call(f32[128,4096]{1,0:T(8,128)S(1)} %get-tuple-element.17.grads_ref, s32[2,2,16,512]{3,2,1,0:T(8,128)S(1)} %get-tuple-element.18.refs_0_, s32[3,2,16,512]{3,2,1,0:T(8,128)S(1)} %get-tuple-element.19.refs_1_, s32[3,2,16,512]{3,2,1,0:T(8,128)S(1)} %get-tuple-element.20.refs_2_), custom_call_target="tpu_custom_call" | custom-call | flops 3000000000 | bytes 4000000 | tf_op jit(solution)/shard_map/pallas_call | solution.py:258
  79.9 1.5 %collective-permute-start.24 = (f32[16,8,256]{2,1,0:T(8,128)S(1)}, f32[16,8,256]{2,1,0:T(8,128)S(1)}, u32[]{:S(2)}, u32[]{:S(2)}) collective-permute-start(f32[16,8,256]{2,1,0:T(8,128)S(1)} %shard_map.81), channel_id=1, source_target_pairs={{0,1},{1,0},{2,3},{3,2},{4,5},{5,4},{6,7},{7,6},{8,9},{9,8},{10,11... | collective-permute-start | bytes 393224 | tf_op jit(solution)/shard_map/ppermute | solution.py:398
  81.4 2.8 %shard_map.82 = f32[16,8,256]{2,1,0:T(8,128)S(1)} custom-call(f32[128,4096]{1,0:T(8,128)S(1)} %get-tuple-element.21.grads_ref, s32[2,2,16,512]{3,2,1,0:T(8,128)S(1)} %get-tuple-element.18.refs_0_, s32[3,2,16,512]{3,2,1,0:T(8,128)S(1)} %get-tuple-element.19.refs_1_, s32[3,2,16,512]{3,2,1,0:T(8,128)S(1)} %get-tuple-element.20.refs_2_), custom_call_target="tpu_custom_call" | custom-call | flops 3000000000 | bytes 4000000 | tf_op jit(solution)/shard_map/pallas_call | solution.py:258
  84.3 0.6 collective-permute-start.21
  85.0 2.9 %collective-permute-start.23 = (f32[32,1024]{1,0:T(8,128)S(1)}, f32[32,1024]{1,0:T(8,128)S(1)}, u32[]{:S(2)}, u32[]{:S(2)}) collective-permute-start(f32[32,1024]{1,0:T(8,128)S(1)} %get-tuple-element.23), channel_id=1, source_target_pairs={{0,17},{1,16},{2,19},{3,18},{4,21},{5,20},{6,23},{7,22},{8,25},{9,... | collective-permute-start | bytes 393224 | tf_op jit(solution)/shard_map/ppermute | solution.py:411
  87.9 0.7 add_bitcast_fusion
  88.6 2.2 %collective-permute-done.21 = f32[32,1024]{1,0:T(8,128)S(1)} collective-permute-done((f32[32,1024]{1,0:T(8,128)S(1)}, f32[32,1024]{1,0:T(8,128)S(1)}, u32[]{:S(2)}, u32[]{:S(2)}) %collective-permute-start.21) | collective-permute-done | bytes 131104 | tf_op jit(solution)/shard_map/ppermute | solution.py:411
  90.8 3.5 %collective-permute-done.23 = f32[32,1024]{1,0:T(8,128)S(1)} collective-permute-done((f32[32,1024]{1,0:T(8,128)S(1)}, f32[32,1024]{1,0:T(8,128)S(1)}, u32[]{:S(2)}, u32[]{:S(2)}) %collective-permute-start.23) | collective-permute-done | bytes 131104 | tf_op jit(solution)/shard_map/ppermute | solution.py:411
  94.3 1.4 %collective-permute-done.22 = f32[32,1024]{1,0:T(8,128)S(1)} collective-permute-done((f32[32,1024]{1,0:T(8,128)S(1)}, f32[32,1024]{1,0:T(8,128)S(1)}, u32[]{:S(2)}, u32[]{:S(2)}) %collective-permute-start.22) | collective-permute-done | bytes 131104 | tf_op jit(solution)/shard_map/ppermute | solution.py:411
  95.7 0.7 fusion.2
  (49 shorter events, 0.6 us)
Async XLA Ops:
  0.6 12.5 %copy-start.2 = (bf16[1,1024]{1,0:T(2,128)(2,1)S(1)}, bf16[1,1024]{1,0:T(2,128)(2,1)}, u32[]{:S(2)}) copy-start(bf16[1,1024]{1,0:T(2,128)(2,1)} %param.11) | copy-start | bytes 6148
  0.6 12.5 %copy-start.3 = (s32[1,1024]{1,0:T(1,128)S(1)}, s32[1,1024]{1,0:T(1,128)}, u32[]{:S(2)}) copy-start(s32[1,1024]{1,0:T(1,128)} %param.10) | copy-start | bytes 12292
  0.7 12.6 %copy-start = (bf16[1,128,1024]{2,1,0:T(8,128)(2,1)S(1)}, bf16[1,128,1024]{2,1,0:T(8,128)(2,1)}, u32[]{:S(2)}) copy-start(bf16[1,128,1024]{2,1,0:T(8,128)(2,1)} %param.6) | copy-start | bytes 786436
  2.6 10.7 %collective-permute-start.5 = (bf16[64,1024]{1,0:T(8,128)(2,1)S(1)}, bf16[64,1024]{1,0:T(8,128)(2,1)S(1)}, u32[]{:S(2)}, u32[]{:S(2)}) collective-permute-start(bf16[64,1024]{1,0:T(8,128)(2,1)S(1)} %maximum_maximum_fusion), channel_id=1, source_target_pairs={{0,6},{2,0},{4,2},{6,4},{1,7},{3,1},{5,3},{7,5},{8,14},{10,8},{12,... | collective-permute-start | bytes 393224 | tf_op jit(solution)/shard_map/ppermute | solution.py:291
  7.7 12.8 %collective-permute-start.4 = (bf16[64,1024]{1,0:T(8,128)(2,1)S(1)}, bf16[64,1024]{1,0:T(8,128)(2,1)S(1)}, u32[]{:S(2)}, u32[]{:S(2)}) collective-permute-start(bf16[64,1024]{1,0:T(8,128)(2,1)S(1)} %maximum_maximum_fusion), channel_id=1, source_target_pairs={{0,4},{2,6},{4,0},{6,2},{1,5},{3,7},{5,1},{7,3},{8,12},{10,14},{12... | collective-permute-start | bytes 393224 | tf_op jit(solution)/shard_map/ppermute | solution.py:291
  7.7 12.9 %collective-permute-start.3 = (bf16[64,1024]{1,0:T(8,128)(2,1)S(1)}, bf16[64,1024]{1,0:T(8,128)(2,1)S(1)}, u32[]{:S(2)}, u32[]{:S(2)}) collective-permute-start(bf16[64,1024]{1,0:T(8,128)(2,1)S(1)} %maximum_maximum_fusion), channel_id=1, source_target_pairs={{0,2},{2,4},{4,6},{6,0},{1,3},{3,5},{5,7},{7,1},{8,10},{10,12},{12... | collective-permute-start | bytes 393224 | tf_op jit(solution)/shard_map/ppermute | solution.py:291
  9.8 15.5 %copy-start.1 = (bf16[32,1024]{1,0:T(8,128)(2,1)S(1)}, bf16[32,1024]{1,0:T(8,128)(2,1)}, u32[]{:S(2)}) copy-start(bf16[32,1024]{1,0:T(8,128)(2,1)} %param.7) | copy-start | bytes 196612
  10.0 15.3 %collective-permute-start.16 = (bf16[128,512]{1,0:T(8,128)(2,1)S(1)}, bf16[128,512]{1,0:T(8,128)(2,1)S(1)}, u32[]{:S(2)}, u32[]{:S(2)}) collective-permute-start(bf16[128,512]{1,0:T(8,128)(2,1)S(1)} %bitcast.123), channel_id=1, source_target_pairs={{0,6},{2,0},{4,2},{6,4},{1,7},{3,1},{5,3},{7,5},{8,14},{10,8},{12,... | collective-permute-start | bytes 393224 | tf_op jit(solution)/shard_map/ppermute | solution.py:308
  12.8 10.9 %collective-permute-start.14 = (bf16[128,512]{1,0:T(8,128)(2,1)S(1)}, bf16[128,512]{1,0:T(8,128)(2,1)S(1)}, u32[]{:S(2)}, u32[]{:S(2)}) collective-permute-start(bf16[128,512]{1,0:T(8,128)(2,1)S(1)} %bitcast.124), channel_id=1, source_target_pairs={{0,2},{2,4},{4,6},{6,0},{1,3},{3,5},{5,7},{7,1},{8,10},{10,12},{12... | collective-permute-start | bytes 393224 | tf_op jit(solution)/shard_map/ppermute | solution.py:308
  13.3 34.3 %collective-permute-start.2 = (bf16[128,1024]{1,0:T(8,128)(2,1)S(1)}, bf16[128,1024]{1,0:T(8,128)(2,1)S(1)}, u32[]{:S(2)}, u32[]{:S(2)}) collective-permute-start(bf16[128,1024]{1,0:T(8,128)(2,1)S(1)} %bitcast.127), channel_id=1, source_target_pairs={{0,6},{2,0},{4,2},{6,4},{1,7},{3,1},{5,3},{7,5},{8,14},{10,8},{12,... | collective-permute-start | bytes 786440 | tf_op jit(solution)/shard_map/ppermute | solution.py:320
  20.5 31.5 %collective-permute-start = (bf16[128,1024]{1,0:T(8,128)(2,1)S(1)}, bf16[128,1024]{1,0:T(8,128)(2,1)S(1)}, u32[]{:S(2)}, u32[]{:S(2)}) collective-permute-start(bf16[128,1024]{1,0:T(8,128)(2,1)S(1)} %bitcast.128), channel_id=1, source_target_pairs={{0,2},{2,4},{4,6},{6,0},{1,3},{3,5},{5,7},{7,1},{8,10},{10,12},{12... | collective-permute-start | bytes 786440 | tf_op jit(solution)/shard_map/ppermute | solution.py:320
  20.6 12.7 %collective-permute-start.13 = (bf16[96,1024]{1,0:T(8,128)(2,1)S(1)}, bf16[96,1024]{1,0:T(8,128)(2,1)S(1)}, u32[]{:S(2)}, u32[]{:S(2)}) collective-permute-start(bf16[96,1024]{1,0:T(8,128)(2,1)S(1)} %pad_maximum_fusion.1), channel_id=1, source_target_pairs={{0,1},{1,0},{2,3},{3,2},{4,5},{5,4},{6,7},{7,6},{8,9},{9,8},{10,11... | collective-permute-start | bytes 589832 | tf_op jit(solution)/shard_map/ppermute | solution.py:296
  23.8 16.8 %collective-permute-start.17 = (bf16[128,512]{1,0:T(8,128)(2,1)S(1)}, bf16[128,512]{1,0:T(8,128)(2,1)S(1)}, u32[]{:S(2)}, u32[]{:S(2)}) collective-permute-start(bf16[128,512]{1,0:T(8,128)(2,1)S(1)} %collective-permute-done.14.refs_0_), channel_id=1, source_target_pairs={{0,1},{1,0},{2,3},{3,2},{4,5},{5,4},{6,7},{7,6},{8,9},{9,8},{10,11... | collective-permute-start | bytes 393224 | tf_op jit(solution)/shard_map/ppermute | solution.py:312
  25.3 15.3 %collective-permute-start.15 = (bf16[128,512]{1,0:T(8,128)(2,1)S(1)}, bf16[128,512]{1,0:T(8,128)(2,1)S(1)}, u32[]{:S(2)}, u32[]{:S(2)}) collective-permute-start(bf16[128,512]{1,0:T(8,128)(2,1)S(1)} %collective-permute-done.14.refs_0_), channel_id=1, source_target_pairs={{0,2},{2,4},{4,6},{6,0},{1,3},{3,5},{5,7},{7,1},{8,10},{10,12},{12... | collective-permute-start | bytes 393224 | tf_op jit(solution)/shard_map/ppermute | solution.py:308
  33.3 5.0 %collective-permute-start.19 = (bf16[128,512]{1,0:T(8,128)(2,1)S(1)}, bf16[128,512]{1,0:T(8,128)(2,1)S(1)}, u32[]{:S(2)}, u32[]{:S(2)}) collective-permute-start(bf16[128,512]{1,0:T(8,128)(2,1)S(1)} %collective-permute-done.16.refs_2_), channel_id=1, source_target_pairs={{0,1},{1,0},{2,3},{3,2},{4,5},{5,4},{6,7},{7,6},{8,9},{9,8},{10,11... | collective-permute-start | bytes 393224 | tf_op jit(solution)/shard_map/ppermute | solution.py:312
  38.3 17.6 %collective-permute-start.8 = (bf16[4,32,1024]{2,1,0:T(8,128)(2,1)S(1)}, bf16[4,32,1024]{2,1,0:T(8,128)(2,1)S(1)}, u32[]{:S(2)}, u32[]{:S(2)}) collective-permute-start(bf16[4,32,1024]{2,1,0:T(8,128)(2,1)S(1)} %pad_maximum_fusion.refs_4_), channel_id=1, source_target_pairs={{0,17},{1,16},{8,25},{9,24},{16,1},{17,0},{24,9},{25,8},{2,19},{3,... | collective-permute-start | bytes 786440 | tf_op jit(solution)/shard_map/ppermute | solution.py:331
  40.6 15.2 %collective-permute-start.7 = (bf16[4,32,1024]{2,1,0:T(8,128)(2,1)S(1)}, bf16[4,32,1024]{2,1,0:T(8,128)(2,1)S(1)}, u32[]{:S(2)}, u32[]{:S(2)}) collective-permute-start(bf16[4,32,1024]{2,1,0:T(8,128)(2,1)S(1)} %pad_maximum_fusion.refs_4_), channel_id=1, source_target_pairs={{0,16},{1,17},{8,24},{9,25},{16,0},{17,1},{24,8},{25,9},{2,18},{3,... | collective-permute-start | bytes 786440 | tf_op jit(solution)/shard_map/ppermute | solution.py:331
  40.6 15.7 %collective-permute-start.6 = (bf16[4,32,1024]{2,1,0:T(8,128)(2,1)S(1)}, bf16[4,32,1024]{2,1,0:T(8,128)(2,1)S(1)}, u32[]{:S(2)}, u32[]{:S(2)}) collective-permute-start(bf16[4,32,1024]{2,1,0:T(8,128)(2,1)S(1)} %pad_maximum_fusion.refs_4_), channel_id=1, source_target_pairs={{0,1},{1,0},{8,9},{9,8},{16,17},{17,16},{24,25},{25,24},{2,3},{3,2... | collective-permute-start | bytes 786440 | tf_op jit(solution)/shard_map/ppermute | solution.py:331
  47.6 5.0 %collective-permute-start.18 = (bf16[128,512]{1,0:T(8,128)(2,1)S(1)}, bf16[128,512]{1,0:T(8,128)(2,1)S(1)}, u32[]{:S(2)}, u32[]{:S(2)}) collective-permute-start(bf16[128,512]{1,0:T(8,128)(2,1)S(1)} %collective-permute-done.15.refs_1_), channel_id=1, source_target_pairs={{0,1},{1,0},{2,3},{3,2},{4,5},{5,4},{6,7},{7,6},{8,9},{9,8},{10,11... | collective-permute-start | bytes 393224 | tf_op jit(solution)/shard_map/ppermute | solution.py:312
  52.1 9.8 %collective-permute-start.9 = (bf16[4,32,1024]{2,1,0:T(8,128)(2,1)S(1)}, bf16[4,32,1024]{2,1,0:T(8,128)(2,1)S(1)}, u32[]{:S(2)}, u32[]{:S(2)}) collective-permute-start(bf16[4,32,1024]{2,1,0:T(8,128)(2,1)S(1)} %pad_maximum_fusion.refs_4_), channel_id=1, source_target_pairs={{0,8},{8,0},{16,24},{24,16},{1,9},{9,1},{17,25},{25,17},{2,10},{10... | collective-permute-start | bytes 786440 | tf_op jit(solution)/shard_map/ppermute | solution.py:332
  52.6 10.0 %collective-permute-start.1 = (bf16[128,1024]{1,0:T(8,128)(2,1)S(1)}, bf16[128,1024]{1,0:T(8,128)(2,1)S(1)}, u32[]{:S(2)}, u32[]{:S(2)}) collective-permute-start(bf16[128,1024]{1,0:T(8,128)(2,1)S(1)} %collective-permute-done.refs_1_), channel_id=1, source_target_pairs={{0,2},{2,4},{4,6},{6,0},{1,3},{3,5},{5,7},{7,1},{8,10},{10,12},{12... | collective-permute-start | bytes 786440 | tf_op jit(solution)/shard_map/ppermute | solution.py:320
  55.8 6.8 %collective-permute-start.12 = (bf16[4,32,1024]{2,1,0:T(8,128)(2,1)S(1)}, bf16[4,32,1024]{2,1,0:T(8,128)(2,1)S(1)}, u32[]{:S(2)}, u32[]{:S(2)}) collective-permute-start(bf16[4,32,1024]{2,1,0:T(8,128)(2,1)S(1)} %collective-permute-done.8.refs_7_), channel_id=1, source_target_pairs={{0,8},{8,0},{16,24},{24,16},{1,9},{9,1},{17,25},{25,17},{2,10},{10... | collective-permute-start | bytes 786440 | tf_op jit(solution)/shard_map/ppermute | solution.py:332
  55.8 6.8 %collective-permute-start.11 = (bf16[4,32,1024]{2,1,0:T(8,128)(2,1)S(1)}, bf16[4,32,1024]{2,1,0:T(8,128)(2,1)S(1)}, u32[]{:S(2)}, u32[]{:S(2)}) collective-permute-start(bf16[4,32,1024]{2,1,0:T(8,128)(2,1)S(1)} %collective-permute-done.7.refs_6_), channel_id=1, source_target_pairs={{0,8},{8,0},{16,24},{24,16},{1,9},{9,1},{17,25},{25,17},{2,10},{10... | collective-permute-start | bytes 786440 | tf_op jit(solution)/shard_map/ppermute | solution.py:332
  56.3 6.3 %collective-permute-start.10 = (bf16[4,32,1024]{2,1,0:T(8,128)(2,1)S(1)}, bf16[4,32,1024]{2,1,0:T(8,128)(2,1)S(1)}, u32[]{:S(2)}, u32[]{:S(2)}) collective-permute-start(bf16[4,32,1024]{2,1,0:T(8,128)(2,1)S(1)} %collective-permute-done.6.refs_5_), channel_id=1, source_target_pairs={{0,8},{8,0},{16,24},{24,16},{1,9},{9,1},{17,25},{25,17},{2,10},{10... | collective-permute-start | bytes 786440 | tf_op jit(solution)/shard_map/ppermute | solution.py:332
  76.8 7.4 %collective-permute-start.20 = (f32[128,1024]{1,0:T(8,128)S(1)}, f32[128,1024]{1,0:T(8,128)S(1)}, u32[]{:S(2)}, u32[]{:S(2)}) collective-permute-start(f32[128,1024]{1,0:T(8,128)S(1)} %get-tuple-element.16), channel_id=1, source_target_pairs={{0,8},{8,0},{16,24},{24,16},{1,9},{9,1},{17,25},{25,17},{2,10},{10... | collective-permute-start | bytes 1572872 | tf_op jit(solution)/shard_map/ppermute | solution.py:386
  79.9 8.0 %collective-permute-start.24 = (f32[16,8,256]{2,1,0:T(8,128)S(1)}, f32[16,8,256]{2,1,0:T(8,128)S(1)}, u32[]{:S(2)}, u32[]{:S(2)}) collective-permute-start(f32[16,8,256]{2,1,0:T(8,128)S(1)} %shard_map.81), channel_id=1, source_target_pairs={{0,1},{1,0},{2,3},{3,2},{4,5},{5,4},{6,7},{7,6},{8,9},{9,8},{10,11... | collective-permute-start | bytes 393224 | tf_op jit(solution)/shard_map/ppermute | solution.py:398
  84.3 6.4 %collective-permute-start.21 = (f32[32,1024]{1,0:T(8,128)S(1)}, f32[32,1024]{1,0:T(8,128)S(1)}, u32[]{:S(2)}, u32[]{:S(2)}) collective-permute-start(f32[32,1024]{1,0:T(8,128)S(1)} %get-tuple-element.22), channel_id=1, source_target_pairs={{0,1},{1,0},{2,3},{3,2},{4,5},{5,4},{6,7},{7,6},{8,9},{9,8},{10,11... | collective-permute-start | bytes 393224 | tf_op jit(solution)/shard_map/ppermute | solution.py:411
  85.0 9.4 %collective-permute-start.23 = (f32[32,1024]{1,0:T(8,128)S(1)}, f32[32,1024]{1,0:T(8,128)S(1)}, u32[]{:S(2)}, u32[]{:S(2)}) collective-permute-start(f32[32,1024]{1,0:T(8,128)S(1)} %get-tuple-element.23), channel_id=1, source_target_pairs={{0,17},{1,16},{2,19},{3,18},{4,21},{5,20},{6,23},{7,22},{8,25},{9,... | collective-permute-start | bytes 393224 | tf_op jit(solution)/shard_map/ppermute | solution.py:411
  87.8 7.9 %collective-permute-start.22 = (f32[32,1024]{1,0:T(8,128)S(1)}, f32[32,1024]{1,0:T(8,128)S(1)}, u32[]{:S(2)}, u32[]{:S(2)}) collective-permute-start(f32[32,1024]{1,0:T(8,128)S(1)} %get-tuple-element.24), channel_id=1, source_target_pairs={{0,16},{1,17},{2,18},{3,19},{4,20},{5,21},{6,22},{7,23},{8,24},{9,... | collective-permute-start | bytes 393224 | tf_op jit(solution)/shard_map/ppermute | solution.py:411

commit v6 on v5

--- a/solution.py
+++ b/solution.py
@@ -36,51 +36,60 @@
 
 def rebuild_kernel(n_t, n_b, place_ref, blocks_ref, *refs):
     code_refs, books = refs[:n_t], refs[n_t : n_t + n_b]
-    out_ref, kept_ref, codes_ref, table = refs[n_t + n_b :]
-    sub, words = table.shape[1:]
+    out_ref, kept_ref, codes_ref, *tables = refs[n_t + n_b :]
     columns = code_refs[0].shape[1]
     kept = kept_ref.shape[2]
+    words = len(tables) * LANES
     for i, code_ref in enumerate(code_refs):
         codes_ref[i] = code_ref[...].astype(I32)
         for b in range(kept_ref.shape[1]):
             kept_ref[i, b] = codes_ref[i, pl.ds(pl.multiple_of(blocks_ref[b] * kept, kept), kept), :]
     for piece, book_ref in enumerate(books):
-        some = book_ref.shape[0] // sub
+        rows = book_ref.shape[0]
         blocks = book_ref.shape[1] // words
         for c in range(blocks):
-            part = book_ref[:, c * words : (c + 1) * words].astype(F32).reshape(some, sub, words)
-            table[pl.ds((place_ref[piece] * blocks + c) * some, some)] = part
-
+            at = pl.ds(pl.multiple_of((place_ref[piece] * blocks + c) * rows, rows), rows)
+            for i, table in enumerate(tables):
+                first = c * words + i * LANES
+                table[at, :] = book_ref[:, first : first + LANES].astype(F32)
     subspaces = code_refs[0].shape[0]
     span = min(subspaces, SPAN)
     steps = subspaces // span
+    sub = tables[0].shape[0] // subspaces
 
     def body(i, _):
         tile, first = i // steps, lax.rem(i, steps) * span
         for j in range(span // 8):
             rows = pl.multiple_of(first + 8 * j, 8)
-            codes = codes_ref[tile, pl.ds(rows, 8), :]
-            for pair in range(4):
-                tables = []
-                for h in range(2):
-                    words_of = table[rows + 2 * pair + h]
-                    tables.append([words_of[:, c : c + LANES] for c in range(0, words, LANES)])
+            index = codes_ref[tile, pl.ds(rows, 8), :]
+            for pair in range(0, sub, 2):
+                held = []
+                for f in range(pair, pair + 2):
+                    held.append([table[pl.ds(rows * sub + f, 8, stride=sub), :] for table in tables])
                 for t in range(0, columns, LANES):
+                    code = index[:, t : t + LANES]
+                    lane = code & (LANES - 1)
                     parts = []
-                    for h in range(2):
-                        row = codes[2 * pair + h : 2 * pair + h + 1, t : t + LANES]
-                        index = jnp.broadcast_to(row, (sub, LANES))
-                        lane = index & (LANES - 1)
+                    for f in range(2):
                         value = None
-                        for c, part in enumerate(tables[h]):
+                        for c, part in enumerate(held[f]):
                             found = jnp.take_along_axis(part, lane, axis=1, mode="promise_in_bounds")
-                            value = found if value is None else jnp.where(index < c * LANES, value, found)
+                            value = found if value is None else jnp.where(code < c * LANES, value, found)
                         parts.append(value)
-                    out_rows = pl.ds(pl.multiple_of((rows + 2 * pair) * sub, 2 * sub), 2 * sub)
+                    out_rows = pl.ds(pl.multiple_of(rows * sub + 8 * pair, 16), 16)
                     out_ref[tile, out_rows, t : t + LANES] = jnp.concatenate(parts, 0).astype(BF16)
         return 0
 
     lax.fori_loop(0, n_t * steps, body, 0)
+
+
+def regroup(x):
+    lane = lax.broadcasted_iota(I32, (x.shape[0], LANES), 1)
+    lane = (lane & 64) + (lane & 7) * 8 + (lax.shift_right_logical(lane, 3) & 7)
+    parts = [x[:, c : c + LANES] for c in range(0, x.shape[1], LANES)]
+    return jnp.concatenate(
+        [jnp.take_along_axis(p, lane, axis=1, mode="promise_in_bounds") for p in parts], 1
+    )
 
 
 def rebuild(place, blocks, kept, sub, words, codes, books):
@@ -96,8 +105,8 @@
         out_specs=(VMEM, VMEM),
         scratch_shapes=[
             pltpu.VMEM((n_t, subspaces, columns), I32),
-            pltpu.VMEM((subspaces, sub, words), F32),
-        ],
+        ]
+        + [pltpu.VMEM((subspaces * sub, LANES), F32)] * (words // LANES),
         compiler_params=pltpu.CompilerParams(vmem_limit_bytes=(6 + n_t) * MIB),
         cost_estimate=cost(n_t * 10**9, n_t * 2 * 10**6),
     )(place, blocks, *codes, *books)
@@ -124,7 +133,7 @@
     inv_rms = lax.rsqrt(jnp.mean(encoded * encoded, axis=1, keepdims=True) + 1e-06)
     normed[...] = encoded * inv_rms
     low = normed[...].astype(BF16)
-    q[...] = low
+    q[...] = regroup(normed[...]).astype(BF16)
     nt[...] = low.T
     features = grads_refs[0].shape[0]
     for i in range(len(grads_refs)):
@@ -170,6 +179,7 @@
         grads = jnp.dot(some[...], gs[...], preferred_element_type=F32)
         for i, grads_ref in enumerate(grads_refs):
             grads_ref[:, n * width : (n + 1) * width] = grads[i * features : (i + 1) * features]
+    gn[...] = regroup(gn[...])
     inner = jnp.mean(gn[...] * normed[...], axis=1, keepdims=True)
     grad = (inv_rms * (gn[...] - normed[...] * inner)).astype(BF16)
     half = rows // 2

time: 96.6 us -> 96.4 us (level)
    pallas_call x3, Pallas kernels: 14.7 us -> 13.3 us  [rebuild(): pl.pallas_call(functools.partial(rebuild_kernel, n_t, n_b), out_shape=(ja...]
  transfers between devices with their start and end apart: 25 -> 25, of which waited for: 8 -> 8; matrix products, arithmetic and copies ran while one was open for 3% -> 3% of each run, Pallas kernels for 21% -> 20%
where the time goes in v6:
time: 96.4 us; the launch traced here: 96.2 us
  starting transfers between devices  38 us (39%)
  Pallas kernels  34 us (35%)
  waiting for transfers between devices  17.4 us (18%)
  other arithmetic  4.59 us (5%)
  local copies, waits for them, and re-layouts  1.21 us (1%)
  between operations  0.97 us (1%)
    pallas_call x1, Pallas kernels, main(): pl.pallas_call(functools.partial(main_kernel, n_q, n_w, n_g), out_shape=(...  14.9 us
    pallas_call x3, Pallas kernels, rebuild(): pl.pallas_call(functools.partial(rebuild_kernel, n_t, n_b), out_shape=(ja...  13.3 us
    ppermute x3, starting transfers between devices, compute(): tiles[0, k] = move(source, 'shard', ring(n_sh, step))  10.8 us
    ppermute x3, starting transfers between devices, compute(): q_held[k] = move(q_held[(k - step) % group], 'shard', pairs)  7.16 us
    ppermute x3, waiting for transfers between devices, compute(): moved = move(summed[i, o], ('dom', 'shard', 'dp'), pairs)  7.08 us
    ppermute x3, starting transfers between devices, compute(): moved = [move(packet, 'shard', ring(n_sh, k)) for k in range(1, n_sh)]  6.14 us
    pallas_call x2, Pallas kernels, word_grads(): pl.pallas_call(functools.partial(words_kernel, words, block), out_shape=j...  5.8 us
    ppermute x3, waiting for transfers between devices, compute(): tiles[t, k] = move(tiles[0, k], 'dp', ring(n_dp, t))  5.72 us
  transfers between devices with their start and end apart: 25, of which 8 were waited for; matrix products, arithmetic and copies ran while one was open for 3% of the time, Pallas kernels for 20%

profile of v6, /device:TPU:0, one launch (start us, length us, event | category | flops | bytes accessed | tf_op | source)
XLA Modules:
  0.0 96.2 jit_solution(10411884510651855716)
XLA Ops:
  0.7 1.0 %convert_element_type.14 = bf16[1,32,8,256]{3,2,1,0:T(8,128)(2,1)S(1)} convert(f32[1,32,8,256]{3,2,1,0:T(8,128)} %param.8) | non-fusion elementwise | flops 65536 | bytes 393216 | tf_op jit(solution)/shard_map/convert_element_type | solution.py:290
  1.7 0.9 maximum_maximum_fusion
  2.6 5.1 %collective-permute-start.5 = (bf16[64,1024]{1,0:T(8,128)(2,1)S(1)}, bf16[64,1024]{1,0:T(8,128)(2,1)S(1)}, u32[]{:S(2)}, u32[]{:S(2)}) collective-permute-start(bf16[64,1024]{1,0:T(8,128)(2,1)S(1)} %maximum_maximum_fusion), channel_id=1, source_target_pairs={{0,6},{2,0},{4,2},{6,4},{1,7},{3,1},{5,3},{7,5},{8,14},{10,8},{12,... | collective-permute-start | bytes 393224 | tf_op jit(solution)/shard_map/ppermute | solution.py:301
  7.7 1.0 %collective-permute-start.3 = (bf16[64,1024]{1,0:T(8,128)(2,1)S(1)}, bf16[64,1024]{1,0:T(8,128)(2,1)S(1)}, u32[]{:S(2)}, u32[]{:S(2)}) collective-permute-start(bf16[64,1024]{1,0:T(8,128)(2,1)S(1)} %maximum_maximum_fusion), channel_id=1, source_target_pairs={{0,2},{2,4},{4,6},{6,0},{1,3},{3,5},{5,7},{7,1},{8,10},{10,12},{12... | collective-permute-start | bytes 393224 | tf_op jit(solution)/shard_map/ppermute | solution.py:301
  8.7 1.1 %convert_element_type.15 = bf16[1,1024,128]{2,1,0:T(8,128)(2,1)S(1)} convert(s32[1,1024,128]{2,1,0:T(8,128)} %param.9) | non-fusion elementwise | flops 131072 | bytes 786432 | tf_op jit(solution)/shard_map/convert_element_type | solution.py:310
  9.9 0.1 copy.10
  10.0 2.9 %collective-permute-start.16 = (bf16[128,512]{1,0:T(8,128)(2,1)S(1)}, bf16[128,512]{1,0:T(8,128)(2,1)S(1)}, u32[]{:S(2)}, u32[]{:S(2)}) collective-permute-start(bf16[128,512]{1,0:T(8,128)(2,1)S(1)} %bitcast.123), channel_id=1, source_target_pairs={{0,6},{2,0},{4,2},{6,4},{1,7},{3,1},{5,3},{7,5},{8,14},{10,8},{12,... | collective-permute-start | bytes 393224 | tf_op jit(solution)/shard_map/ppermute | solution.py:318
  12.8 0.1 stack.236
  13.0 0.1 stack.257
  13.1 0.1 iota_add_fusion
  13.3 3.9 %collective-permute-start.2 = (bf16[128,1024]{1,0:T(8,128)(2,1)S(1)}, bf16[128,1024]{1,0:T(8,128)(2,1)S(1)}, u32[]{:S(2)}, u32[]{:S(2)}) collective-permute-start(bf16[128,1024]{1,0:T(8,128)(2,1)S(1)} %bitcast.127), channel_id=1, source_target_pairs={{0,6},{2,0},{4,2},{6,4},{1,7},{3,1},{5,3},{7,5},{8,14},{10,8},{12,... | collective-permute-start | bytes 786440 | tf_op jit(solution)/shard_map/ppermute | solution.py:330
  17.2 3.4 %collective-permute-done.4 = bf16[64,1024]{1,0:T(8,128)(2,1)S(1)} collective-permute-done((bf16[64,1024]{1,0:T(8,128)(2,1)S(1)}, bf16[64,1024]{1,0:T(8,128)(2,1)S(1)}, u32[]{:S(2)}, u32[]{:S(2)}) %collective-permute-start.4) | collective-permute-done | bytes 131104 | tf_op jit(solution)/shard_map/ppermute | solution.py:301
  20.6 1.6 %collective-permute-start.13 = (bf16[96,1024]{1,0:T(8,128)(2,1)S(1)}, bf16[96,1024]{1,0:T(8,128)(2,1)S(1)}, u32[]{:S(2)}, u32[]{:S(2)}) collective-permute-start(bf16[96,1024]{1,0:T(8,128)(2,1)S(1)} %pad_maximum_fusion.1), channel_id=1, source_target_pairs={{0,1},{1,0},{2,3},{3,2},{4,5},{5,4},{6,7},{7,6},{8,9},{9,8},{10,11... | collective-permute-start | bytes 589832 | tf_op jit(solution)/shard_map/ppermute | solution.py:306
  22.2 0.1 pad_add_fusion.1.blocks_ref
  22.2 0.1 add.492.frow_ref
  22.4 0.1 copy.14.wt_ref
  22.5 0.1 copy.13.pos_ref
  22.7 0.1 copy.11
  22.8 0.1 stack.271.place_ref
  22.9 0.1 stack.245.tbase_ref
  23.0 0.8 collective-permute-done.14.refs_0_
  23.8 1.5 %collective-permute-start.17 = (bf16[128,512]{1,0:T(8,128)(2,1)S(1)}, bf16[128,512]{1,0:T(8,128)(2,1)S(1)}, u32[]{:S(2)}, u32[]{:S(2)}) collective-permute-start(bf16[128,512]{1,0:T(8,128)(2,1)S(1)} %collective-permute-done.14.refs_0_), channel_id=1, source_target_pairs={{0,1},{1,0},{2,3},{3,2},{4,5},{5,4},{6,7},{7,6},{8,9},{9,8},{10,11... | collective-permute-start | bytes 393224 | tf_op jit(solution)/shard_map/ppermute | solution.py:322
  25.3 8.0 %collective-permute-start.15 = (bf16[128,512]{1,0:T(8,128)(2,1)S(1)}, bf16[128,512]{1,0:T(8,128)(2,1)S(1)}, u32[]{:S(2)}, u32[]{:S(2)}) collective-permute-start(bf16[128,512]{1,0:T(8,128)(2,1)S(1)} %collective-permute-done.14.refs_0_), channel_id=1, source_target_pairs={{0,2},{2,4},{4,6},{6,0},{1,3},{3,5},{5,7},{7,1},{8,10},{10,12},{12... | collective-permute-start | bytes 393224 | tf_op jit(solution)/shard_map/ppermute | solution.py:318
  33.3 0.5 collective-permute-start.19
  33.8 4.4 %collective-permute-done.19.refs_2_ = bf16[128,512]{1,0:T(8,128)(2,1)S(1)} collective-permute-done((bf16[128,512]{1,0:T(8,128)(2,1)S(1)}, bf16[128,512]{1,0:T(8,128)(2,1)S(1)}, u32[]{:S(2)}, u32[]{:S(2)}) %collective-permute-start.19) | collective-permute-done | bytes 131104 | tf_op jit(solution)/shard_map/ppermute | solution.py:322
  38.3 2.3 %collective-permute-start.8 = (bf16[4,32,1024]{2,1,0:T(8,128)(2,1)S(1)}, bf16[4,32,1024]{2,1,0:T(8,128)(2,1)S(1)}, u32[]{:S(2)}, u32[]{:S(2)}) collective-permute-start(bf16[4,32,1024]{2,1,0:T(8,128)(2,1)S(1)} %pad_maximum_fusion.refs_4_), channel_id=1, source_target_pairs={{0,17},{1,16},{8,25},{9,24},{16,1},{17,0},{24,9},{25,8},{2,19},{3,... | collective-permute-start | bytes 786440 | tf_op jit(solution)/shard_map/ppermute | solution.py:341
  40.6 1.5 %collective-permute-start.6 = (bf16[4,32,1024]{2,1,0:T(8,128)(2,1)S(1)}, bf16[4,32,1024]{2,1,0:T(8,128)(2,1)S(1)}, u32[]{:S(2)}, u32[]{:S(2)}) collective-permute-start(bf16[4,32,1024]{2,1,0:T(8,128)(2,1)S(1)} %pad_maximum_fusion.refs_4_), channel_id=1, source_target_pairs={{0,1},{1,0},{8,9},{9,8},{16,17},{17,16},{24,25},{25,24},{2,3},{3,2... | collective-permute-start | bytes 786440 | tf_op jit(solution)/shard_map/ppermute | solution.py:341
  42.2 4.9 %shard_map.78 = (bf16[3,1024,512]{2,1,0:T(8,128)(2,1)S(1)}, s32[3,2,16,512]{3,2,1,0:T(8,128)S(1)}) custom-call(s32[8]{0:T(128)S(1)} %stack.271.place_ref, s32[2]{0:T(128)S(1)} %pad_add_fusion.1.blocks_ref, bf16[128,512]{1,0:T(8,128)(2,1)S(1)} %collective-permute-done.14.refs_0_, bf16[128,512]{1,0:T(8,128)(2,1)S(1)} %collective-permute-done.15.refs_1_, ...), custom_call_target="tpu_custom_call" | custom-call | flops 3000000000 | bytes 6000000 | tf_op jit(solution)/shard_map/pallas_call | solution.py:98
  47.1 0.6 collective-permute-start.18
  47.7 3.5 %shard_map.77 = (bf16[2,1024,512]{2,1,0:T(8,128)(2,1)S(1)}, s32[2,2,16,512]{3,2,1,0:T(8,128)S(1)}) custom-call(s32[8]{0:T(128)S(1)} %stack.271.place_ref, s32[2]{0:T(128)S(1)} %pad_add_fusion.1.blocks_ref, bf16[128,512]{1,0:T(8,128)(2,1)S(1)} %bitcast.125, bf16[128,512]{1,0:T(8,128)(2,1)S(1)} %bitcast.126, ...), custom_call_target="tpu_custom_call" | custom-call | flops 2000000000 | bytes 4000000 | tf_op jit(solution)/shard_map/pallas_call | solution.py:98
  51.2 1.3 %collective-permute-done.18.refs_1_ = bf16[128,512]{1,0:T(8,128)(2,1)S(1)} collective-permute-done((bf16[128,512]{1,0:T(8,128)(2,1)S(1)}, bf16[128,512]{1,0:T(8,128)(2,1)S(1)}, u32[]{:S(2)}, u32[]{:S(2)}) %collective-permute-start.18) | collective-permute-done | bytes 131104 | tf_op jit(solution)/shard_map/ppermute | solution.py:322
  52.5 3.3 %collective-permute-start.1 = (bf16[128,1024]{1,0:T(8,128)(2,1)S(1)}, bf16[128,1024]{1,0:T(8,128)(2,1)S(1)}, u32[]{:S(2)}, u32[]{:S(2)}) collective-permute-start(bf16[128,1024]{1,0:T(8,128)(2,1)S(1)} %collective-permute-done.refs_1_), channel_id=1, source_target_pairs={{0,2},{2,4},{4,6},{6,0},{1,3},{3,5},{5,7},{7,1},{8,10},{10,12},{12... | collective-permute-start | bytes 786440 | tf_op jit(solution)/shard_map/ppermute | solution.py:330
  55.8 0.5 collective-permute-start.11
  56.4 4.9 %shard_map.79 = (bf16[3,1024,512]{2,1,0:T(8,128)(2,1)S(1)}, s32[3,2,16,512]{3,2,1,0:T(8,128)S(1)}) custom-call(s32[8]{0:T(128)S(1)} %stack.271.place_ref, s32[2]{0:T(128)S(1)} %pad_add_fusion.1.blocks_ref, bf16[128,512]{1,0:T(8,128)(2,1)S(1)} %collective-permute-done.17.refs_0_, bf16[128,512]{1,0:T(8,128)(2,1)S(1)} %collective-permute-done.18.refs_1_, ...), custom_call_target="tpu_custom_call" | custom-call | flops 3000000000 | bytes 6000000 | tf_op jit(solution)/shard_map/pallas_call | solution.py:98
  61.3 0.4 collective-permute-done.1.refs_2_
  61.7 14.9 %shard_map.80 = (f32[128,1024]{1,0:T(8,128)S(1)}, f32[128,1024]{1,0:T(8,128)S(1)}, f32[128,4096]{1,0:T(8,128)S(1)}, f32[128,4096]{1,0:T(8,128)S(1)}) custom-call(s32[32]{0:T(128)S(1)} %broadcast_multiply_fusion.woff_ref, s32[8]{0:T(128)S(1)} %stack.245.tbase_ref, s32[2]{0:T(128)S(1)} %pad_add_fusion.1.blocks_ref, s32[256,1]{1,0:T(8,128)S(1)} %add.492.frow_ref, ...), custom_call_target="tpu_custom_call" | custom-call | flops 20000000000 | bytes 20000000 | tf_op jit(solution)/shard_map/pallas_call | solution.py:197
  76.7 0.1 collective-permute-start.20
  76.8 3.0 %shard_map.81 = f32[16,8,256]{2,1,0:T(8,128)S(1)} custom-call(f32[128,4096]{1,0:T(8,128)S(1)} %get-tuple-element.17.grads_ref, s32[2,2,16,512]{3,2,1,0:T(8,128)S(1)} %get-tuple-element.18.refs_0_, s32[3,2,16,512]{3,2,1,0:T(8,128)S(1)} %get-tuple-element.19.refs_1_, s32[3,2,16,512]{3,2,1,0:T(8,128)S(1)} %get-tuple-element.20.refs_2_), custom_call_target="tpu_custom_call" | custom-call | flops 3000000000 | bytes 4000000 | tf_op jit(solution)/shard_map/pallas_call | solution.py:268
  79.8 1.5 %collective-permute-start.24 = (f32[16,8,256]{2,1,0:T(8,128)S(1)}, f32[16,8,256]{2,1,0:T(8,128)S(1)}, u32[]{:S(2)}, u32[]{:S(2)}) collective-permute-start(f32[16,8,256]{2,1,0:T(8,128)S(1)} %shard_map.81), channel_id=1, source_target_pairs={{0,1},{1,0},{2,3},{3,2},{4,5},{5,4},{6,7},{7,6},{8,9},{9,8},{10,11... | collective-permute-start | bytes 393224 | tf_op jit(solution)/shard_map/ppermute | solution.py:408
  81.3 2.8 %shard_map.82 = f32[16,8,256]{2,1,0:T(8,128)S(1)} custom-call(f32[128,4096]{1,0:T(8,128)S(1)} %get-tuple-element.21.grads_ref, s32[2,2,16,512]{3,2,1,0:T(8,128)S(1)} %get-tuple-element.18.refs_0_, s32[3,2,16,512]{3,2,1,0:T(8,128)S(1)} %get-tuple-element.19.refs_1_, s32[3,2,16,512]{3,2,1,0:T(8,128)S(1)} %get-tuple-element.20.refs_2_), custom_call_target="tpu_custom_call" | custom-call | flops 3000000000 | bytes 4000000 | tf_op jit(solution)/shard_map/pallas_call | solution.py:268
  84.2 0.6 collective-permute-start.21
  84.8 2.8 %collective-permute-start.23 = (f32[32,1024]{1,0:T(8,128)S(1)}, f32[32,1024]{1,0:T(8,128)S(1)}, u32[]{:S(2)}, u32[]{:S(2)}) collective-permute-start(f32[32,1024]{1,0:T(8,128)S(1)} %get-tuple-element.23), channel_id=1, source_target_pairs={{0,17},{1,16},{2,19},{3,18},{4,21},{5,20},{6,23},{7,22},{8,25},{9,... | collective-permute-start | bytes 393224 | tf_op jit(solution)/shard_map/ppermute | solution.py:421
  87.7 0.1 collective-permute-start.22
  87.8 0.7 add_bitcast_fusion
  88.4 2.2 %collective-permute-done.21 = f32[32,1024]{1,0:T(8,128)S(1)} collective-permute-done((f32[32,1024]{1,0:T(8,128)S(1)}, f32[32,1024]{1,0:T(8,128)S(1)}, u32[]{:S(2)}, u32[]{:S(2)}) %collective-permute-start.21) | collective-permute-done | bytes 131104 | tf_op jit(solution)/shard_map/ppermute | solution.py:421
  90.6 3.5 %collective-permute-done.23 = f32[32,1024]{1,0:T(8,128)S(1)} collective-permute-done((f32[32,1024]{1,0:T(8,128)S(1)}, f32[32,1024]{1,0:T(8,128)S(1)}, u32[]{:S(2)}, u32[]{:S(2)}) %collective-permute-start.23) | collective-permute-done | bytes 131104 | tf_op jit(solution)/shard_map/ppermute | solution.py:421
  94.2 1.4 %collective-permute-done.22 = f32[32,1024]{1,0:T(8,128)S(1)} collective-permute-done((f32[32,1024]{1,0:T(8,128)S(1)}, f32[32,1024]{1,0:T(8,128)S(1)}, u32[]{:S(2)}, u32[]{:S(2)}) %collective-permute-start.22) | collective-permute-done | bytes 131104 | tf_op jit(solution)/shard_map/ppermute | solution.py:421
  95.5 0.7 fusion.2
  (49 shorter events, 0.6 us)
Async XLA Ops:
  0.6 12.5 %copy-start.2 = (bf16[1,1024]{1,0:T(2,128)(2,1)S(1)}, bf16[1,1024]{1,0:T(2,128)(2,1)}, u32[]{:S(2)}) copy-start(bf16[1,1024]{1,0:T(2,128)(2,1)} %param.11) | copy-start | bytes 6148
  0.6 12.5 %copy-start.3 = (s32[1,1024]{1,0:T(1,128)S(1)}, s32[1,1024]{1,0:T(1,128)}, u32[]{:S(2)}) copy-start(s32[1,1024]{1,0:T(1,128)} %param.10) | copy-start | bytes 12292
  0.7 12.6 %copy-start = (bf16[1,128,1024]{2,1,0:T(8,128)(2,1)S(1)}, bf16[1,128,1024]{2,1,0:T(8,128)(2,1)}, u32[]{:S(2)}) copy-start(bf16[1,128,1024]{2,1,0:T(8,128)(2,1)} %param.6) | copy-start | bytes 786436
  2.6 10.7 %collective-permute-start.5 = (bf16[64,1024]{1,0:T(8,128)(2,1)S(1)}, bf16[64,1024]{1,0:T(8,128)(2,1)S(1)}, u32[]{:S(2)}, u32[]{:S(2)}) collective-permute-start(bf16[64,1024]{1,0:T(8,128)(2,1)S(1)} %maximum_maximum_fusion), channel_id=1, source_target_pairs={{0,6},{2,0},{4,2},{6,4},{1,7},{3,1},{5,3},{7,5},{8,14},{10,8},{12,... | collective-permute-start | bytes 393224 | tf_op jit(solution)/shard_map/ppermute | solution.py:301
  7.7 12.8 %collective-permute-start.4 = (bf16[64,1024]{1,0:T(8,128)(2,1)S(1)}, bf16[64,1024]{1,0:T(8,128)(2,1)S(1)}, u32[]{:S(2)}, u32[]{:S(2)}) collective-permute-start(bf16[64,1024]{1,0:T(8,128)(2,1)S(1)} %maximum_maximum_fusion), channel_id=1, source_target_pairs={{0,4},{2,6},{4,0},{6,2},{1,5},{3,7},{5,1},{7,3},{8,12},{10,14},{12... | collective-permute-start | bytes 393224 | tf_op jit(solution)/shard_map/ppermute | solution.py:301
  7.7 12.9 %collective-permute-start.3 = (bf16[64,1024]{1,0:T(8,128)(2,1)S(1)}, bf16[64,1024]{1,0:T(8,128)(2,1)S(1)}, u32[]{:S(2)}, u32[]{:S(2)}) collective-permute-start(bf16[64,1024]{1,0:T(8,128)(2,1)S(1)} %maximum_maximum_fusion), channel_id=1, source_target_pairs={{0,2},{2,4},{4,6},{6,0},{1,3},{3,5},{5,7},{7,1},{8,10},{10,12},{12... | collective-permute-start | bytes 393224 | tf_op jit(solution)/shard_map/ppermute | solution.py:301
  9.8 15.5 %copy-start.1 = (bf16[32,1024]{1,0:T(8,128)(2,1)S(1)}, bf16[32,1024]{1,0:T(8,128)(2,1)}, u32[]{:S(2)}) copy-start(bf16[32,1024]{1,0:T(8,128)(2,1)} %param.7) | copy-start | bytes 196612
  10.0 15.3 %collective-permute-start.16 = (bf16[128,512]{1,0:T(8,128)(2,1)S(1)}, bf16[128,512]{1,0:T(8,128)(2,1)S(1)}, u32[]{:S(2)}, u32[]{:S(2)}) collective-permute-start(bf16[128,512]{1,0:T(8,128)(2,1)S(1)} %bitcast.123), channel_id=1, source_target_pairs={{0,6},{2,0},{4,2},{6,4},{1,7},{3,1},{5,3},{7,5},{8,14},{10,8},{12,... | collective-permute-start | bytes 393224 | tf_op jit(solution)/shard_map/ppermute | solution.py:318
  12.8 10.9 %collective-permute-start.14 = (bf16[128,512]{1,0:T(8,128)(2,1)S(1)}, bf16[128,512]{1,0:T(8,128)(2,1)S(1)}, u32[]{:S(2)}, u32[]{:S(2)}) collective-permute-start(bf16[128,512]{1,0:T(8,128)(2,1)S(1)} %bitcast.124), channel_id=1, source_target_pairs={{0,2},{2,4},{4,6},{6,0},{1,3},{3,5},{5,7},{7,1},{8,10},{10,12},{12... | collective-permute-start | bytes 393224 | tf_op jit(solution)/shard_map/ppermute | solution.py:318
  13.3 33.8 %collective-permute-start.2 = (bf16[128,1024]{1,0:T(8,128)(2,1)S(1)}, bf16[128,1024]{1,0:T(8,128)(2,1)S(1)}, u32[]{:S(2)}, u32[]{:S(2)}) collective-permute-start(bf16[128,1024]{1,0:T(8,128)(2,1)S(1)} %bitcast.127), channel_id=1, source_target_pairs={{0,6},{2,0},{4,2},{6,4},{1,7},{3,1},{5,3},{7,5},{8,14},{10,8},{12,... | collective-permute-start | bytes 786440 | tf_op jit(solution)/shard_map/ppermute | solution.py:330
  20.5 30.6 %collective-permute-start = (bf16[128,1024]{1,0:T(8,128)(2,1)S(1)}, bf16[128,1024]{1,0:T(8,128)(2,1)S(1)}, u32[]{:S(2)}, u32[]{:S(2)}) collective-permute-start(bf16[128,1024]{1,0:T(8,128)(2,1)S(1)} %bitcast.128), channel_id=1, source_target_pairs={{0,2},{2,4},{4,6},{6,0},{1,3},{3,5},{5,7},{7,1},{8,10},{10,12},{12... | collective-permute-start | bytes 786440 | tf_op jit(solution)/shard_map/ppermute | solution.py:330
  20.6 12.7 %collective-permute-start.13 = (bf16[96,1024]{1,0:T(8,128)(2,1)S(1)}, bf16[96,1024]{1,0:T(8,128)(2,1)S(1)}, u32[]{:S(2)}, u32[]{:S(2)}) collective-permute-start(bf16[96,1024]{1,0:T(8,128)(2,1)S(1)} %pad_maximum_fusion.1), channel_id=1, source_target_pairs={{0,1},{1,0},{2,3},{3,2},{4,5},{5,4},{6,7},{7,6},{8,9},{9,8},{10,11... | collective-permute-start | bytes 589832 | tf_op jit(solution)/shard_map/ppermute | solution.py:306
  23.8 16.8 %collective-permute-start.17 = (bf16[128,512]{1,0:T(8,128)(2,1)S(1)}, bf16[128,512]{1,0:T(8,128)(2,1)S(1)}, u32[]{:S(2)}, u32[]{:S(2)}) collective-permute-start(bf16[128,512]{1,0:T(8,128)(2,1)S(1)} %collective-permute-done.14.refs_0_), channel_id=1, source_target_pairs={{0,1},{1,0},{2,3},{3,2},{4,5},{5,4},{6,7},{7,6},{8,9},{9,8},{10,11... | collective-permute-start | bytes 393224 | tf_op jit(solution)/shard_map/ppermute | solution.py:322
  25.3 15.3 %collective-permute-start.15 = (bf16[128,512]{1,0:T(8,128)(2,1)S(1)}, bf16[128,512]{1,0:T(8,128)(2,1)S(1)}, u32[]{:S(2)}, u32[]{:S(2)}) collective-permute-start(bf16[128,512]{1,0:T(8,128)(2,1)S(1)} %collective-permute-done.14.refs_0_), channel_id=1, source_target_pairs={{0,2},{2,4},{4,6},{6,0},{1,3},{3,5},{5,7},{7,1},{8,10},{10,12},{12... | collective-permute-start | bytes 393224 | tf_op jit(solution)/shard_map/ppermute | solution.py:318
  33.3 5.0 %collective-permute-start.19 = (bf16[128,512]{1,0:T(8,128)(2,1)S(1)}, bf16[128,512]{1,0:T(8,128)(2,1)S(1)}, u32[]{:S(2)}, u32[]{:S(2)}) collective-permute-start(bf16[128,512]{1,0:T(8,128)(2,1)S(1)} %collective-permute-done.16.refs_2_), channel_id=1, source_target_pairs={{0,1},{1,0},{2,3},{3,2},{4,5},{5,4},{6,7},{7,6},{8,9},{9,8},{10,11... | collective-permute-start | bytes 393224 | tf_op jit(solution)/shard_map/ppermute | solution.py:322
  38.3 17.6 %collective-permute-start.8 = (bf16[4,32,1024]{2,1,0:T(8,128)(2,1)S(1)}, bf16[4,32,1024]{2,1,0:T(8,128)(2,1)S(1)}, u32[]{:S(2)}, u32[]{:S(2)}) collective-permute-start(bf16[4,32,1024]{2,1,0:T(8,128)(2,1)S(1)} %pad_maximum_fusion.refs_4_), channel_id=1, source_target_pairs={{0,17},{1,16},{8,25},{9,24},{16,1},{17,0},{24,9},{25,8},{2,19},{3,... | collective-permute-start | bytes 786440 | tf_op jit(solution)/shard_map/ppermute | solution.py:341
  40.6 15.2 %collective-permute-start.7 = (bf16[4,32,1024]{2,1,0:T(8,128)(2,1)S(1)}, bf16[4,32,1024]{2,1,0:T(8,128)(2,1)S(1)}, u32[]{:S(2)}, u32[]{:S(2)}) collective-permute-start(bf16[4,32,1024]{2,1,0:T(8,128)(2,1)S(1)} %pad_maximum_fusion.refs_4_), channel_id=1, source_target_pairs={{0,16},{1,17},{8,24},{9,25},{16,0},{17,1},{24,8},{25,9},{2,18},{3,... | collective-permute-start | bytes 786440 | tf_op jit(solution)/shard_map/ppermute | solution.py:341
  40.6 15.7 %collective-permute-start.6 = (bf16[4,32,1024]{2,1,0:T(8,128)(2,1)S(1)}, bf16[4,32,1024]{2,1,0:T(8,128)(2,1)S(1)}, u32[]{:S(2)}, u32[]{:S(2)}) collective-permute-start(bf16[4,32,1024]{2,1,0:T(8,128)(2,1)S(1)} %pad_maximum_fusion.refs_4_), channel_id=1, source_target_pairs={{0,1},{1,0},{8,9},{9,8},{16,17},{17,16},{24,25},{25,24},{2,3},{3,2... | collective-permute-start | bytes 786440 | tf_op jit(solution)/shard_map/ppermute | solution.py:341
  47.1 5.5 %collective-permute-start.18 = (bf16[128,512]{1,0:T(8,128)(2,1)S(1)}, bf16[128,512]{1,0:T(8,128)(2,1)S(1)}, u32[]{:S(2)}, u32[]{:S(2)}) collective-permute-start(bf16[128,512]{1,0:T(8,128)(2,1)S(1)} %collective-permute-done.15.refs_1_), channel_id=1, source_target_pairs={{0,1},{1,0},{2,3},{3,2},{4,5},{5,4},{6,7},{7,6},{8,9},{9,8},{10,11... | collective-permute-start | bytes 393224 | tf_op jit(solution)/shard_map/ppermute | solution.py:322
  51.1 10.2 %collective-permute-start.9 = (bf16[4,32,1024]{2,1,0:T(8,128)(2,1)S(1)}, bf16[4,32,1024]{2,1,0:T(8,128)(2,1)S(1)}, u32[]{:S(2)}, u32[]{:S(2)}) collective-permute-start(bf16[4,32,1024]{2,1,0:T(8,128)(2,1)S(1)} %pad_maximum_fusion.refs_4_), channel_id=1, source_target_pairs={{0,8},{8,0},{16,24},{24,16},{1,9},{9,1},{17,25},{25,17},{2,10},{10... | collective-permute-start | bytes 786440 | tf_op jit(solution)/shard_map/ppermute | solution.py:342
  52.5 9.2 %collective-permute-start.1 = (bf16[128,1024]{1,0:T(8,128)(2,1)S(1)}, bf16[128,1024]{1,0:T(8,128)(2,1)S(1)}, u32[]{:S(2)}, u32[]{:S(2)}) collective-permute-start(bf16[128,1024]{1,0:T(8,128)(2,1)S(1)} %collective-permute-done.refs_1_), channel_id=1, source_target_pairs={{0,2},{2,4},{4,6},{6,0},{1,3},{3,5},{5,7},{7,1},{8,10},{10,12},{12... | collective-permute-start | bytes 786440 | tf_op jit(solution)/shard_map/ppermute | solution.py:330
  55.8 5.9 %collective-permute-start.12 = (bf16[4,32,1024]{2,1,0:T(8,128)(2,1)S(1)}, bf16[4,32,1024]{2,1,0:T(8,128)(2,1)S(1)}, u32[]{:S(2)}, u32[]{:S(2)}) collective-permute-start(bf16[4,32,1024]{2,1,0:T(8,128)(2,1)S(1)} %collective-permute-done.8.refs_7_), channel_id=1, source_target_pairs={{0,8},{8,0},{16,24},{24,16},{1,9},{9,1},{17,25},{25,17},{2,10},{10... | collective-permute-start | bytes 786440 | tf_op jit(solution)/shard_map/ppermute | solution.py:342
  55.8 5.9 %collective-permute-start.11 = (bf16[4,32,1024]{2,1,0:T(8,128)(2,1)S(1)}, bf16[4,32,1024]{2,1,0:T(8,128)(2,1)S(1)}, u32[]{:S(2)}, u32[]{:S(2)}) collective-permute-start(bf16[4,32,1024]{2,1,0:T(8,128)(2,1)S(1)} %collective-permute-done.7.refs_6_), channel_id=1, source_target_pairs={{0,8},{8,0},{16,24},{24,16},{1,9},{9,1},{17,25},{25,17},{2,10},{10... | collective-permute-start | bytes 786440 | tf_op jit(solution)/shard_map/ppermute | solution.py:342
  56.3 5.4 %collective-permute-start.10 = (bf16[4,32,1024]{2,1,0:T(8,128)(2,1)S(1)}, bf16[4,32,1024]{2,1,0:T(8,128)(2,1)S(1)}, u32[]{:S(2)}, u32[]{:S(2)}) collective-permute-start(bf16[4,32,1024]{2,1,0:T(8,128)(2,1)S(1)} %collective-permute-done.6.refs_5_), channel_id=1, source_target_pairs={{0,8},{8,0},{16,24},{24,16},{1,9},{9,1},{17,25},{25,17},{2,10},{10... | collective-permute-start | bytes 786440 | tf_op jit(solution)/shard_map/ppermute | solution.py:342
  76.7 7.4 %collective-permute-start.20 = (f32[128,1024]{1,0:T(8,128)S(1)}, f32[128,1024]{1,0:T(8,128)S(1)}, u32[]{:S(2)}, u32[]{:S(2)}) collective-permute-start(f32[128,1024]{1,0:T(8,128)S(1)} %get-tuple-element.16), channel_id=1, source_target_pairs={{0,8},{8,0},{16,24},{24,16},{1,9},{9,1},{17,25},{25,17},{2,10},{10... | collective-permute-start | bytes 1572872 | tf_op jit(solution)/shard_map/ppermute | solution.py:396
  79.8 8.0 %collective-permute-start.24 = (f32[16,8,256]{2,1,0:T(8,128)S(1)}, f32[16,8,256]{2,1,0:T(8,128)S(1)}, u32[]{:S(2)}, u32[]{:S(2)}) collective-permute-start(f32[16,8,256]{2,1,0:T(8,128)S(1)} %shard_map.81), channel_id=1, source_target_pairs={{0,1},{1,0},{2,3},{3,2},{4,5},{5,4},{6,7},{7,6},{8,9},{9,8},{10,11... | collective-permute-start | bytes 393224 | tf_op jit(solution)/shard_map/ppermute | solution.py:408
  84.2 6.4 %collective-permute-start.21 = (f32[32,1024]{1,0:T(8,128)S(1)}, f32[32,1024]{1,0:T(8,128)S(1)}, u32[]{:S(2)}, u32[]{:S(2)}) collective-permute-start(f32[32,1024]{1,0:T(8,128)S(1)} %get-tuple-element.22), channel_id=1, source_target_pairs={{0,1},{1,0},{2,3},{3,2},{4,5},{5,4},{6,7},{7,6},{8,9},{9,8},{10,11... | collective-permute-start | bytes 393224 | tf_op jit(solution)/shard_map/ppermute | solution.py:421
  84.8 9.3 %collective-permute-start.23 = (f32[32,1024]{1,0:T(8,128)S(1)}, f32[32,1024]{1,0:T(8,128)S(1)}, u32[]{:S(2)}, u32[]{:S(2)}) collective-permute-start(f32[32,1024]{1,0:T(8,128)S(1)} %get-tuple-element.23), channel_id=1, source_target_pairs={{0,17},{1,16},{2,19},{3,18},{4,21},{5,20},{6,23},{7,22},{8,25},{9,... | collective-permute-start | bytes 393224 | tf_op jit(solution)/shard_map/ppermute | solution.py:421
  87.7 7.9 %collective-permute-start.22 = (f32[32,1024]{1,0:T(8,128)S(1)}, f32[32,1024]{1,0:T(8,128)S(1)}, u32[]{:S(2)}, u32[]{:S(2)}) collective-permute-start(f32[32,1024]{1,0:T(8,128)S(1)} %get-tuple-element.24), channel_id=1, source_target_pairs={{0,16},{1,17},{2,18},{3,19},{4,20},{5,21},{6,22},{7,23},{8,24},{9,... | collective-permute-start | bytes 393224 | tf_op jit(solution)/shard_map/ppermute | solution.py:421

commit v7 on v5

--- a/solution.py
+++ b/solution.py
@@ -302,10 +302,8 @@
     width = pass_rows // n_dp
     share = [lax.dynamic_slice_in_dim(codes_t, lanes[t] * width, width, 1) for t in range(n_dp)]
     tiles = {(0, 0): share[0]}
-    for k in relay(n_sh):
-        step = 1 if 2 * k <= n_sh else n_sh - 1
-        source = tiles[0, (k - step) % n_sh]
-        tiles[0, k] = move(source, "shard", ring(n_sh, step))
+    for k in range(1, n_sh):
+        tiles[0, k] = move(share[0], "shard", ring(n_sh, k))
     for t in range(1, n_dp):
         tiles[t, 0] = share[t]
         for k in range(1, n_sh):

time: 96.6 us -> 95.7 us (level)
  starting transfers between devices: 37.9 us -> 34.3 us
  waiting for transfers between devices: 17 us -> 19.7 us
    ppermute x3, starting transfers between devices: 10.8 us -> 4.05 us  [compute(): tiles[0, k] = move(share[0], 'shard', ring(n_sh, k))]
    ppermute x3, waiting for transfers between devices: 4.93 us -> 0.25 us  [compute(): tiles[t, k] = move(tiles[0, k], 'dp', ring(n_dp, t))]
    ppermute x3, waiting for transfers between devices: 0.78 us -> 3.85 us  [compute(): q_held[k] = move(q_held[(k - step) % group], 'shard', pairs)]
    ppermute x3, waiting for transfers between devices: 3.4 us -> 6.08 us  [compute(): moved = [move(packet, 'shard', ring(n_sh, k)) for k in range(1, n_sh)]]
    ppermute x3, starting transfers between devices: 7.05 us -> 9.47 us  [compute(): q_held[k] = move(q_held[(k - step) % group], 'shard', pairs)]
    ppermute x3, waiting for transfers between devices: 0.79 us -> 2.55 us  [compute(): tiles[0, k] = move(share[0], 'shard', ring(n_sh, k))]
    ppermute x1, starting transfers between devices: 1.52 us -> 0.05 us  [compute(): part = move(part, ('shard', 'dp'), pairs)]
  transfers between devices with their start and end apart: 25 -> 25, of which waited for: 8 -> 7; matrix products, arithmetic and copies ran while one was open for 3% -> 3% of each run, Pallas kernels for 21% -> 21%
where the time goes in v7:
time: 95.7 us; the launch traced here: 95.5 us
  Pallas kernels  34.7 us (36%)
  starting transfers between devices  34.3 us (36%)
  waiting for transfers between devices  19.7 us (21%)
  other arithmetic  4.59 us (5%)
  local copies, waits for them, and re-layouts  1.21 us (1%)
  between operations  1 us (1%)
    pallas_call x3, Pallas kernels, rebuild(): pl.pallas_call(functools.partial(rebuild_kernel, n_t, n_b), out_shape=(ja...  14.7 us
    pallas_call x1, Pallas kernels, main(): pl.pallas_call(functools.partial(main_kernel, n_q, n_w, n_g), out_shape=(...  14.2 us
    ppermute x3, starting transfers between devices, compute(): q_held[k] = move(q_held[(k - step) % group], 'shard', pairs)  9.47 us
    ppermute x3, waiting for transfers between devices, compute(): moved = move(summed[i, o], ('dom', 'shard', 'dp'), pairs)  6.97 us
    ppermute x3, starting transfers between devices, compute(): moved = [move(packet, 'shard', ring(n_sh, k)) for k in range(1, n_sh)]  6.14 us
    ppermute x3, waiting for transfers between devices, compute(): moved = [move(packet, 'shard', ring(n_sh, k)) for k in range(1, n_sh)]  6.08 us
    pallas_call x2, Pallas kernels, word_grads(): pl.pallas_call(functools.partial(words_kernel, words, block), out_shape=j...  5.81 us
    ppermute x3, starting transfers between devices, compute(): w_pieces.append(w_z if e == t == 0 else move(w_z, ('dom', 'dp'), pairs))  4.51 us
  transfers between devices with their start and end apart: 25, of which 7 were waited for; matrix products, arithmetic and copies ran while one was open for 3% of the time, Pallas kernels for 21%

profile of v7, /device:TPU:0, one launch (start us, length us, event | category | flops | bytes accessed | tf_op | source)
XLA Modules:
  0.0 95.5 jit_solution(13538385375295930159)
XLA Ops:
  0.7 1.0 %convert_element_type.14 = bf16[1,32,8,256]{3,2,1,0:T(8,128)(2,1)S(1)} convert(f32[1,32,8,256]{3,2,1,0:T(8,128)} %param.8) | non-fusion elementwise | flops 65536 | bytes 393216 | tf_op jit(solution)/shard_map/convert_element_type | solution.py:280
  1.7 0.9 maximum_maximum_fusion
  2.6 5.1 %collective-permute-start.5 = (bf16[64,1024]{1,0:T(8,128)(2,1)S(1)}, bf16[64,1024]{1,0:T(8,128)(2,1)S(1)}, u32[]{:S(2)}, u32[]{:S(2)}) collective-permute-start(bf16[64,1024]{1,0:T(8,128)(2,1)S(1)} %maximum_maximum_fusion), channel_id=1, source_target_pairs={{0,6},{2,0},{4,2},{6,4},{1,7},{3,1},{5,3},{7,5},{8,14},{10,8},{12,... | collective-permute-start | bytes 393224 | tf_op jit(solution)/shard_map/ppermute | solution.py:291
  7.7 1.0 %collective-permute-start.3 = (bf16[64,1024]{1,0:T(8,128)(2,1)S(1)}, bf16[64,1024]{1,0:T(8,128)(2,1)S(1)}, u32[]{:S(2)}, u32[]{:S(2)}) collective-permute-start(bf16[64,1024]{1,0:T(8,128)(2,1)S(1)} %maximum_maximum_fusion), channel_id=1, source_target_pairs={{0,2},{2,4},{4,6},{6,0},{1,3},{3,5},{5,7},{7,1},{8,10},{10,12},{12... | collective-permute-start | bytes 393224 | tf_op jit(solution)/shard_map/ppermute | solution.py:291
  8.7 1.1 %convert_element_type.15 = bf16[1,1024,128]{2,1,0:T(8,128)(2,1)S(1)} convert(s32[1,1024,128]{2,1,0:T(8,128)} %param.9) | non-fusion elementwise | flops 131072 | bytes 786432 | tf_op jit(solution)/shard_map/convert_element_type | solution.py:300
  9.9 0.1 copy.10
  10.0 2.9 %collective-permute-start.16 = (bf16[128,512]{1,0:T(8,128)(2,1)S(1)}, bf16[128,512]{1,0:T(8,128)(2,1)S(1)}, u32[]{:S(2)}, u32[]{:S(2)}) collective-permute-start(bf16[128,512]{1,0:T(8,128)(2,1)S(1)} %bitcast.123), channel_id=1, source_target_pairs={{0,6},{2,0},{4,2},{6,4},{1,7},{3,1},{5,3},{7,5},{8,14},{10,8},{12,... | collective-permute-start | bytes 393224 | tf_op jit(solution)/shard_map/ppermute | solution.py:306
  12.8 1.1 %collective-permute-start.15 = (bf16[128,512]{1,0:T(8,128)(2,1)S(1)}, bf16[128,512]{1,0:T(8,128)(2,1)S(1)}, u32[]{:S(2)}, u32[]{:S(2)}) collective-permute-start(bf16[128,512]{1,0:T(8,128)(2,1)S(1)} %bitcast.124), channel_id=1, source_target_pairs={{0,4},{2,6},{4,0},{6,2},{1,5},{3,7},{5,1},{7,3},{8,12},{10,14},{12... | collective-permute-start | bytes 393224 | tf_op jit(solution)/shard_map/ppermute | solution.py:306
  14.0 0.1 stack.236
  14.1 0.1 stack.257
  14.2 0.1 iota_add_fusion
  14.5 6.1 %collective-permute-done.4 = bf16[64,1024]{1,0:T(8,128)(2,1)S(1)} collective-permute-done((bf16[64,1024]{1,0:T(8,128)(2,1)S(1)}, bf16[64,1024]{1,0:T(8,128)(2,1)S(1)}, u32[]{:S(2)}, u32[]{:S(2)}) %collective-permute-start.4) | collective-permute-done | bytes 131104 | tf_op jit(solution)/shard_map/ppermute | solution.py:291
  20.5 1.0 %collective-permute-start.2 = (bf16[128,1024]{1,0:T(8,128)(2,1)S(1)}, bf16[128,1024]{1,0:T(8,128)(2,1)S(1)}, u32[]{:S(2)}, u32[]{:S(2)}) collective-permute-start(bf16[128,1024]{1,0:T(8,128)(2,1)S(1)} %bitcast.128), channel_id=1, source_target_pairs={{0,6},{2,0},{4,2},{6,4},{1,7},{3,1},{5,3},{7,5},{8,14},{10,8},{12,... | collective-permute-start | bytes 786440 | tf_op jit(solution)/shard_map/ppermute | solution.py:318
  21.6 1.6 %collective-permute-start.13 = (bf16[96,1024]{1,0:T(8,128)(2,1)S(1)}, bf16[96,1024]{1,0:T(8,128)(2,1)S(1)}, u32[]{:S(2)}, u32[]{:S(2)}) collective-permute-start(bf16[96,1024]{1,0:T(8,128)(2,1)S(1)} %pad_maximum_fusion.1), channel_id=1, source_target_pairs={{0,1},{1,0},{2,3},{3,2},{4,5},{5,4},{6,7},{7,6},{8,9},{9,8},{10,11... | collective-permute-start | bytes 589832 | tf_op jit(solution)/shard_map/ppermute | solution.py:296
  23.2 0.1 pad_add_fusion.1.blocks_ref
  23.3 0.1 add.492.frow_ref
  23.4 0.1 copy.14.wt_ref
  23.6 0.1 copy.13.pos_ref
  23.7 0.1 copy.11
  23.8 0.1 stack.271.place_ref
  23.9 0.1 stack.245.tbase_ref
  24.1 5.1 %collective-permute-start = (bf16[128,1024]{1,0:T(8,128)(2,1)S(1)}, bf16[128,1024]{1,0:T(8,128)(2,1)S(1)}, u32[]{:S(2)}, u32[]{:S(2)}) collective-permute-start(bf16[128,1024]{1,0:T(8,128)(2,1)S(1)} %bitcast.129), channel_id=1, source_target_pairs={{0,2},{2,4},{4,6},{6,0},{1,3},{3,5},{5,7},{7,1},{8,10},{10,12},{12... | collective-permute-start | bytes 786440 | tf_op jit(solution)/shard_map/ppermute | solution.py:318
  29.2 2.5 %collective-permute-done.15.refs_1_ = bf16[128,512]{1,0:T(8,128)(2,1)S(1)} collective-permute-done((bf16[128,512]{1,0:T(8,128)(2,1)S(1)}, bf16[128,512]{1,0:T(8,128)(2,1)S(1)}, u32[]{:S(2)}, u32[]{:S(2)}) %collective-permute-start.15) | collective-permute-done | bytes 131104 | tf_op jit(solution)/shard_map/ppermute | solution.py:306
  31.7 1.5 %collective-permute-start.19 = (bf16[128,512]{1,0:T(8,128)(2,1)S(1)}, bf16[128,512]{1,0:T(8,128)(2,1)S(1)}, u32[]{:S(2)}, u32[]{:S(2)}) collective-permute-start(bf16[128,512]{1,0:T(8,128)(2,1)S(1)} %collective-permute-done.16.refs_2_), channel_id=1, source_target_pairs={{0,1},{1,0},{2,3},{3,2},{4,5},{5,4},{6,7},{7,6},{8,9},{9,8},{10,11... | collective-permute-start | bytes 393224 | tf_op jit(solution)/shard_map/ppermute | solution.py:310
  33.2 0.5 collective-permute-start.18
  33.8 1.5 %collective-permute-start.17 = (bf16[128,512]{1,0:T(8,128)(2,1)S(1)}, bf16[128,512]{1,0:T(8,128)(2,1)S(1)}, u32[]{:S(2)}, u32[]{:S(2)}) collective-permute-start(bf16[128,512]{1,0:T(8,128)(2,1)S(1)} %collective-permute-done.14.refs_0_), channel_id=1, source_target_pairs={{0,1},{1,0},{2,3},{3,2},{4,5},{5,4},{6,7},{7,6},{8,9},{9,8},{10,11... | collective-permute-start | bytes 393224 | tf_op jit(solution)/shard_map/ppermute | solution.py:310
  35.3 3.8 %shard_map.77 = (bf16[2,1024,512]{2,1,0:T(8,128)(2,1)S(1)}, s32[2,2,16,512]{3,2,1,0:T(8,128)S(1)}) custom-call(s32[8]{0:T(128)S(1)} %stack.271.place_ref, s32[2]{0:T(128)S(1)} %pad_add_fusion.1.blocks_ref, bf16[128,512]{1,0:T(8,128)(2,1)S(1)} %bitcast.126, bf16[128,512]{1,0:T(8,128)(2,1)S(1)} %bitcast.127, ...), custom_call_target="tpu_custom_call" | custom-call | flops 2000000000 | bytes 4000000 | tf_op jit(solution)/shard_map/pallas_call | solution.py:89
  39.1 1.6 %collective-permute-start.8 = (bf16[4,32,1024]{2,1,0:T(8,128)(2,1)S(1)}, bf16[4,32,1024]{2,1,0:T(8,128)(2,1)S(1)}, u32[]{:S(2)}, u32[]{:S(2)}) collective-permute-start(bf16[4,32,1024]{2,1,0:T(8,128)(2,1)S(1)} %pad_maximum_fusion.refs_4_), channel_id=1, source_target_pairs={{0,17},{1,16},{8,25},{9,24},{16,1},{17,0},{24,9},{25,8},{2,19},{3,... | collective-permute-start | bytes 786440 | tf_op jit(solution)/shard_map/ppermute | solution.py:329
  40.7 0.5 collective-permute-start.7
  41.2 0.2 collective-permute-done.17.refs_0_
  41.4 2.4 %collective-permute-start.6 = (bf16[4,32,1024]{2,1,0:T(8,128)(2,1)S(1)}, bf16[4,32,1024]{2,1,0:T(8,128)(2,1)S(1)}, u32[]{:S(2)}, u32[]{:S(2)}) collective-permute-start(bf16[4,32,1024]{2,1,0:T(8,128)(2,1)S(1)} %pad_maximum_fusion.refs_4_), channel_id=1, source_target_pairs={{0,1},{1,0},{8,9},{9,8},{16,17},{17,16},{24,25},{25,24},{2,3},{3,2... | collective-permute-start | bytes 786440 | tf_op jit(solution)/shard_map/ppermute | solution.py:329
  43.9 5.4 %shard_map.78 = (bf16[3,1024,512]{2,1,0:T(8,128)(2,1)S(1)}, s32[3,2,16,512]{3,2,1,0:T(8,128)S(1)}) custom-call(s32[8]{0:T(128)S(1)} %stack.271.place_ref, s32[2]{0:T(128)S(1)} %pad_add_fusion.1.blocks_ref, bf16[128,512]{1,0:T(8,128)(2,1)S(1)} %collective-permute-done.14.refs_0_, bf16[128,512]{1,0:T(8,128)(2,1)S(1)} %collective-permute-done.15.refs_1_, ...), custom_call_target="tpu_custom_call" | custom-call | flops 3000000000 | bytes 6000000 | tf_op jit(solution)/shard_map/pallas_call | solution.py:89
  49.4 3.3 %collective-permute-start.1 = (bf16[128,1024]{1,0:T(8,128)(2,1)S(1)}, bf16[128,1024]{1,0:T(8,128)(2,1)S(1)}, u32[]{:S(2)}, u32[]{:S(2)}) collective-permute-start(bf16[128,1024]{1,0:T(8,128)(2,1)S(1)} %collective-permute-done.refs_1_), channel_id=1, source_target_pairs={{0,2},{2,4},{4,6},{6,0},{1,3},{3,5},{5,7},{7,1},{8,10},{10,12},{12... | collective-permute-start | bytes 786440 | tf_op jit(solution)/shard_map/ppermute | solution.py:318
  52.8 0.5 collective-permute-start.11
  53.3 5.4 %shard_map.79 = (bf16[3,1024,512]{2,1,0:T(8,128)(2,1)S(1)}, s32[3,2,16,512]{3,2,1,0:T(8,128)S(1)}) custom-call(s32[8]{0:T(128)S(1)} %stack.271.place_ref, s32[2]{0:T(128)S(1)} %pad_add_fusion.1.blocks_ref, bf16[128,512]{1,0:T(8,128)(2,1)S(1)} %collective-permute-done.17.refs_0_, bf16[128,512]{1,0:T(8,128)(2,1)S(1)} %collective-permute-done.18.refs_1_, ...), custom_call_target="tpu_custom_call" | custom-call | flops 3000000000 | bytes 6000000 | tf_op jit(solution)/shard_map/pallas_call | solution.py:89
  58.8 3.8 %collective-permute-done.1.refs_2_ = bf16[128,1024]{1,0:T(8,128)(2,1)S(1)} collective-permute-done((bf16[128,1024]{1,0:T(8,128)(2,1)S(1)}, bf16[128,1024]{1,0:T(8,128)(2,1)S(1)}, u32[]{:S(2)}, u32[]{:S(2)}) %collective-permute-start.1) | collective-permute-done | bytes 262176 | tf_op jit(solution)/shard_map/ppermute | solution.py:318
  62.7 14.2 %shard_map.80 = (f32[128,1024]{1,0:T(8,128)S(1)}, f32[128,1024]{1,0:T(8,128)S(1)}, f32[128,4096]{1,0:T(8,128)S(1)}, f32[128,4096]{1,0:T(8,128)S(1)}) custom-call(s32[32]{0:T(128)S(1)} %broadcast_multiply_fusion.woff_ref, s32[8]{0:T(128)S(1)} %stack.245.tbase_ref, s32[2]{0:T(128)S(1)} %pad_add_fusion.1.blocks_ref, s32[256,1]{1,0:T(8,128)S(1)} %add.492.frow_ref, ...), custom_call_target="tpu_custom_call" | custom-call | flops 20000000000 | bytes 20000000 | tf_op jit(solution)/shard_map/pallas_call | solution.py:187
  76.8 0.1 collective-permute-start.20
  76.9 3.0 %shard_map.81 = f32[16,8,256]{2,1,0:T(8,128)S(1)} custom-call(f32[128,4096]{1,0:T(8,128)S(1)} %get-tuple-element.17.grads_ref, s32[2,2,16,512]{3,2,1,0:T(8,128)S(1)} %get-tuple-element.18.refs_0_, s32[3,2,16,512]{3,2,1,0:T(8,128)S(1)} %get-tuple-element.19.refs_1_, s32[3,2,16,512]{3,2,1,0:T(8,128)S(1)} %get-tuple-element.20.refs_2_), custom_call_target="tpu_custom_call" | custom-call | flops 3000000000 | bytes 4000000 | tf_op jit(solution)/shard_map/pallas_call | solution.py:258
  80.0 2.8 %shard_map.82 = f32[16,8,256]{2,1,0:T(8,128)S(1)} custom-call(f32[128,4096]{1,0:T(8,128)S(1)} %get-tuple-element.21.grads_ref, s32[2,2,16,512]{3,2,1,0:T(8,128)S(1)} %get-tuple-element.18.refs_0_, s32[3,2,16,512]{3,2,1,0:T(8,128)S(1)} %get-tuple-element.19.refs_1_, s32[3,2,16,512]{3,2,1,0:T(8,128)S(1)} %get-tuple-element.20.refs_2_), custom_call_target="tpu_custom_call" | custom-call | flops 3000000000 | bytes 4000000 | tf_op jit(solution)/shard_map/pallas_call | solution.py:258
  82.9 2.1 %collective-permute-start.21 = (f32[32,1024]{1,0:T(8,128)S(1)}, f32[32,1024]{1,0:T(8,128)S(1)}, u32[]{:S(2)}, u32[]{:S(2)}) collective-permute-start(f32[32,1024]{1,0:T(8,128)S(1)} %get-tuple-element.22), channel_id=1, source_target_pairs={{0,1},{1,0},{2,3},{3,2},{4,5},{5,4},{6,7},{7,6},{8,9},{9,8},{10,11... | collective-permute-start | bytes 393224 | tf_op jit(solution)/shard_map/ppermute | solution.py:409
  84.9 1.7 %collective-permute-start.23 = (f32[32,1024]{1,0:T(8,128)S(1)}, f32[32,1024]{1,0:T(8,128)S(1)}, u32[]{:S(2)}, u32[]{:S(2)}) collective-permute-start(f32[32,1024]{1,0:T(8,128)S(1)} %get-tuple-element.23), channel_id=1, source_target_pairs={{0,17},{1,16},{2,19},{3,18},{4,21},{5,20},{6,23},{7,22},{8,25},{9,... | collective-permute-start | bytes 393224 | tf_op jit(solution)/shard_map/ppermute | solution.py:409
  86.7 0.5 collective-permute-start.22
  87.2 0.7 add_bitcast_fusion
  87.8 1.0 %collective-permute-done.21 = f32[32,1024]{1,0:T(8,128)S(1)} collective-permute-done((f32[32,1024]{1,0:T(8,128)S(1)}, f32[32,1024]{1,0:T(8,128)S(1)}, u32[]{:S(2)}, u32[]{:S(2)}) %collective-permute-start.21) | collective-permute-done | bytes 131104 | tf_op jit(solution)/shard_map/ppermute | solution.py:409
  88.8 4.6 %collective-permute-done.23 = f32[32,1024]{1,0:T(8,128)S(1)} collective-permute-done((f32[32,1024]{1,0:T(8,128)S(1)}, f32[32,1024]{1,0:T(8,128)S(1)}, u32[]{:S(2)}, u32[]{:S(2)}) %collective-permute-start.23) | collective-permute-done | bytes 131104 | tf_op jit(solution)/shard_map/ppermute | solution.py:409
  93.4 1.4 %collective-permute-done.22 = f32[32,1024]{1,0:T(8,128)S(1)} collective-permute-done((f32[32,1024]{1,0:T(8,128)S(1)}, f32[32,1024]{1,0:T(8,128)S(1)}, u32[]{:S(2)}, u32[]{:S(2)}) %collective-permute-start.22) | collective-permute-done | bytes 131104 | tf_op jit(solution)/shard_map/ppermute | solution.py:409
  94.8 0.7 fusion.2
  (49 shorter events, 0.6 us)
Async XLA Ops:
  0.6 13.6 %copy-start.2 = (bf16[1,1024]{1,0:T(2,128)(2,1)S(1)}, bf16[1,1024]{1,0:T(2,128)(2,1)}, u32[]{:S(2)}) copy-start(bf16[1,1024]{1,0:T(2,128)(2,1)} %param.11) | copy-start | bytes 6148
  0.6 13.6 %copy-start.3 = (s32[1,1024]{1,0:T(1,128)S(1)}, s32[1,1024]{1,0:T(1,128)}, u32[]{:S(2)}) copy-start(s32[1,1024]{1,0:T(1,128)} %param.10) | copy-start | bytes 12292
  0.7 19.9 %copy-start = (bf16[1,128,1024]{2,1,0:T(8,128)(2,1)S(1)}, bf16[1,128,1024]{2,1,0:T(8,128)(2,1)}, u32[]{:S(2)}) copy-start(bf16[1,128,1024]{2,1,0:T(8,128)(2,1)} %param.6) | copy-start | bytes 786436
  2.6 11.8 %collective-permute-start.5 = (bf16[64,1024]{1,0:T(8,128)(2,1)S(1)}, bf16[64,1024]{1,0:T(8,128)(2,1)S(1)}, u32[]{:S(2)}, u32[]{:S(2)}) collective-permute-start(bf16[64,1024]{1,0:T(8,128)(2,1)S(1)} %maximum_maximum_fusion), channel_id=1, source_target_pairs={{0,6},{2,0},{4,2},{6,4},{1,7},{3,1},{5,3},{7,5},{8,14},{10,8},{12,... | collective-permute-start | bytes 393224 | tf_op jit(solution)/shard_map/ppermute | solution.py:291
  7.7 12.8 %collective-permute-start.4 = (bf16[64,1024]{1,0:T(8,128)(2,1)S(1)}, bf16[64,1024]{1,0:T(8,128)(2,1)S(1)}, u32[]{:S(2)}, u32[]{:S(2)}) collective-permute-start(bf16[64,1024]{1,0:T(8,128)(2,1)S(1)} %maximum_maximum_fusion), channel_id=1, source_target_pairs={{0,4},{2,6},{4,0},{6,2},{1,5},{3,7},{5,1},{7,3},{8,12},{10,14},{12... | collective-permute-start | bytes 393224 | tf_op jit(solution)/shard_map/ppermute | solution.py:291
  7.7 13.9 %collective-permute-start.3 = (bf16[64,1024]{1,0:T(8,128)(2,1)S(1)}, bf16[64,1024]{1,0:T(8,128)(2,1)S(1)}, u32[]{:S(2)}, u32[]{:S(2)}) collective-permute-start(bf16[64,1024]{1,0:T(8,128)(2,1)S(1)} %maximum_maximum_fusion), channel_id=1, source_target_pairs={{0,2},{2,4},{4,6},{6,0},{1,3},{3,5},{5,7},{7,1},{8,10},{10,12},{12... | collective-permute-start | bytes 393224 | tf_op jit(solution)/shard_map/ppermute | solution.py:291
  9.8 14.2 %copy-start.1 = (bf16[32,1024]{1,0:T(8,128)(2,1)S(1)}, bf16[32,1024]{1,0:T(8,128)(2,1)}, u32[]{:S(2)}) copy-start(bf16[32,1024]{1,0:T(8,128)(2,1)} %param.7) | copy-start | bytes 196612
  10.0 14.1 %collective-permute-start.16 = (bf16[128,512]{1,0:T(8,128)(2,1)S(1)}, bf16[128,512]{1,0:T(8,128)(2,1)S(1)}, u32[]{:S(2)}, u32[]{:S(2)}) collective-permute-start(bf16[128,512]{1,0:T(8,128)(2,1)S(1)} %bitcast.123), channel_id=1, source_target_pairs={{0,6},{2,0},{4,2},{6,4},{1,7},{3,1},{5,3},{7,5},{8,14},{10,8},{12,... | collective-permute-start | bytes 393224 | tf_op jit(solution)/shard_map/ppermute | solution.py:306
  12.8 18.9 %collective-permute-start.15 = (bf16[128,512]{1,0:T(8,128)(2,1)S(1)}, bf16[128,512]{1,0:T(8,128)(2,1)S(1)}, u32[]{:S(2)}, u32[]{:S(2)}) collective-permute-start(bf16[128,512]{1,0:T(8,128)(2,1)S(1)} %bitcast.124), channel_id=1, source_target_pairs={{0,4},{2,6},{4,0},{6,2},{1,5},{3,7},{5,1},{7,3},{8,12},{10,14},{12... | collective-permute-start | bytes 393224 | tf_op jit(solution)/shard_map/ppermute | solution.py:306
  14.4 18.9 %collective-permute-start.14 = (bf16[128,512]{1,0:T(8,128)(2,1)S(1)}, bf16[128,512]{1,0:T(8,128)(2,1)S(1)}, u32[]{:S(2)}, u32[]{:S(2)}) collective-permute-start(bf16[128,512]{1,0:T(8,128)(2,1)S(1)} %bitcast.125), channel_id=1, source_target_pairs={{0,2},{2,4},{4,6},{6,0},{1,3},{3,5},{5,7},{7,1},{8,10},{10,12},{12... | collective-permute-start | bytes 393224 | tf_op jit(solution)/shard_map/ppermute | solution.py:306
  20.5 28.8 %collective-permute-start.2 = (bf16[128,1024]{1,0:T(8,128)(2,1)S(1)}, bf16[128,1024]{1,0:T(8,128)(2,1)S(1)}, u32[]{:S(2)}, u32[]{:S(2)}) collective-permute-start(bf16[128,1024]{1,0:T(8,128)(2,1)S(1)} %bitcast.128), channel_id=1, source_target_pairs={{0,6},{2,0},{4,2},{6,4},{1,7},{3,1},{5,3},{7,5},{8,14},{10,8},{12,... | collective-permute-start | bytes 786440 | tf_op jit(solution)/shard_map/ppermute | solution.py:318
  21.6 12.1 %collective-permute-start.13 = (bf16[96,1024]{1,0:T(8,128)(2,1)S(1)}, bf16[96,1024]{1,0:T(8,128)(2,1)S(1)}, u32[]{:S(2)}, u32[]{:S(2)}) collective-permute-start(bf16[96,1024]{1,0:T(8,128)(2,1)S(1)} %pad_maximum_fusion.1), channel_id=1, source_target_pairs={{0,1},{1,0},{2,3},{3,2},{4,5},{5,4},{6,7},{7,6},{8,9},{9,8},{10,11... | collective-permute-start | bytes 589832 | tf_op jit(solution)/shard_map/ppermute | solution.py:296
  24.1 25.4 %collective-permute-start = (bf16[128,1024]{1,0:T(8,128)(2,1)S(1)}, bf16[128,1024]{1,0:T(8,128)(2,1)S(1)}, u32[]{:S(2)}, u32[]{:S(2)}) collective-permute-start(bf16[128,1024]{1,0:T(8,128)(2,1)S(1)} %bitcast.129), channel_id=1, source_target_pairs={{0,2},{2,4},{4,6},{6,0},{1,3},{3,5},{5,7},{7,1},{8,10},{10,12},{12... | collective-permute-start | bytes 786440 | tf_op jit(solution)/shard_map/ppermute | solution.py:318
  31.7 7.4 %collective-permute-start.19 = (bf16[128,512]{1,0:T(8,128)(2,1)S(1)}, bf16[128,512]{1,0:T(8,128)(2,1)S(1)}, u32[]{:S(2)}, u32[]{:S(2)}) collective-permute-start(bf16[128,512]{1,0:T(8,128)(2,1)S(1)} %collective-permute-done.16.refs_2_), channel_id=1, source_target_pairs={{0,1},{1,0},{2,3},{3,2},{4,5},{5,4},{6,7},{7,6},{8,9},{9,8},{10,11... | collective-permute-start | bytes 393224 | tf_op jit(solution)/shard_map/ppermute | solution.py:310
  33.2 7.5 %collective-permute-start.18 = (bf16[128,512]{1,0:T(8,128)(2,1)S(1)}, bf16[128,512]{1,0:T(8,128)(2,1)S(1)}, u32[]{:S(2)}, u32[]{:S(2)}) collective-permute-start(bf16[128,512]{1,0:T(8,128)(2,1)S(1)} %collective-permute-done.15.refs_1_), channel_id=1, source_target_pairs={{0,1},{1,0},{2,3},{3,2},{4,5},{5,4},{6,7},{7,6},{8,9},{9,8},{10,11... | collective-permute-start | bytes 393224 | tf_op jit(solution)/shard_map/ppermute | solution.py:310
  33.8 7.7 %collective-permute-start.17 = (bf16[128,512]{1,0:T(8,128)(2,1)S(1)}, bf16[128,512]{1,0:T(8,128)(2,1)S(1)}, u32[]{:S(2)}, u32[]{:S(2)}) collective-permute-start(bf16[128,512]{1,0:T(8,128)(2,1)S(1)} %collective-permute-done.14.refs_0_), channel_id=1, source_target_pairs={{0,1},{1,0},{2,3},{3,2},{4,5},{5,4},{6,7},{7,6},{8,9},{9,8},{10,11... | collective-permute-start | bytes 393224 | tf_op jit(solution)/shard_map/ppermute | solution.py:310
  39.1 13.6 %collective-permute-start.8 = (bf16[4,32,1024]{2,1,0:T(8,128)(2,1)S(1)}, bf16[4,32,1024]{2,1,0:T(8,128)(2,1)S(1)}, u32[]{:S(2)}, u32[]{:S(2)}) collective-permute-start(bf16[4,32,1024]{2,1,0:T(8,128)(2,1)S(1)} %pad_maximum_fusion.refs_4_), channel_id=1, source_target_pairs={{0,17},{1,16},{8,25},{9,24},{16,1},{17,0},{24,9},{25,8},{2,19},{3,... | collective-permute-start | bytes 786440 | tf_op jit(solution)/shard_map/ppermute | solution.py:329
  40.7 12.1 %collective-permute-start.7 = (bf16[4,32,1024]{2,1,0:T(8,128)(2,1)S(1)}, bf16[4,32,1024]{2,1,0:T(8,128)(2,1)S(1)}, u32[]{:S(2)}, u32[]{:S(2)}) collective-permute-start(bf16[4,32,1024]{2,1,0:T(8,128)(2,1)S(1)} %pad_maximum_fusion.refs_4_), channel_id=1, source_target_pairs={{0,16},{1,17},{8,24},{9,25},{16,0},{17,1},{24,8},{25,9},{2,18},{3,... | collective-permute-start | bytes 786440 | tf_op jit(solution)/shard_map/ppermute | solution.py:329
  41.4 11.8 %collective-permute-start.6 = (bf16[4,32,1024]{2,1,0:T(8,128)(2,1)S(1)}, bf16[4,32,1024]{2,1,0:T(8,128)(2,1)S(1)}, u32[]{:S(2)}, u32[]{:S(2)}) collective-permute-start(bf16[4,32,1024]{2,1,0:T(8,128)(2,1)S(1)} %pad_maximum_fusion.refs_4_), channel_id=1, source_target_pairs={{0,1},{1,0},{8,9},{9,8},{16,17},{17,16},{24,25},{25,24},{2,3},{3,2... | collective-permute-start | bytes 786440 | tf_op jit(solution)/shard_map/ppermute | solution.py:329
  49.3 9.4 %collective-permute-start.9 = (bf16[4,32,1024]{2,1,0:T(8,128)(2,1)S(1)}, bf16[4,32,1024]{2,1,0:T(8,128)(2,1)S(1)}, u32[]{:S(2)}, u32[]{:S(2)}) collective-permute-start(bf16[4,32,1024]{2,1,0:T(8,128)(2,1)S(1)} %pad_maximum_fusion.refs_4_), channel_id=1, source_target_pairs={{0,8},{8,0},{16,24},{24,16},{1,9},{9,1},{17,25},{25,17},{2,10},{10... | collective-permute-start | bytes 786440 | tf_op jit(solution)/shard_map/ppermute | solution.py:330
  49.4 13.2 %collective-permute-start.1 = (bf16[128,1024]{1,0:T(8,128)(2,1)S(1)}, bf16[128,1024]{1,0:T(8,128)(2,1)S(1)}, u32[]{:S(2)}, u32[]{:S(2)}) collective-permute-start(bf16[128,1024]{1,0:T(8,128)(2,1)S(1)} %collective-permute-done.refs_1_), channel_id=1, source_target_pairs={{0,2},{2,4},{4,6},{6,0},{1,3},{3,5},{5,7},{7,1},{8,10},{10,12},{12... | collective-permute-start | bytes 786440 | tf_op jit(solution)/shard_map/ppermute | solution.py:318
  52.8 9.9 %collective-permute-start.12 = (bf16[4,32,1024]{2,1,0:T(8,128)(2,1)S(1)}, bf16[4,32,1024]{2,1,0:T(8,128)(2,1)S(1)}, u32[]{:S(2)}, u32[]{:S(2)}) collective-permute-start(bf16[4,32,1024]{2,1,0:T(8,128)(2,1)S(1)} %collective-permute-done.8.refs_7_), channel_id=1, source_target_pairs={{0,8},{8,0},{16,24},{24,16},{1,9},{9,1},{17,25},{25,17},{2,10},{10... | collective-permute-start | bytes 786440 | tf_op jit(solution)/shard_map/ppermute | solution.py:330
  52.8 9.9 %collective-permute-start.11 = (bf16[4,32,1024]{2,1,0:T(8,128)(2,1)S(1)}, bf16[4,32,1024]{2,1,0:T(8,128)(2,1)S(1)}, u32[]{:S(2)}, u32[]{:S(2)}) collective-permute-start(bf16[4,32,1024]{2,1,0:T(8,128)(2,1)S(1)} %collective-permute-done.7.refs_6_), channel_id=1, source_target_pairs={{0,8},{8,0},{16,24},{24,16},{1,9},{9,1},{17,25},{25,17},{2,10},{10... | collective-permute-start | bytes 786440 | tf_op jit(solution)/shard_map/ppermute | solution.py:330
  53.3 9.4 %collective-permute-start.10 = (bf16[4,32,1024]{2,1,0:T(8,128)(2,1)S(1)}, bf16[4,32,1024]{2,1,0:T(8,128)(2,1)S(1)}, u32[]{:S(2)}, u32[]{:S(2)}) collective-permute-start(bf16[4,32,1024]{2,1,0:T(8,128)(2,1)S(1)} %collective-permute-done.6.refs_5_), channel_id=1, source_target_pairs={{0,8},{8,0},{16,24},{24,16},{1,9},{9,1},{17,25},{25,17},{2,10},{10... | collective-permute-start | bytes 786440 | tf_op jit(solution)/shard_map/ppermute | solution.py:330
  76.8 5.9 %collective-permute-start.20 = (f32[128,1024]{1,0:T(8,128)S(1)}, f32[128,1024]{1,0:T(8,128)S(1)}, u32[]{:S(2)}, u32[]{:S(2)}) collective-permute-start(f32[128,1024]{1,0:T(8,128)S(1)} %get-tuple-element.16), channel_id=1, source_target_pairs={{0,8},{8,0},{16,24},{24,16},{1,9},{9,1},{17,25},{25,17},{2,10},{10... | collective-permute-start | bytes 1572872 | tf_op jit(solution)/shard_map/ppermute | solution.py:384
  79.9 7.3 %collective-permute-start.24 = (f32[16,8,256]{2,1,0:T(8,128)S(1)}, f32[16,8,256]{2,1,0:T(8,128)S(1)}, u32[]{:S(2)}, u32[]{:S(2)}) collective-permute-start(f32[16,8,256]{2,1,0:T(8,128)S(1)} %shard_map.81), channel_id=1, source_target_pairs={{0,1},{1,0},{2,3},{3,2},{4,5},{5,4},{6,7},{7,6},{8,9},{9,8},{10,11... | collective-permute-start | bytes 393224 | tf_op jit(solution)/shard_map/ppermute | solution.py:396
  82.9 6.0 %collective-permute-start.21 = (f32[32,1024]{1,0:T(8,128)S(1)}, f32[32,1024]{1,0:T(8,128)S(1)}, u32[]{:S(2)}, u32[]{:S(2)}) collective-permute-start(f32[32,1024]{1,0:T(8,128)S(1)} %get-tuple-element.22), channel_id=1, source_target_pairs={{0,1},{1,0},{2,3},{3,2},{4,5},{5,4},{6,7},{7,6},{8,9},{9,8},{10,11... | collective-permute-start | bytes 393224 | tf_op jit(solution)/shard_map/ppermute | solution.py:409
  84.9 8.4 %collective-permute-start.23 = (f32[32,1024]{1,0:T(8,128)S(1)}, f32[32,1024]{1,0:T(8,128)S(1)}, u32[]{:S(2)}, u32[]{:S(2)}) collective-permute-start(f32[32,1024]{1,0:T(8,128)S(1)} %get-tuple-element.23), channel_id=1, source_target_pairs={{0,17},{1,16},{2,19},{3,18},{4,21},{5,20},{6,23},{7,22},{8,25},{9,... | collective-permute-start | bytes 393224 | tf_op jit(solution)/shard_map/ppermute | solution.py:409
  86.7 8.1 %collective-permute-start.22 = (f32[32,1024]{1,0:T(8,128)S(1)}, f32[32,1024]{1,0:T(8,128)S(1)}, u32[]{:S(2)}, u32[]{:S(2)}) collective-permute-start(f32[32,1024]{1,0:T(8,128)S(1)} %get-tuple-element.24), channel_id=1, source_target_pairs={{0,16},{1,17},{2,18},{3,19},{4,20},{5,21},{6,22},{7,23},{8,24},{9,... | collective-permute-start | bytes 393224 | tf_op jit(solution)/shard_map/ppermute | solution.py:409
